TPU v7x, 32 devices: a whole 2x2x4 slice. The times are simulated.
32 devices in a mesh: grp: 8 (over z, y), ep: 4 (over x, core).
Axes of the slice: x: 2, y: 2, z: 4, core: 2. Of those that a mesh axis runs over, the one named last changes fastest.
Arguments:
- tokens: bfloat16 [6144, 4096], P(('grp', 'ep')), may hold values from -6 to 6
- expert_ids: int32 [6144, 8], P(('grp', 'ep')), may hold values from 0 to 127, all different within a row; in each aligned block of 192 rows (0 to 191, 192 to 383, ...) at most 24 rows name the same one
- gate_probs: float32 [6144, 8], P(('grp', 'ep')), may hold values from 0.02 to 0.25
- placement: int32 [8, 1], P('grp'), may hold values from 0 to 1
- gate_weight: bfloat16 [8, 4096, 768], P('grp', None, 'ep'), may hold values from -0.09375 to 0.09375
- up_weight: bfloat16 [8, 4096, 768], P('grp', None, 'ep'), may hold values from -0.09375 to 0.09375
- down_weight: bfloat16 [8, 768, 4096], P('grp', 'ep'), may hold values from -0.21875 to 0.21875
- out_grad: bfloat16 [6144, 4096], P(('grp', 'ep')), may hold values from -6 to 6
- moment_first: float32 [2, 768, 4096], P(None, 'ep', 'grp'), may hold values from -2 to 2
- moment_second: float32 [2, 768, 4096], P(None, 'ep', 'grp'), may hold values from 0.01 to 1
Outputs:
- token_grad: bfloat16 [6144, 4096], P(('grp', 'ep'))
- step_dir: bfloat16 [8, 768, 4096], P('grp', 'ep')
- new_first: float32 [2, 768, 4096], P(None, 'ep', 'grp')
- new_second: float32 [2, 768, 4096], P(None, 'ep', 'grp')
Inputs may be any that keep to these rules, and one draw needn't show every extreme that they name: `expert_ids`: each row names 8 different experts. In the rows of one device no expert is named more than 24 times, a bound that some block reaches. Group g holds expert placement[g, s] + s in its slot s.
All inputs are finite; a program needn't handle non-finite values.
Results may differ from a plain program's by a relative error of at most 0.015.
Values may be sent and summed in bfloat16 or wider, within the bound.
No kernel may reach another device: no remote copies, remote signals or barrier semaphores. Data moves between devices by JAX's collectives and lax.ppermute only.
A program may use at most 128 MiB of HBM per device.

v0:
```python
import functools
import math

import jax
import jax.numpy as jnp
from jax import lax
from jax.experimental import pallas as pl
from jax.experimental.pallas import tpu as pltpu
from jax.sharding import PartitionSpec as P


QUARTERS = 4
CANDS = 2
CAP = 24
TAG = 16


beta_one = 0.9
beta_two = 0.999
adam_eps = 1e-08
first_fix = 1.0 - math.exp(1000.0 * math.log(0.9))
second_fix = 1.0 - math.exp(1000.0 * math.log(0.999))

F32 = jnp.float32
BF16 = jnp.bfloat16
NT = (((1,), (1,)), ((), ()))
TN = (((0,), (0,)), ((), ()))


SCALARS = pl.BlockSpec(memory_space=pltpu.SMEM)
LOCAL = pl.BlockSpec(memory_space=pltpu.VMEM)
PARAMS = pltpu.CompilerParams(vmem_limit_bytes=16 * 2**20)


def cost(flops, moved):
    return pl.CostEstimate(flops=int(flops), bytes_accessed=int(moved), transcendentals=0)


def rows_of(parts):
    return jnp.concatenate([part.astype(F32) for part in parts], axis=0).astype(BF16)


def select_kernel(slots, pieces, place, ids, probs, tokens, rows, mask, coefs, held, sems):
    tok, width = tokens.shape
    step = width // pieces
    copies = []
    for piece in range(pieces):
        at = slice(piece * step, (piece + 1) * step)
        copy = pltpu.make_async_copy(tokens.at[:, at], held.at[:, at], sems.at[piece])
        copy.start()
        copies.append(copy)
    below = lax.broadcasted_iota(jnp.int32, (tok, tok), 0)
    right = lax.broadcasted_iota(jnp.int32, (tok, tok), 1)
    upper = jnp.where(below <= right, 1.0, 0.0).astype(BF16)
    for slot in range(slots):
        expert = place[0, slot] * slots + slot
        match = ids[...] == expert
        hit = jnp.max(jnp.where(match, 1.0, 0.0), axis=0, keepdims=True)
        coef = jnp.sum(jnp.where(match, probs[...], 0.0), axis=0, keepdims=True)
        rank = jnp.dot(hit.astype(BF16), upper, preferred_element_type=F32)
        want = lax.broadcasted_iota(jnp.int32, (CAP, tok), 0).astype(F32) + 1.0
        chosen = jnp.where((rank == want) & (hit > 0.0), 1.0, 0.0)
        at = slice(slot * CAP, (slot + 1) * CAP)
        mask[at, :] = chosen.astype(BF16)
        total = jnp.sum(chosen * coef, axis=1, keepdims=True)
        coefs[at, :] = jnp.broadcast_to(total, (CAP, coefs.shape[1]))
    left = mask[...]
    for piece in range(pieces):
        at = slice(piece * step, (piece + 1) * step)
        copies[piece].wait()
        rows[:, at] = jnp.dot(left, held[:, at], preferred_element_type=F32).astype(BF16)


def select(placement, ids, probs, tokens, slots):
    tok, width = tokens.shape
    pieces = 4
    count = slots * CAP
    return pl.pallas_call(
        functools.partial(select_kernel, slots, pieces),
        in_specs=[SCALARS, LOCAL, LOCAL, pl.BlockSpec(memory_space=pltpu.HBM)],
        out_specs=[LOCAL] * 3,
        out_shape=[
            jax.ShapeDtypeStruct((count, width), BF16),
            jax.ShapeDtypeStruct((count, tok), BF16),
            jax.ShapeDtypeStruct((count, 128), F32),
        ],
        scratch_shapes=[pltpu.VMEM((tok, width), BF16), pltpu.SemaphoreType.DMA((pieces,))],
        compiler_params=PARAMS,
        cost_estimate=cost(2 * count * tok * width, tok * width * 2),
        name="select_rows",
    )(placement, ids, probs, tokens)


def scale_kernel(mask, coefs, grads, rows, blocks):
    groups, _, step = blocks.shape
    left = mask[...]
    coef = coefs[:, 0:1]
    for block in range(groups):
        at = slice(block * step, (block + 1) * step)
        picked = jnp.dot(left, grads[:, at], preferred_element_type=F32)
        scaled = (coef * picked).astype(BF16)
        rows[:, at] = scaled
        blocks[block] = scaled


def scale(mask, coefs, grads, groups):
    tok, width = grads.shape
    count = mask.shape[0]
    return pl.pallas_call(
        scale_kernel,
        in_specs=[LOCAL] * 3,
        out_specs=[LOCAL] * 2,
        out_shape=[
            jax.ShapeDtypeStruct((count, width), BF16),
            jax.ShapeDtypeStruct((groups, count, width // groups), BF16),
        ],
        compiler_params=PARAMS,
        cost_estimate=cost(2 * count * tok * width, tok * width * 2),
        name="scale_rows",
    )(mask, coefs, grads)


def forward_kernel(parts, place, *refs):
    blocks, (w_gate, w_up, pre_gate, pre_up, hidden) = refs[:parts], refs[parts:]
    inputs = rows_of([block[...] for block in blocks])
    gate = lax.dot_general(inputs, w_gate[...], NT, preferred_element_type=F32)
    up = lax.dot_general(inputs, w_up[...], NT, preferred_element_type=F32)
    pre_gate[...] = gate
    pre_up[...] = up
    count = gate.shape[0]
    hidden[0:count, :] = (gate * jax.nn.sigmoid(gate) * up).astype(BF16)
    tag = place[0, 0].astype(F32)
    hidden[count : count + TAG, :] = jnp.full((TAG, gate.shape[1]), tag, F32).astype(BF16)


def forward(my_cand, blocks, w_gate, w_up):
    units, width = w_gate.shape
    count = len(blocks) * CAP
    return pl.pallas_call(
        functools.partial(forward_kernel, len(blocks)),
        in_specs=[SCALARS] + [LOCAL] * (len(blocks) + 2),
        out_specs=[LOCAL] * 3,
        out_shape=[
            jax.ShapeDtypeStruct((count, units), F32),
            jax.ShapeDtypeStruct((count, units), F32),
            jax.ShapeDtypeStruct((count + TAG, units), BF16),
        ],
        compiler_params=PARAMS,
        cost_estimate=cost(4 * count * units * width, 4 * units * width),
        name="forward",
    )(my_cand, *blocks, w_gate, w_up)


def adam_kernel(groups, parts, me, *refs):
    hiddens, refs = refs[:groups], refs[groups:]
    blocks, refs = refs[:parts], refs[parts:]
    first, second, summed = refs[:3]
    dirs = refs[3:]
    count = parts * CAP
    rights = []
    lefts = [[] for _ in range(CANDS)]
    for peer in range(groups):
        held = hiddens[peer]
        part_rows = held[0:count, :].astype(F32)
        tag = held[count : count + TAG, :].astype(F32)[0:1, :]
        for cand in range(CANDS):
            lefts[cand].append(jnp.where(tag == float(cand), part_rows, 0.0))
        for part in range(parts):
            rights.append(blocks[part][me[0, 0] ^ peer].astype(F32))
    right = jnp.concatenate(rights, axis=0).astype(BF16)
    dir_list = []
    for cand in range(CANDS):
        left = jnp.concatenate(lefts[cand], axis=0).astype(BF16)
        grad = lax.dot_general(left, right, TN, preferred_element_type=F32)
        summed[cand] = grad
        one, two = moments(grad, first[cand], second[cand])
        dir_list.append(one / first_fix / (jnp.sqrt(two / second_fix) + adam_eps))
    for peer in range(groups):
        tag = hiddens[peer][count : count + TAG, :].astype(F32)[0:1, 0:1]
        out = dir_list[0]
        for cand in range(1, CANDS):
            out = jnp.where(tag == float(cand), dir_list[cand], out)
        dirs[peer][...] = out.astype(BF16)


def moments(gradient, first_moment, second):
    new_first = beta_one * first_moment + (1.0 - beta_one) * gradient
    new_second = beta_two * second + (1.0 - beta_two) * gradient * gradient
    return (new_first, new_second)


def adam(me, hiddens, blocks, first, second):
    groups, parts = len(hiddens), len(blocks)
    units, columns = first.shape[1:]
    rows = groups * parts * CAP
    return pl.pallas_call(
        functools.partial(adam_kernel, groups, parts),
        in_specs=[SCALARS] + [LOCAL] * (groups + parts + 2),
        out_specs=[LOCAL] * (1 + groups),
        out_shape=[jax.ShapeDtypeStruct(first.shape, F32)]
        + [jax.ShapeDtypeStruct((units, columns), BF16)] * groups,
        compiler_params=PARAMS,
        cost_estimate=cost(2 * CANDS * rows * units * columns, 8 * first.size),
        name="adam",
    )(me, *hiddens, *blocks, first, second)


def backward_kernel(parts, *refs):
    blocks, refs = refs[:parts], refs[parts:]
    w_down, w_gate, w_up, pre_gate, pre_up = refs[:5]
    outs = refs[5:]
    inputs = rows_of([block[...] for block in blocks])
    d_hidden = lax.dot_general(inputs, w_down[...], NT, preferred_element_type=F32)
    gate, up = pre_gate[...], pre_up[...]
    sig = jax.nn.sigmoid(gate)
    d_gate = (d_hidden * up * sig * (1.0 + gate * (1.0 - sig))).astype(BF16)
    d_up = (d_hidden * (gate * sig)).astype(BF16)
    width = w_gate.shape[1]
    step = width // 4
    for piece in range(4):
        at = slice(piece * step, (piece + 1) * step)
        out = jnp.dot(d_gate, w_gate[:, at], preferred_element_type=F32)
        out = out + jnp.dot(d_up, w_up[:, at], preferred_element_type=F32)
        for part in range(parts):
            outs[part][:, at] = out[part * CAP : (part + 1) * CAP, :].astype(BF16)


def backward(blocks, w_down, w_gate, w_up, pre_gate, pre_up):
    units, width = w_down.shape
    parts = len(blocks)
    count = parts * CAP
    return pl.pallas_call(
        functools.partial(backward_kernel, parts),
        in_specs=[LOCAL] * (parts + 5),
        out_specs=[LOCAL] * parts,
        out_shape=[jax.ShapeDtypeStruct((CAP, width), BF16)] * parts,
        compiler_params=PARAMS,
        cost_estimate=cost(6 * count * units * width, 6 * units * width),
        name="backward",
    )(*blocks, w_down, w_gate, w_up, pre_gate, pre_up)


def combine_kernel(parts, pieces, *refs):
    masks, blocks, out, held, sems = refs[0], refs[1 : 1 + parts], *refs[1 + parts :]
    width = out.shape[1]
    step = width // pieces
    left = masks[...]
    copies = []
    for piece in range(pieces):
        at = slice(piece * step, (piece + 1) * step)
        rows = rows_of([block[:, at] for block in blocks])
        held[:, at] = lax.dot_general(left, rows, TN, preferred_element_type=F32).astype(BF16)
        copy = pltpu.make_async_copy(held.at[:, at], out.at[:, at], sems.at[piece])
        copy.start()
        copies.append(copy)
    for copy in copies:
        copy.wait()


def combine(masks, blocks):
    count, tok = masks.shape
    width = blocks[0].shape[1]
    pieces = 4
    return pl.pallas_call(
        functools.partial(combine_kernel, len(blocks), pieces),
        in_specs=[LOCAL] * (1 + len(blocks)),
        out_specs=pl.BlockSpec(memory_space=pltpu.HBM),
        out_shape=jax.ShapeDtypeStruct((tok, width), BF16),
        scratch_shapes=[pltpu.VMEM((tok, width), BF16), pltpu.SemaphoreType.DMA((pieces,))],
        compiler_params=PARAMS,
        cost_estimate=cost(2 * count * tok * width, 2 * tok * width),
        name="combine",
    )(masks, *blocks)


def place_kernel(groups, me, *refs):
    blocks, out, sems = refs[:groups], refs[groups], refs[groups + 1]
    columns = blocks[0].shape[1]
    copies = []
    for peer in range(groups):
        start = pl.multiple_of((me[0, 0] ^ peer) * columns, 128)
        copies.append(
            pltpu.make_async_copy(
                blocks[peer], out.at[:, pl.ds(start, columns)], sems.at[peer]
            )
        )
        copies[-1].start()
    for copy in copies:
        copy.wait()


def place_blocks(me, blocks):
    groups = len(blocks)
    units, columns = blocks[0].shape
    return pl.pallas_call(
        functools.partial(place_kernel, groups),
        in_specs=[SCALARS] + [LOCAL] * groups,
        out_specs=pl.BlockSpec(memory_space=pltpu.HBM),
        out_shape=jax.ShapeDtypeStruct((units, groups * columns), BF16),
        scratch_shapes=[pltpu.SemaphoreType.DMA((groups,))],
        compiler_params=PARAMS,
        cost_estimate=cost(0, 4 * groups * units * columns),
        name="place_blocks",
    )(me, *blocks)


def swap(value, axis, size, bits):
    return lax.ppermute(value, axis, [(i, i ^ bits) for i in range(size)])


def body(
    tokens,
    expert_ids,
    gate_probs,
    placement,
    gate_weight,
    up_weight,
    down_weight,
    out_grad,
    moment_first,
    moment_second,
):
    num_ep = lax.axis_size("ep")
    groups = lax.axis_size("grp")
    slots = num_ep // QUARTERS
    ep_index = lax.axis_index("ep")
    me = lax.axis_index("grp").astype(jnp.int32).reshape(1, 1)

    def slot_of(bits):
        return (ep_index ^ bits) // QUARTERS

    def of_slot(value, bits, axis):
        if slots == 1:
            return lax.squeeze(value, (axis,))
        return lax.dynamic_index_in_dim(value, slot_of(bits), axis, keepdims=False)

    def share(value, axis):
        got = [None] * num_ep
        for far in range(0, num_ep, 2):
            piece = of_slot(value, far, axis)
            got[far] = swap(piece, "ep", num_ep, far) if far else piece
        for far in range(0, num_ep, 2):
            got[far + 1] = swap(got[far], "ep", num_ep, 1)
        return got

    def exchange(values):
        got = [values[0]]
        for bits in range(1, groups):
            got.append(swap(values[bits], "grp", groups, bits))
        return got

    def per_slot(value):
        return value.reshape((slots, CAP) + value.shape[1:])

    w_gate = gate_weight[0].T
    w_up = up_weight[0].T
    w_down = down_weight[0]

    rows, mask, coefs = select(placement, expert_ids.T, gate_probs.T, tokens, slots)
    in_rows = share(per_slot(rows), 0)
    scaled, blocks = scale(mask, coefs, out_grad, groups)
    columns = lax.all_to_all(blocks, "grp", split_axis=0, concat_axis=0, tiled=True)
    columns = share(columns.reshape(groups, slots, CAP, columns.shape[-1]), 1)
    my_cand = placement
    if slots > 1:
        my_cand = lax.dynamic_index_in_dim(placement, slot_of(0), 1, keepdims=True)
    pre_gate, pre_up, hidden = forward(my_cand, in_rows, w_gate, w_up)
    hiddens = exchange([hidden] * groups)
    summed, *dirs = adam(me, hiddens, columns, moment_first, moment_second)
    got_dirs = exchange(dirs)
    new_first, new_second = moments(summed, moment_first, moment_second)

    in_scaled = share(per_slot(scaled), 0)
    partials = backward(in_scaled, w_down, w_gate, w_up, pre_gate, pre_up)
    returned = [partials[0]]
    for bits in range(1, num_ep):
        returned.append(swap(partials[bits], "ep", num_ep, bits))
    masks = per_slot(mask)
    masks = jnp.concatenate([of_slot(masks, bits, 0) for bits in range(num_ep)], axis=0)
    token_grad = combine(masks, returned)
    step_dir = place_blocks(me, got_dirs)[None]
    return (token_grad, step_dir, new_first, new_second)


def solution(mesh):
    return jax.shard_map(
        body,
        mesh=mesh,
        in_specs=(
            P(("grp", "ep"), None),
            P(("grp", "ep"), None),
            P(("grp", "ep"), None),
            P("grp", None),
            P("grp", None, "ep"),
            P("grp", None, "ep"),
            P("grp", "ep", None),
            P(("grp", "ep"), None),
            P(None, "ep", "grp"),
            P(None, "ep", "grp"),
        ),
        out_specs=(
            P(("grp", "ep"), None),
            P("grp", "ep", None),
            P(None, "ep", "grp"),
            P(None, "ep", "grp"),
        ),
        check_vma=False,
    )
```

profile of v0, /device:TPU:8, one launch (start us, length us, event | category | flops | bytes accessed | tf_op | source)
XLA Modules:
  0.0 111.9 jit_solution(5775224428414616469)
XLA Ops:
  1.3 1.4 %copy-done.4 = bf16[192,4096]{1,0:T(8,128)(2,1)S(1)} copy-done((bf16[192,4096]{1,0:T(8,128)(2,1)S(1)}, bf16[192,4096]{1,0:T(8,128)(2,1)}, u32[]{:S(2)}) %copy-start.4) | copy-done | bytes 1572888
  2.7 0.7 copy-done.20
  3.4 0.7 copy-done.21
  4.1 1.2 %select_rows.1 = (bf16[24,4096]{1,0:T(8,128)(2,1)S(1)}, bf16[24,192]{1,0:T(8,128)(2,1)S(1)}, f32[24,128]{1,0:T(8,128)S(1)}) custom-call(s32[1,1]{1,0:T(1,128)S(6)} %copy.14.place, s32[8,192]{1,0:T(8,128)S(1)} %bitcast.16, f32[8,192]{1,0:T(8,128)S(1)} %bitcast.17, bf16[192,4096]{1,0:T(8,128)(2,1)S(1)} %copy-done.4), custom_call_target="tpu_custom_call" | custom-call | flops 37748736 | bytes 1572864 | tf_op jit(solution)/shard_map/select_rows/pallas_call | solution.py:78
  5.3 0.0 copy-start.11
  5.3 0.7 copy-done.11
  6.0 1.4 %copy-done.5 = bf16[192,4096]{1,0:T(8,128)(2,1)S(1)} copy-done((bf16[192,4096]{1,0:T(8,128)(2,1)S(1)}, bf16[192,4096]{1,0:T(8,128)(2,1)}, u32[]{:S(2)}) %copy-start.5) | copy-done | bytes 1572888
  7.4 0.4 scale_rows.1
  7.8 0.7 copy-done.13
  8.5 6.3 %all-to-all-start = ((bf16[8,24,512]{2,1,0:T(8,128)(2,1)}), bf16[8,24,512]{2,1,0:T(8,128)(2,1)S(1)}, u32[]{:S(2)}, u32[]{:S(2)}) async-start(bf16[8,24,512]{2,1,0:T(8,128)(2,1)} %copy-done.13), calls=%async_computation | async-start | bytes 393216 | tf_op jit(solution)/shard_map/all_to_all | solution.py:362
  14.7 1.5 %collective-permute-start.4 = (bf16[24,4096]{1,0:T(8,128)(2,1)}, bf16[24,4096]{1,0:T(8,128)(2,1)}, u32[]{:S(2)}, u32[]{:S(2)}) collective-permute-start(bf16[24,4096]{1,0:T(8,128)(2,1)} %copy-done.11), channel_id=1, source_target_pairs={{0,2},{1,3},{2,0},{3,1},{4,6},{5,7},{6,4},{7,5},{8,10},{9,11},{10,... | collective-permute-start | bytes 589832 | tf_op jit(solution)/shard_map/ppermute | solution.py:308
  16.2 0.5 collective-permute-start.1
  16.8 4.2 %all-to-all-done.refs_8_ = bf16[8,24,512]{2,1,0:T(8,128)(2,1)S(1)} async-done(((bf16[8,24,512]{2,1,0:T(8,128)(2,1)}), bf16[8,24,512]{2,1,0:T(8,128)(2,1)S(1)}, u32[]{:S(2)}, u32[]{:S(2)}) %all-to-all-start) | async-done | bytes 196640 | tf_op jit(solution)/shard_map/all_to_all | solution.py:362
  20.9 1.5 %collective-permute-start.17 = (bf16[8,24,512]{2,1,0:T(8,128)(2,1)S(1)}, bf16[8,24,512]{2,1,0:T(8,128)(2,1)}, u32[]{:S(2)}, u32[]{:S(2)}) collective-permute-start(bf16[8,24,512]{2,1,0:T(8,128)(2,1)S(1)} %all-to-all-done.refs_8_), channel_id=1, source_target_pairs={{0,2},{1,3},{2,0},{3,1},{4,6},{5,7},{6,4},{7,5},{8,10},{9,11},{10,... | collective-permute-start | bytes 589832 | tf_op jit(solution)/shard_map/ppermute | solution.py:308
  22.4 0.4 collective-permute-done.4.refs_2_
  22.8 0.0 collective-permute-start.5
  22.8 0.5 collective-permute-start
  23.3 3.7 %collective-permute-done.1.refs_2_ = bf16[24,4096]{1,0:T(8,128)(2,1)} collective-permute-done((bf16[24,4096]{1,0:T(8,128)(2,1)S(1)}, bf16[24,4096]{1,0:T(8,128)(2,1)}, u32[]{:S(2)}, u32[]{:S(2)}) %collective-permute-start.1) | collective-permute-done | bytes 196640 | tf_op jit(solution)/shard_map/ppermute | solution.py:308
  27.0 0.5 collective-permute-start.16
  27.6 2.0 %collective-permute-done.17.refs_10_ = bf16[8,24,512]{2,1,0:T(8,128)(2,1)} collective-permute-done((bf16[8,24,512]{2,1,0:T(8,128)(2,1)S(1)}, bf16[8,24,512]{2,1,0:T(8,128)(2,1)}, u32[]{:S(2)}, u32[]{:S(2)}) %collective-permute-start.17) | collective-permute-done | bytes 196640 | tf_op jit(solution)/shard_map/ppermute | solution.py:308
  29.6 0.0 copy-start.12
  29.6 0.9 copy-done.12
  30.5 2.8 %forward.1 = (f32[96,192]{1,0:T(8,128)S(1)}, f32[96,192]{1,0:T(8,128)S(1)}, bf16[112,192]{1,0:T(8,128)(2,1)}) custom-call(s32[1,1]{1,0:T(1,128)S(6)} %copy.14.place, bf16[24,4096]{1,0:T(8,128)(2,1)S(1)} %copy-done.12, bf16[24,4096]{1,0:T(8,128)(2,1)} %collective-permute-done.3.refs_1_, bf16[24,4096]{1,0:T(8,128)(2,1)} %collective-permute-done.4.refs_2_, ...), custom_call_target="tpu_custom_call" | custom-call | flops 301989888 | bytes 3145728 | tf_op jit(solution)/shard_map/forward/pallas_call | solution.py:139
  33.3 0.6 copy-done.14
  33.9 0.6 copy-done.16
  34.6 2.4 %collective-permute-start.15 = (bf16[112,192]{1,0:T(8,128)(2,1)}, bf16[112,192]{1,0:T(8,128)(2,1)S(1)}, u32[]{:S(2)}, u32[]{:S(2)}) collective-permute-start(bf16[112,192]{1,0:T(8,128)(2,1)} %get-tuple-element.35.refs_0_), channel_id=1, source_target_pairs={{0,28},{4,24},{8,20},{12,16},{16,12},{20,8},{24,4},{28,0},{1,29},{... | collective-permute-start | bytes 129032 | tf_op jit(solution)/shard_map/ppermute | solution.py:308
  36.9 0.7 copy-done.7
  37.6 0.6 collective-permute-start.14
  38.2 0.7 copy-done.9
  38.9 4.2 %collective-permute-start.13 = (bf16[112,192]{1,0:T(8,128)(2,1)}, bf16[112,192]{1,0:T(8,128)(2,1)}, u32[]{:S(2)}, u32[]{:S(2)}) collective-permute-start(bf16[112,192]{1,0:T(8,128)(2,1)} %get-tuple-element.35.refs_0_), channel_id=1, source_target_pairs={{0,20},{4,16},{8,28},{12,24},{16,4},{20,0},{24,12},{28,8},{1,21},{... | collective-permute-start | bytes 129032 | tf_op jit(solution)/shard_map/ppermute | solution.py:308
  43.0 0.6 copy-done.18
  43.6 1.7 %collective-permute-start.12 = (bf16[112,192]{1,0:T(8,128)(2,1)}, bf16[112,192]{1,0:T(8,128)(2,1)}, u32[]{:S(2)}, u32[]{:S(2)}) collective-permute-start(bf16[112,192]{1,0:T(8,128)(2,1)} %get-tuple-element.35.refs_0_), channel_id=1, source_target_pairs={{0,16},{4,20},{8,24},{12,28},{16,0},{20,4},{24,8},{28,12},{1,17},{... | collective-permute-start | bytes 129032 | tf_op jit(solution)/shard_map/ppermute | solution.py:308
  45.3 1.6 %collective-permute-start.11 = (bf16[112,192]{1,0:T(8,128)(2,1)}, bf16[112,192]{1,0:T(8,128)(2,1)}, u32[]{:S(2)}, u32[]{:S(2)}) collective-permute-start(bf16[112,192]{1,0:T(8,128)(2,1)} %get-tuple-element.35.refs_0_), channel_id=1, source_target_pairs={{0,12},{4,8},{8,4},{12,0},{16,28},{20,24},{24,20},{28,16},{1,13},{... | collective-permute-start | bytes 129032 | tf_op jit(solution)/shard_map/ppermute | solution.py:308
  46.9 0.0 collective-permute-done.13.refs_5_
  46.9 1.8 %collective-permute-start.10 = (bf16[112,192]{1,0:T(8,128)(2,1)}, bf16[112,192]{1,0:T(8,128)(2,1)}, u32[]{:S(2)}, u32[]{:S(2)}) collective-permute-start(bf16[112,192]{1,0:T(8,128)(2,1)} %get-tuple-element.35.refs_0_), channel_id=1, source_target_pairs={{0,8},{4,12},{8,0},{12,4},{16,24},{20,28},{24,16},{28,20},{1,9},{5... | collective-permute-start | bytes 129032 | tf_op jit(solution)/shard_map/ppermute | solution.py:308
  48.8 0.4 collective-permute-done.12.refs_4_
  49.1 1.9 %collective-permute-start.9 = (bf16[112,192]{1,0:T(8,128)(2,1)}, bf16[112,192]{1,0:T(8,128)(2,1)}, u32[]{:S(2)}, u32[]{:S(2)}) collective-permute-start(bf16[112,192]{1,0:T(8,128)(2,1)} %get-tuple-element.35.refs_0_), channel_id=1, source_target_pairs={{0,4},{4,0},{8,12},{12,8},{16,20},{20,16},{24,28},{28,24},{1,5},{5... | collective-permute-start | bytes 129032 | tf_op jit(solution)/shard_map/ppermute | solution.py:308
  51.1 1.4 %copy-done.6 = bf16[1,192,4096]{2,1,0:T(8,128)(2,1)S(1)} copy-done((bf16[1,192,4096]{2,1,0:T(8,128)(2,1)S(1)}, bf16[1,192,4096]{2,1,0:T(8,128)(2,1)}, u32[]{:S(2)}) %copy-start.6) | copy-done | bytes 1572888
  52.5 0.9 copy-done.8
  53.4 0.9 copy-done.10
  54.3 0.9 copy-done.15
  55.2 0.9 copy-done.17
  56.1 2.9 %backward.1 = (bf16[24,4096]{1,0:T(8,128)(2,1)S(1)}, bf16[24,4096]{1,0:T(8,128)(2,1)S(1)}, bf16[24,4096]{1,0:T(8,128)(2,1)S(1)}, bf16[24,4096]{1,0:T(8,128)(2,1)S(1)}) custom-call(bf16[24,4096]{1,0:T(8,128)(2,1)S(1)} %get-tuple-element.27.refs_0_, bf16[24,4096]{1,0:T(8,128)(2,1)S(1)} %copy-done.8, bf16[24,4096]{1,0:T(8,128)(2,1)} %collective-permute-done.1.refs_2_, ...), custom_call_target="tpu_custom_call" | custom-call | flops 452984832 | bytes 4718592 | tf_op jit(solution)/shard_map/backward/pallas_call | solution.py:232
  59.1 0.1 collective-permute-start.6
  59.2 1.6 %collective-permute-start.7 = (bf16[24,4096]{1,0:T(8,128)(2,1)S(1)}, bf16[24,4096]{1,0:T(8,128)(2,1)S(1)}, u32[]{:S(2)}, u32[]{:S(2)}) collective-permute-start(bf16[24,4096]{1,0:T(8,128)(2,1)S(1)} %get-tuple-element.33), channel_id=1, source_target_pairs={{0,2},{1,3},{2,0},{3,1},{4,6},{5,7},{6,4},{7,5},{8,10},{9,11},{10,... | collective-permute-start | bytes 589832 | tf_op jit(solution)/shard_map/ppermute | solution.py:308
  60.7 0.3 collective-permute-start.8
  61.0 2.4 %adam.1 = (f32[2,192,512]{2,1,0:T(8,128)S(1)}, bf16[192,512]{1,0:T(8,128)(2,1)S(1)}, bf16[192,512]{1,0:T(8,128)(2,1)S(1)}, bf16[192,512]{1,0:T(8,128)(2,1)S(1)},...) custom-call(s32[1,1]{1,0:T(1,128)} %bitcast.9.me, ...), custom_call_target="tpu_custom_call" | custom-call | flops 301989888 | bytes 1572864 | tf_op jit(solution)/shard_map/adam/pallas_call | solution.py:196
  63.5 0.2 collective-permute-start.19
  63.6 1.7 %collective-permute-start.20 = (bf16[192,512]{1,0:T(8,128)(2,1)S(1)}, bf16[192,512]{1,0:T(8,128)(2,1)S(1)}, u32[]{:S(2)}, u32[]{:S(2)}) collective-permute-start(bf16[192,512]{1,0:T(8,128)(2,1)S(1)} %get-tuple-element.39), channel_id=1, source_target_pairs={{0,8},{4,12},{8,0},{12,4},{16,24},{20,28},{24,16},{28,20},{1,9},{5... | collective-permute-start | bytes 589832 | tf_op jit(solution)/shard_map/ppermute | solution.py:308
  65.3 1.7 %collective-permute-done.7.refs_3_ = bf16[24,4096]{1,0:T(8,128)(2,1)S(1)} collective-permute-done((bf16[24,4096]{1,0:T(8,128)(2,1)S(1)}, bf16[24,4096]{1,0:T(8,128)(2,1)S(1)}, u32[]{:S(2)}, u32[]{:S(2)}) %collective-permute-start.7) | collective-permute-done | bytes 196640 | tf_op jit(solution)/shard_map/ppermute | solution.py:308
  67.0 3.1 %collective-permute-done.8.refs_4_ = bf16[24,4096]{1,0:T(8,128)(2,1)S(1)} collective-permute-done((bf16[24,4096]{1,0:T(8,128)(2,1)S(1)}, bf16[24,4096]{1,0:T(8,128)(2,1)S(1)}, u32[]{:S(2)}, u32[]{:S(2)}) %collective-permute-start.8) | collective-permute-done | bytes 196640 | tf_op jit(solution)/shard_map/ppermute | solution.py:308
  70.1 1.5 %combine.1 = bf16[192,4096]{1,0:T(8,128)(2,1)} custom-call(bf16[96,192]{1,0:T(8,128)(2,1)S(1)} %pad_maximum_fusion.refs_0_, bf16[24,4096]{1,0:T(8,128)(2,1)S(1)} %get-tuple-element.31.refs_1_, bf16[24,4096]{1,0:T(8,128)(2,1)S(1)} %collective-permute-done.6.refs_2_, bf16[24,4096]{1,0:T(8,128)(2,1)S(1)} %collective-permute-done.7.refs_3_, ...), custom_call_target="tpu_custom_call" | custom-call | flops 150994944 | bytes 1572864 | tf_op jit(solution)/shard_map/combine/pallas_call | solution.py:264
  71.6 1.3 %collective-permute-start.21 = (bf16[192,512]{1,0:T(8,128)(2,1)S(1)}, bf16[192,512]{1,0:T(8,128)(2,1)S(1)}, u32[]{:S(2)}, u32[]{:S(2)}) collective-permute-start(bf16[192,512]{1,0:T(8,128)(2,1)S(1)} %get-tuple-element.40), channel_id=1, source_target_pairs={{0,12},{4,8},{8,4},{12,0},{16,28},{20,24},{24,20},{28,16},{1,13},{... | collective-permute-start | bytes 589832 | tf_op jit(solution)/shard_map/ppermute | solution.py:308
  72.9 2.2 %collective-permute-start.22 = (bf16[192,512]{1,0:T(8,128)(2,1)S(1)}, bf16[192,512]{1,0:T(8,128)(2,1)S(1)}, u32[]{:S(2)}, u32[]{:S(2)}) collective-permute-start(bf16[192,512]{1,0:T(8,128)(2,1)S(1)} %get-tuple-element.41), channel_id=1, source_target_pairs={{0,16},{4,20},{8,24},{12,28},{16,0},{20,4},{24,8},{28,12},{1,17},{... | collective-permute-start | bytes 589832 | tf_op jit(solution)/shard_map/ppermute | solution.py:308
  75.1 0.4 collective-permute-start.23
  75.5 1.7 %collective-permute-start.24 = (bf16[192,512]{1,0:T(8,128)(2,1)S(1)}, bf16[192,512]{1,0:T(8,128)(2,1)S(1)}, u32[]{:S(2)}, u32[]{:S(2)}) collective-permute-start(bf16[192,512]{1,0:T(8,128)(2,1)S(1)} %get-tuple-element.43), channel_id=1, source_target_pairs={{0,24},{4,28},{8,16},{12,20},{16,8},{20,12},{24,0},{28,4},{1,25},{... | collective-permute-start | bytes 589832 | tf_op jit(solution)/shard_map/ppermute | solution.py:308
  77.2 1.5 %collective-permute-start.25 = (bf16[192,512]{1,0:T(8,128)(2,1)S(1)}, bf16[192,512]{1,0:T(8,128)(2,1)S(1)}, u32[]{:S(2)}, u32[]{:S(2)}) collective-permute-start(bf16[192,512]{1,0:T(8,128)(2,1)S(1)} %get-tuple-element.44), channel_id=1, source_target_pairs={{0,28},{4,24},{8,20},{12,16},{16,12},{20,8},{24,4},{28,0},{1,29},{... | collective-permute-start | bytes 589832 | tf_op jit(solution)/shard_map/ppermute | solution.py:308
  78.7 1.4 %fusion = (f32[2,192,512]{2,1,0:T(8,128)}, f32[2,192,512]{2,1,0:T(8,128)}) fusion(f32[2,192,512]{2,1,0:T(8,128)S(1)} %get-tuple-element.45, f32[2,192,512]{2,1,0:T(8,128)S(1)} %copy-done.3, f32[2,192,512]{2,1,0:T(8,128)S(1)} %copy-done.2), kind=kLoop, calls=%fused_computation.1 | loop fusion | flops 1376256 | bytes 3932160 | tf_op jit(solution)/shard_map/add | solution.py:188
  80.2 2.6 %collective-permute-done.21.refs_3_ = bf16[192,512]{1,0:T(8,128)(2,1)S(1)} collective-permute-done((bf16[192,512]{1,0:T(8,128)(2,1)S(1)}, bf16[192,512]{1,0:T(8,128)(2,1)S(1)}, u32[]{:S(2)}, u32[]{:S(2)}) %collective-permute-start.21) | collective-permute-done | bytes 196640 | tf_op jit(solution)/shard_map/ppermute | solution.py:308
  82.8 14.5 %collective-permute-done.22.refs_4_ = bf16[192,512]{1,0:T(8,128)(2,1)S(1)} collective-permute-done((bf16[192,512]{1,0:T(8,128)(2,1)S(1)}, bf16[192,512]{1,0:T(8,128)(2,1)S(1)}, u32[]{:S(2)}, u32[]{:S(2)}) %collective-permute-start.22) | collective-permute-done | bytes 196640 | tf_op jit(solution)/shard_map/ppermute | solution.py:308
  97.3 4.2 %collective-permute-done.23.refs_5_ = bf16[192,512]{1,0:T(8,128)(2,1)S(1)} collective-permute-done((bf16[192,512]{1,0:T(8,128)(2,1)S(1)}, bf16[192,512]{1,0:T(8,128)(2,1)S(1)}, u32[]{:S(2)}, u32[]{:S(2)}) %collective-permute-start.23) | collective-permute-done | bytes 196640 | tf_op jit(solution)/shard_map/ppermute | solution.py:308
  101.5 4.3 %collective-permute-done.24.refs_6_ = bf16[192,512]{1,0:T(8,128)(2,1)S(1)} collective-permute-done((bf16[192,512]{1,0:T(8,128)(2,1)S(1)}, bf16[192,512]{1,0:T(8,128)(2,1)S(1)}, u32[]{:S(2)}, u32[]{:S(2)}) %collective-permute-start.24) | collective-permute-done | bytes 196640 | tf_op jit(solution)/shard_map/ppermute | solution.py:308
  105.7 5.0 %collective-permute-done.25.refs_7_ = bf16[192,512]{1,0:T(8,128)(2,1)S(1)} collective-permute-done((bf16[192,512]{1,0:T(8,128)(2,1)S(1)}, bf16[192,512]{1,0:T(8,128)(2,1)S(1)}, u32[]{:S(2)}, u32[]{:S(2)}) %collective-permute-start.25) | collective-permute-done | bytes 196640 | tf_op jit(solution)/shard_map/ppermute | solution.py:308
  110.7 1.2 %place_blocks.1 = bf16[192,4096]{1,0:T(8,128)(2,1)} custom-call(s32[1,1]{1,0:T(1,128)} %bitcast.9.me, bf16[192,512]{1,0:T(8,128)(2,1)S(1)} %get-tuple-element.37.refs_0_, bf16[192,512]{1,0:T(8,128)(2,1)S(1)} %collective-permute-done.19.refs_1_, bf16[192,512]{1,0:T(8,128)(2,1)S(1)} %collective-permute-done.20.refs_2_, ...), custom_call_target="tpu_custom_call" | custom-call | bytes 3145728 | tf_op jit(solution)/shard_map/place_blocks/pallas_call | solution.py:295
  (43 shorter events, 0.1 us)
Async XLA Ops:
  1.3 1.4 %copy-start.4 = (bf16[192,4096]{1,0:T(8,128)(2,1)S(1)}, bf16[192,4096]{1,0:T(8,128)(2,1)}, u32[]{:S(2)}) copy-start(bf16[192,4096]{1,0:T(8,128)(2,1)} %tokens.1) | copy-start | bytes 4718596
  2.7 0.7 copy-start.20
  3.4 0.7 copy-start.21
  4.1 25.5 %copy-start = (bf16[1,4096,192]{1,2,0:T(8,128)(2,1)S(1)}, bf16[1,4096,192]{1,2,0:T(8,128)(2,1)}, u32[]{:S(2)}) copy-start(bf16[1,4096,192]{1,2,0:T(8,128)(2,1)} %param.14) | copy-start | bytes 4718596
  4.1 25.5 %copy-start.1 = (bf16[1,4096,192]{1,2,0:T(8,128)(2,1)S(1)}, bf16[1,4096,192]{1,2,0:T(8,128)(2,1)}, u32[]{:S(2)}) copy-start(bf16[1,4096,192]{1,2,0:T(8,128)(2,1)} %param.15) | copy-start | bytes 4718596
  5.3 0.7 copy-start.11
  6.0 1.4 %copy-start.5 = (bf16[192,4096]{1,0:T(8,128)(2,1)S(1)}, bf16[192,4096]{1,0:T(8,128)(2,1)}, u32[]{:S(2)}) copy-start(bf16[192,4096]{1,0:T(8,128)(2,1)} %grads.1) | copy-start | bytes 4718596
  7.8 0.7 copy-start.13
  8.5 12.5 %all-to-all-start = ((bf16[8,24,512]{2,1,0:T(8,128)(2,1)}), bf16[8,24,512]{2,1,0:T(8,128)(2,1)S(1)}, u32[]{:S(2)}, u32[]{:S(2)}) async-start(bf16[8,24,512]{2,1,0:T(8,128)(2,1)} %copy-done.13), calls=%async_computation | async-start | bytes 393216 | tf_op jit(solution)/shard_map/all_to_all | solution.py:362
  14.7 8.1 %collective-permute-start.4 = (bf16[24,4096]{1,0:T(8,128)(2,1)}, bf16[24,4096]{1,0:T(8,128)(2,1)}, u32[]{:S(2)}, u32[]{:S(2)}) collective-permute-start(bf16[24,4096]{1,0:T(8,128)(2,1)} %copy-done.11), channel_id=1, source_target_pairs={{0,2},{1,3},{2,0},{3,1},{4,6},{5,7},{6,4},{7,5},{8,10},{9,11},{10,... | collective-permute-start | bytes 589832 | tf_op jit(solution)/shard_map/ppermute | solution.py:308
  16.2 10.8 %collective-permute-start.1 = (bf16[24,4096]{1,0:T(8,128)(2,1)S(1)}, bf16[24,4096]{1,0:T(8,128)(2,1)}, u32[]{:S(2)}, u32[]{:S(2)}) collective-permute-start(bf16[24,4096]{1,0:T(8,128)(2,1)S(1)} %get-tuple-element.27.refs_0_), channel_id=1, source_target_pairs={{0,2},{1,3},{2,0},{3,1},{4,6},{5,7},{6,4},{7,5},{8,10},{9,11},{10,... | collective-permute-start | bytes 589832 | tf_op jit(solution)/shard_map/ppermute | solution.py:308
  16.8 10.3 %collective-permute-start.3 = (bf16[24,4096]{1,0:T(8,128)(2,1)}, bf16[24,4096]{1,0:T(8,128)(2,1)}, u32[]{:S(2)}, u32[]{:S(2)}) collective-permute-start(bf16[24,4096]{1,0:T(8,128)(2,1)} %copy-done.11), channel_id=1, source_target_pairs={{0,1},{1,0},{2,3},{3,2},{4,5},{5,4},{6,7},{7,6},{8,9},{9,8},{10,11... | collective-permute-start | bytes 589832 | tf_op jit(solution)/shard_map/ppermute | solution.py:308
  20.9 8.6 %collective-permute-start.17 = (bf16[8,24,512]{2,1,0:T(8,128)(2,1)S(1)}, bf16[8,24,512]{2,1,0:T(8,128)(2,1)}, u32[]{:S(2)}, u32[]{:S(2)}) collective-permute-start(bf16[8,24,512]{2,1,0:T(8,128)(2,1)S(1)} %all-to-all-done.refs_8_), channel_id=1, source_target_pairs={{0,2},{1,3},{2,0},{3,1},{4,6},{5,7},{6,4},{7,5},{8,10},{9,11},{10,... | collective-permute-start | bytes 589832 | tf_op jit(solution)/shard_map/ppermute | solution.py:308
  22.8 6.7 %collective-permute-start.5 = (bf16[24,4096]{1,0:T(8,128)(2,1)}, bf16[24,4096]{1,0:T(8,128)(2,1)S(1)}, u32[]{:S(2)}, u32[]{:S(2)}) collective-permute-start(bf16[24,4096]{1,0:T(8,128)(2,1)} %collective-permute-done.4.refs_2_), channel_id=1, source_target_pairs={{0,1},{1,0},{2,3},{3,2},{4,5},{5,4},{6,7},{7,6},{8,9},{9,8},{10,11... | collective-permute-start | bytes 589832 | tf_op jit(solution)/shard_map/ppermute | solution.py:308
  22.8 14.1 %collective-permute-start = (bf16[24,4096]{1,0:T(8,128)(2,1)S(1)}, bf16[24,4096]{1,0:T(8,128)(2,1)S(1)}, u32[]{:S(2)}, u32[]{:S(2)}) collective-permute-start(bf16[24,4096]{1,0:T(8,128)(2,1)S(1)} %get-tuple-element.27.refs_0_), channel_id=1, source_target_pairs={{0,1},{1,0},{2,3},{3,2},{4,5},{5,4},{6,7},{7,6},{8,9},{9,8},{10,11... | collective-permute-start | bytes 589832 | tf_op jit(solution)/shard_map/ppermute | solution.py:308
  27.0 11.1 %collective-permute-start.2 = (bf16[24,4096]{1,0:T(8,128)(2,1)}, bf16[24,4096]{1,0:T(8,128)(2,1)S(1)}, u32[]{:S(2)}, u32[]{:S(2)}) collective-permute-start(bf16[24,4096]{1,0:T(8,128)(2,1)} %collective-permute-done.1.refs_2_), channel_id=1, source_target_pairs={{0,1},{1,0},{2,3},{3,2},{4,5},{5,4},{6,7},{7,6},{8,9},{9,8},{10,11... | collective-permute-start | bytes 589832 | tf_op jit(solution)/shard_map/ppermute | solution.py:308
  27.0 34.0 %collective-permute-start.16 = (bf16[8,24,512]{2,1,0:T(8,128)(2,1)S(1)}, bf16[8,24,512]{2,1,0:T(8,128)(2,1)}, u32[]{:S(2)}, u32[]{:S(2)}) collective-permute-start(bf16[8,24,512]{2,1,0:T(8,128)(2,1)S(1)} %all-to-all-done.refs_8_), channel_id=1, source_target_pairs={{0,1},{1,0},{2,3},{3,2},{4,5},{5,4},{6,7},{7,6},{8,9},{9,8},{10,11... | collective-permute-start | bytes 589832 | tf_op jit(solution)/shard_map/ppermute | solution.py:308
  29.6 31.5 %collective-permute-start.18 = (bf16[8,24,512]{2,1,0:T(8,128)(2,1)}, bf16[8,24,512]{2,1,0:T(8,128)(2,1)}, u32[]{:S(2)}, u32[]{:S(2)}) collective-permute-start(bf16[8,24,512]{2,1,0:T(8,128)(2,1)} %collective-permute-done.17.refs_10_), channel_id=1, source_target_pairs={{0,1},{1,0},{2,3},{3,2},{4,5},{5,4},{6,7},{7,6},{8,9},{9,8},{10,11... | collective-permute-start | bytes 589832 | tf_op jit(solution)/shard_map/ppermute | solution.py:308
  29.6 0.9 copy-start.12
  33.3 0.6 copy-start.14
  33.9 0.6 copy-start.16
  34.6 8.5 %collective-permute-start.15 = (bf16[112,192]{1,0:T(8,128)(2,1)}, bf16[112,192]{1,0:T(8,128)(2,1)S(1)}, u32[]{:S(2)}, u32[]{:S(2)}) collective-permute-start(bf16[112,192]{1,0:T(8,128)(2,1)} %get-tuple-element.35.refs_0_), channel_id=1, source_target_pairs={{0,28},{4,24},{8,20},{12,16},{16,12},{20,8},{24,4},{28,0},{1,29},{... | collective-permute-start | bytes 129032 | tf_op jit(solution)/shard_map/ppermute | solution.py:308
  36.9 0.7 copy-start.7
  37.6 7.7 %collective-permute-start.14 = (bf16[112,192]{1,0:T(8,128)(2,1)}, bf16[112,192]{1,0:T(8,128)(2,1)}, u32[]{:S(2)}, u32[]{:S(2)}) collective-permute-start(bf16[112,192]{1,0:T(8,128)(2,1)} %get-tuple-element.35.refs_0_), channel_id=1, source_target_pairs={{0,24},{4,28},{8,16},{12,20},{16,8},{20,12},{24,0},{28,4},{1,25},{... | collective-permute-start | bytes 129032 | tf_op jit(solution)/shard_map/ppermute | solution.py:308
  38.2 0.7 copy-start.9
  38.9 8.1 %collective-permute-start.13 = (bf16[112,192]{1,0:T(8,128)(2,1)}, bf16[112,192]{1,0:T(8,128)(2,1)}, u32[]{:S(2)}, u32[]{:S(2)}) collective-permute-start(bf16[112,192]{1,0:T(8,128)(2,1)} %get-tuple-element.35.refs_0_), channel_id=1, source_target_pairs={{0,20},{4,16},{8,28},{12,24},{16,4},{20,0},{24,12},{28,8},{1,21},{... | collective-permute-start | bytes 129032 | tf_op jit(solution)/shard_map/ppermute | solution.py:308
  43.0 0.6 copy-start.18
  43.6 5.5 %collective-permute-start.12 = (bf16[112,192]{1,0:T(8,128)(2,1)}, bf16[112,192]{1,0:T(8,128)(2,1)}, u32[]{:S(2)}, u32[]{:S(2)}) collective-permute-start(bf16[112,192]{1,0:T(8,128)(2,1)} %get-tuple-element.35.refs_0_), channel_id=1, source_target_pairs={{0,16},{4,20},{8,24},{12,28},{16,0},{20,4},{24,8},{28,12},{1,17},{... | collective-permute-start | bytes 129032 | tf_op jit(solution)/shard_map/ppermute | solution.py:308
  45.3 13.7 %collective-permute-start.11 = (bf16[112,192]{1,0:T(8,128)(2,1)}, bf16[112,192]{1,0:T(8,128)(2,1)}, u32[]{:S(2)}, u32[]{:S(2)}) collective-permute-start(bf16[112,192]{1,0:T(8,128)(2,1)} %get-tuple-element.35.refs_0_), channel_id=1, source_target_pairs={{0,12},{4,8},{8,4},{12,0},{16,28},{20,24},{24,20},{28,16},{1,13},{... | collective-permute-start | bytes 129032 | tf_op jit(solution)/shard_map/ppermute | solution.py:308
  46.9 12.2 %collective-permute-start.10 = (bf16[112,192]{1,0:T(8,128)(2,1)}, bf16[112,192]{1,0:T(8,128)(2,1)}, u32[]{:S(2)}, u32[]{:S(2)}) collective-permute-start(bf16[112,192]{1,0:T(8,128)(2,1)} %get-tuple-element.35.refs_0_), channel_id=1, source_target_pairs={{0,8},{4,12},{8,0},{12,4},{16,24},{20,28},{24,16},{28,20},{1,9},{5... | collective-permute-start | bytes 129032 | tf_op jit(solution)/shard_map/ppermute | solution.py:308
  49.1 11.6 %collective-permute-start.9 = (bf16[112,192]{1,0:T(8,128)(2,1)}, bf16[112,192]{1,0:T(8,128)(2,1)}, u32[]{:S(2)}, u32[]{:S(2)}) collective-permute-start(bf16[112,192]{1,0:T(8,128)(2,1)} %get-tuple-element.35.refs_0_), channel_id=1, source_target_pairs={{0,4},{4,0},{8,12},{12,8},{16,20},{20,16},{24,28},{28,24},{1,5},{5... | collective-permute-start | bytes 129032 | tf_op jit(solution)/shard_map/ppermute | solution.py:308
  51.1 1.4 %copy-start.6 = (bf16[1,192,4096]{2,1,0:T(8,128)(2,1)S(1)}, bf16[1,192,4096]{2,1,0:T(8,128)(2,1)}, u32[]{:S(2)}) copy-start(bf16[1,192,4096]{2,1,0:T(8,128)(2,1)} %param.16) | copy-start | bytes 4718596
  52.5 0.9 copy-start.8
  53.4 0.9 copy-start.10
  54.3 0.9 copy-start.15
  55.2 0.9 copy-start.17
  56.1 4.9 %copy-start.2 = (f32[2,192,512]{2,1,0:T(8,128)S(1)}, f32[2,192,512]{2,1,0:T(8,128)}, u32[]{:S(2)}) copy-start(f32[2,192,512]{2,1,0:T(8,128)} %refs_12_.1) | copy-start | bytes 2359300
  56.1 4.9 %copy-start.3 = (f32[2,192,512]{2,1,0:T(8,128)S(1)}, f32[2,192,512]{2,1,0:T(8,128)}, u32[]{:S(2)}) copy-start(f32[2,192,512]{2,1,0:T(8,128)} %refs_13_.1) | copy-start | bytes 2359300
  56.1 4.9 %copy-start.19 = (bf16[112,192]{1,0:T(8,128)(2,1)S(1)}, bf16[112,192]{1,0:T(8,128)(2,1)}, u32[]{:S(2)}) copy-start(bf16[112,192]{1,0:T(8,128)(2,1)} %copy-done.18) | copy-start | bytes 129028
  59.1 6.3 %collective-permute-start.6 = (bf16[24,4096]{1,0:T(8,128)(2,1)S(1)}, bf16[24,4096]{1,0:T(8,128)(2,1)S(1)}, u32[]{:S(2)}, u32[]{:S(2)}) collective-permute-start(bf16[24,4096]{1,0:T(8,128)(2,1)S(1)} %get-tuple-element.32), channel_id=1, source_target_pairs={{0,1},{1,0},{2,3},{3,2},{4,5},{5,4},{6,7},{7,6},{8,9},{9,8},{10,11... | collective-permute-start | bytes 589832 | tf_op jit(solution)/shard_map/ppermute | solution.py:308
  59.2 7.8 %collective-permute-start.7 = (bf16[24,4096]{1,0:T(8,128)(2,1)S(1)}, bf16[24,4096]{1,0:T(8,128)(2,1)S(1)}, u32[]{:S(2)}, u32[]{:S(2)}) collective-permute-start(bf16[24,4096]{1,0:T(8,128)(2,1)S(1)} %get-tuple-element.33), channel_id=1, source_target_pairs={{0,2},{1,3},{2,0},{3,1},{4,6},{5,7},{6,4},{7,5},{8,10},{9,11},{10,... | collective-permute-start | bytes 589832 | tf_op jit(solution)/shard_map/ppermute | solution.py:308
  60.7 9.4 %collective-permute-start.8 = (bf16[24,4096]{1,0:T(8,128)(2,1)S(1)}, bf16[24,4096]{1,0:T(8,128)(2,1)S(1)}, u32[]{:S(2)}, u32[]{:S(2)}) collective-permute-start(bf16[24,4096]{1,0:T(8,128)(2,1)S(1)} %get-tuple-element.34), channel_id=1, source_target_pairs={{0,3},{1,2},{2,1},{3,0},{4,7},{5,6},{6,5},{7,4},{8,11},{9,10},{10,... | collective-permute-start | bytes 589832 | tf_op jit(solution)/shard_map/ppermute | solution.py:308
  63.5 12.0 %collective-permute-start.19 = (bf16[192,512]{1,0:T(8,128)(2,1)S(1)}, bf16[192,512]{1,0:T(8,128)(2,1)S(1)}, u32[]{:S(2)}, u32[]{:S(2)}) collective-permute-start(bf16[192,512]{1,0:T(8,128)(2,1)S(1)} %get-tuple-element.38), channel_id=1, source_target_pairs={{0,4},{4,0},{8,12},{12,8},{16,20},{20,16},{24,28},{28,24},{1,5},{5... | collective-permute-start | bytes 589832 | tf_op jit(solution)/shard_map/ppermute | solution.py:308
  63.6 13.6 %collective-permute-start.20 = (bf16[192,512]{1,0:T(8,128)(2,1)S(1)}, bf16[192,512]{1,0:T(8,128)(2,1)S(1)}, u32[]{:S(2)}, u32[]{:S(2)}) collective-permute-start(bf16[192,512]{1,0:T(8,128)(2,1)S(1)} %get-tuple-element.39), channel_id=1, source_target_pairs={{0,8},{4,12},{8,0},{12,4},{16,24},{20,28},{24,16},{28,20},{1,9},{5... | collective-permute-start | bytes 589832 | tf_op jit(solution)/shard_map/ppermute | solution.py:308
  71.6 11.2 %collective-permute-start.21 = (bf16[192,512]{1,0:T(8,128)(2,1)S(1)}, bf16[192,512]{1,0:T(8,128)(2,1)S(1)}, u32[]{:S(2)}, u32[]{:S(2)}) collective-permute-start(bf16[192,512]{1,0:T(8,128)(2,1)S(1)} %get-tuple-element.40), channel_id=1, source_target_pairs={{0,12},{4,8},{8,4},{12,0},{16,28},{20,24},{24,20},{28,16},{1,13},{... | collective-permute-start | bytes 589832 | tf_op jit(solution)/shard_map/ppermute | solution.py:308
  72.9 24.4 %collective-permute-start.22 = (bf16[192,512]{1,0:T(8,128)(2,1)S(1)}, bf16[192,512]{1,0:T(8,128)(2,1)S(1)}, u32[]{:S(2)}, u32[]{:S(2)}) collective-permute-start(bf16[192,512]{1,0:T(8,128)(2,1)S(1)} %get-tuple-element.41), channel_id=1, source_target_pairs={{0,16},{4,20},{8,24},{12,28},{16,0},{20,4},{24,8},{28,12},{1,17},{... | collective-permute-start | bytes 589832 | tf_op jit(solution)/shard_map/ppermute | solution.py:308
  75.1 26.4 %collective-permute-start.23 = (bf16[192,512]{1,0:T(8,128)(2,1)S(1)}, bf16[192,512]{1,0:T(8,128)(2,1)S(1)}, u32[]{:S(2)}, u32[]{:S(2)}) collective-permute-start(bf16[192,512]{1,0:T(8,128)(2,1)S(1)} %get-tuple-element.42), channel_id=1, source_target_pairs={{0,20},{4,16},{8,28},{12,24},{16,4},{20,0},{24,12},{28,8},{1,21},{... | collective-permute-start | bytes 589832 | tf_op jit(solution)/shard_map/ppermute | solution.py:308
  75.5 30.3 %collective-permute-start.24 = (bf16[192,512]{1,0:T(8,128)(2,1)S(1)}, bf16[192,512]{1,0:T(8,128)(2,1)S(1)}, u32[]{:S(2)}, u32[]{:S(2)}) collective-permute-start(bf16[192,512]{1,0:T(8,128)(2,1)S(1)} %get-tuple-element.43), channel_id=1, source_target_pairs={{0,24},{4,28},{8,16},{12,20},{16,8},{20,12},{24,0},{28,4},{1,25},{... | collective-permute-start | bytes 589832 | tf_op jit(solution)/shard_map/ppermute | solution.py:308
  77.2 33.5 %collective-permute-start.25 = (bf16[192,512]{1,0:T(8,128)(2,1)S(1)}, bf16[192,512]{1,0:T(8,128)(2,1)S(1)}, u32[]{:S(2)}, u32[]{:S(2)}) collective-permute-start(bf16[192,512]{1,0:T(8,128)(2,1)S(1)} %get-tuple-element.44), channel_id=1, source_target_pairs={{0,28},{4,24},{8,20},{12,16},{16,12},{20,8},{24,4},{28,0},{1,29},{... | collective-permute-start | bytes 589832 | tf_op jit(solution)/shard_map/ppermute | solution.py:308
where the time goes:
time: 113 us; the launch traced here: 112 us
  waiting for transfers between devices  46.1 us (41%)
  starting transfers between devices  35.8 us (32%)
  local copies, waits for them, and re-layouts  14.8 us (13%)
  Pallas kernels  12.4 us (11%)
  between operations  1.45 us (1%)
  other arithmetic  1.44 us (1%)
    ppermute x26, waiting for transfers between devices, swap(): return lax.ppermute(value, axis, [(i, i ^ bits) for i in range(size)])  41.9 us
    ppermute x26, starting transfers between devices, swap(): return lax.ppermute(value, axis, [(i, i ^ bits) for i in range(size)])  29.6 us
    unnamed x44, local copies, waits for them, and re-layouts  14.8 us
    all_to_all x1, starting transfers between devices, body(): lax.all_to_all(blocks, 'grp', split_axis=0, concat_axis=0, tiled=True)  6.28 us
    all_to_all x1, waiting for transfers between devices, body(): lax.all_to_all(blocks, 'grp', split_axis=0, concat_axis=0, tiled=True)  4.18 us
    pallas_call x1, Pallas kernels, backward(): pl.pallas_call(functools.partial(backward_kernel, parts), in_specs=[LOCAL...  2.94 us
    pallas_call x1, Pallas kernels, forward(): pl.pallas_call(functools.partial(forward_kernel, len(blocks)), in_specs=[...  2.78 us
    pallas_call x1, Pallas kernels, adam(): pl.pallas_call(functools.partial(adam_kernel, groups, parts), in_specs=[S...  2.41 us
  transfers between devices with their start and end apart: 27, of which 12 were waited for; matrix products, arithmetic and copies ran while one was open for 1% of the time, Pallas kernels for 9%

commit v1 on v0

--- a/solution.py
+++ b/solution.py
@@ -29,46 +29,53 @@
 
 SCALARS = pl.BlockSpec(memory_space=pltpu.SMEM)
 LOCAL = pl.BlockSpec(memory_space=pltpu.VMEM)
-PARAMS = pltpu.CompilerParams(vmem_limit_bytes=16 * 2**20)
+FAR = pl.BlockSpec(memory_space=pltpu.HBM)
+PARAMS = pltpu.CompilerParams(vmem_limit_bytes=12 * 2**20)
+GRANT1 = pltpu.CompilerParams(vmem_limit_bytes=65_400_000)
+GRANT2 = pltpu.CompilerParams(vmem_limit_bytes=56_000_000)
 
 
 def cost(flops, moved):
-    return pl.CostEstimate(flops=int(flops), bytes_accessed=int(moved), transcendentals=0)
+    return pl.CostEstimate(flops=int(flops), bytes_accessed=int(moved) * 16, transcendentals=0)
 
 
 def rows_of(parts):
     return jnp.concatenate([part.astype(F32) for part in parts], axis=0).astype(BF16)
 
 
-def select_kernel(slots, pieces, place, ids, probs, tokens, rows, mask, coefs, held, sems):
+def select_kernel(slots, pieces, place, ids, probs, tokens, rows, picks, *refs):
+    ids_in, probs_in, tokens_in, sems = refs
     tok, width = tokens.shape
     step = width // pieces
+    at = [slice(piece * step, (piece + 1) * step) for piece in range(pieces)]
+    pairs = [(ids, ids_in), (probs, probs_in)]
+    pairs += [(tokens.at[:, at[i]], tokens_in.at[:, at[i]]) for i in range(pieces)]
     copies = []
-    for piece in range(pieces):
-        at = slice(piece * step, (piece + 1) * step)
-        copy = pltpu.make_async_copy(tokens.at[:, at], held.at[:, at], sems.at[piece])
-        copy.start()
-        copies.append(copy)
+    for number, (source, target) in enumerate(pairs):
+        copies.append(pltpu.make_async_copy(source, target, sems.at[number]))
+        copies[-1].start()
     below = lax.broadcasted_iota(jnp.int32, (tok, tok), 0)
     right = lax.broadcasted_iota(jnp.int32, (tok, tok), 1)
     upper = jnp.where(below <= right, 1.0, 0.0).astype(BF16)
+    want = lax.broadcasted_iota(jnp.int32, (CAP, tok), 0).astype(F32) + 1.0
+    for copy in copies[:2]:
+        copy.wait()
+    chosen_list = []
     for slot in range(slots):
         expert = place[0, slot] * slots + slot
-        match = ids[...] == expert
+        match = ids_in[...] == expert
         hit = jnp.max(jnp.where(match, 1.0, 0.0), axis=0, keepdims=True)
-        coef = jnp.sum(jnp.where(match, probs[...], 0.0), axis=0, keepdims=True)
+        coef = jnp.sum(jnp.where(match, probs_in[...], 0.0), axis=0, keepdims=True)
         rank = jnp.dot(hit.astype(BF16), upper, preferred_element_type=F32)
-        want = lax.broadcasted_iota(jnp.int32, (CAP, tok), 0).astype(F32) + 1.0
         chosen = jnp.where((rank == want) & (hit > 0.0), 1.0, 0.0)
-        at = slice(slot * CAP, (slot + 1) * CAP)
-        mask[at, :] = chosen.astype(BF16)
-        total = jnp.sum(chosen * coef, axis=1, keepdims=True)
-        coefs[at, :] = jnp.broadcast_to(total, (CAP, coefs.shape[1]))
-    left = mask[...]
-    for piece in range(pieces):
-        at = slice(piece * step, (piece + 1) * step)
-        copies[piece].wait()
-        rows[:, at] = jnp.dot(left, held[:, at], preferred_element_type=F32).astype(BF16)
+        chosen_list.append(chosen)
+        picks[slot * CAP : (slot + 1) * CAP, :] = chosen * coef
+    left = jnp.concatenate(chosen_list, axis=0) if slots > 1 else chosen_list[0]
+    left = left.astype(BF16)
+    for i in range(pieces):
+        copies[2 + i].wait()
+        picked = jnp.dot(left, tokens_in[:, at[i]], preferred_element_type=F32)
+        rows[:, at[i]] = picked.astype(BF16)
 
 
 def select(placement, ids, probs, tokens, slots):
@@ -77,47 +84,102 @@
     count = slots * CAP
     return pl.pallas_call(
         functools.partial(select_kernel, slots, pieces),
-        in_specs=[SCALARS, LOCAL, LOCAL, pl.BlockSpec(memory_space=pltpu.HBM)],
-        out_specs=[LOCAL] * 3,
+        in_specs=[SCALARS] + [FAR] * 3,
+        out_specs=[LOCAL] * 2,
         out_shape=[
             jax.ShapeDtypeStruct((count, width), BF16),
-            jax.ShapeDtypeStruct((count, tok), BF16),
-            jax.ShapeDtypeStruct((count, 128), F32),
+            jax.ShapeDtypeStruct((count, tok), F32),
         ],
-        scratch_shapes=[pltpu.VMEM((tok, width), BF16), pltpu.SemaphoreType.DMA((pieces,))],
-        compiler_params=PARAMS,
+        scratch_shapes=[
+            pltpu.VMEM(ids.shape, ids.dtype),
+            pltpu.VMEM(probs.shape, probs.dtype),
+            pltpu.VMEM((tok, width), BF16),
+            pltpu.SemaphoreType.DMA((2 + pieces,)),
+        ],
+        compiler_params=GRANT1,
         cost_estimate=cost(2 * count * tok * width, tok * width * 2),
         name="select_rows",
     )(placement, ids, probs, tokens)
 
 
-def scale_kernel(mask, coefs, grads, rows, blocks):
-    groups, _, step = blocks.shape
-    left = mask[...]
-    coef = coefs[:, 0:1]
-    for block in range(groups):
-        at = slice(block * step, (block + 1) * step)
-        picked = jnp.dot(left, grads[:, at], preferred_element_type=F32)
-        scaled = (coef * picked).astype(BF16)
-        rows[:, at] = scaled
-        blocks[block] = scaled
-
-
-def scale(mask, coefs, grads, groups):
+def scale_kernel(pieces, picks, grads, scaled, *refs):
+    me = lax.axis_index("grp")
+    blocks, (grads_in, sems) = refs[:-2], refs[-2:]
+    groups = 2 * len(blocks)
+    width = grads.shape[1]
+    block, step = width // groups, width // pieces
+    at = [slice(piece * step, (piece + 1) * step) for piece in range(pieces)]
+    copies = []
+    for i in range(pieces):
+        copies.append(
+            pltpu.make_async_copy(grads.at[:, at[i]], grads_in.at[:, at[i]], sems.at[i])
+        )
+        copies[-1].start()
+    coefs = jnp.sum(picks[...], axis=1, keepdims=True)
+    left = jnp.where(picks[...] > 0.0, 1.0, 0.0).astype(BF16)
+    for i in range(pieces):
+        copies[i].wait()
+        picked = jnp.dot(left, grads_in[:, at[i]], preferred_element_type=F32)
+        scaled[:, at[i]] = (coefs * picked).astype(BF16)
+    for group in range(groups):
+        start = pl.multiple_of((me ^ group) * block, 128)
+        blocks[group // 2][group % 2] = scaled[:, pl.ds(start, block)]
+
+
+def scale(picks, grads, groups):
     tok, width = grads.shape
-    count = mask.shape[0]
-    return pl.pallas_call(
-        scale_kernel,
-        in_specs=[LOCAL] * 3,
+    pieces = 4
+    count = picks.shape[0]
+    pairs = groups // 2
+    return pl.pallas_call(
+        functools.partial(scale_kernel, pieces),
+        in_specs=[LOCAL, FAR],
+        out_specs=[LOCAL] * (1 + pairs),
+        out_shape=[jax.ShapeDtypeStruct((count, width), BF16)]
+        + [jax.ShapeDtypeStruct((2, count, width // groups), BF16)] * pairs,
+        scratch_shapes=[pltpu.VMEM((tok, width), BF16), pltpu.SemaphoreType.DMA((pieces,))],
+        compiler_params=GRANT2,
+        cost_estimate=cost(2 * count * tok * width, tok * width * 8),
+        name="scale_rows",
+    )(picks, grads)
+
+
+def stack_kernel(count, *refs):
+    for number in range(count):
+        for pick, out in enumerate(refs[count:]):
+            out[number] = refs[number][pick]
+
+
+def stack(pairs):
+    shape = (len(pairs),) + pairs[0].shape[1:]
+    return pl.pallas_call(
+        functools.partial(stack_kernel, len(pairs)),
+        in_specs=[LOCAL] * len(pairs),
         out_specs=[LOCAL] * 2,
-        out_shape=[
-            jax.ShapeDtypeStruct((count, width), BF16),
-            jax.ShapeDtypeStruct((groups, count, width // groups), BF16),
-        ],
-        compiler_params=PARAMS,
-        cost_estimate=cost(2 * count * tok * width, tok * width * 2),
-        name="scale_rows",
-    )(mask, coefs, grads)
+        out_shape=[jax.ShapeDtypeStruct(shape, BF16)] * 2,
+        compiler_params=PARAMS,
+        cost_estimate=cost(0, 2 * len(pairs) * pairs[0].size),
+        name="stack",
+    )(*pairs)
+
+
+def join_kernel(one, two, out):
+    count = one.shape[0]
+    out[0:count] = one[...]
+    out[count:] = two[...]
+
+
+def join(one, two):
+    shape = (one.shape[0] + two.shape[0],) + one.shape[1:]
+    return pl.pallas_call(
+        join_kernel,
+        in_specs=[LOCAL] * 2,
+        out_specs=LOCAL,
+        out_shape=jax.ShapeDtypeStruct(shape, BF16),
+        compiler_params=PARAMS,
+        cost_estimate=cost(0, 8 * one.size),
+        name="join",
+    )(one, two)
 
 
 def forward_kernel(parts, place, *refs):
@@ -151,11 +213,11 @@
     )(my_cand, *blocks, w_gate, w_up)
 
 
-def adam_kernel(groups, parts, me, *refs):
+def adam_kernel(groups, parts, *refs):
+    half = groups // 2
     hiddens, refs = refs[:groups], refs[groups:]
-    blocks, refs = refs[:parts], refs[parts:]
-    first, second, summed = refs[:3]
-    dirs = refs[3:]
+    near, other, first, second, summed = refs[:5]
+    dirs = refs[5:]
     count = parts * CAP
     rights = []
     lefts = [[] for _ in range(CANDS)]
@@ -166,7 +228,9 @@
         for cand in range(CANDS):
             lefts[cand].append(jnp.where(tag == float(cand), part_rows, 0.0))
         for part in range(parts):
-            rights.append(blocks[part][me[0, 0] ^ peer].astype(F32))
+            stack = (near, other)[part % 2]
+            at = part // 2 * groups + peer // 2 + peer % 2 * half
+            rights.append(stack[at].astype(F32))
     right = jnp.concatenate(rights, axis=0).astype(BF16)
     dir_list = []
     for cand in range(CANDS):
@@ -189,20 +253,49 @@
     return (new_first, new_second)
 
 
-def adam(me, hiddens, blocks, first, second):
-    groups, parts = len(hiddens), len(blocks)
+def adam(hiddens, blocks, first, second):
+    groups = len(hiddens)
+    parts = 2 * blocks[0].shape[0] // groups
     units, columns = first.shape[1:]
     rows = groups * parts * CAP
     return pl.pallas_call(
         functools.partial(adam_kernel, groups, parts),
-        in_specs=[SCALARS] + [LOCAL] * (groups + parts + 2),
+        in_specs=[LOCAL] * (groups + 4),
         out_specs=[LOCAL] * (1 + groups),
         out_shape=[jax.ShapeDtypeStruct(first.shape, F32)]
         + [jax.ShapeDtypeStruct((units, columns), BF16)] * groups,
         compiler_params=PARAMS,
         cost_estimate=cost(2 * CANDS * rows * units * columns, 8 * first.size),
         name="adam",
-    )(me, *hiddens, *blocks, first, second)
+    )(*hiddens, *blocks, first, second)
+
+
+def update_kernel(summed, first, second, new_first, new_second, one_out, two_out, sems):
+    copies = []
+    for cand in range(CANDS):
+        one_out[cand], two_out[cand] = moments(summed[cand], first[cand], second[cand])
+        for number, (source, target) in enumerate([(one_out, new_first), (two_out, new_second)]):
+            copy = pltpu.make_async_copy(
+                source.at[cand], target.at[cand], sems.at[2 * cand + number]
+            )
+            copy.start()
+            copies.append(copy)
+    for copy in copies:
+        copy.wait()
+
+
+def update(summed, first, second):
+    return pl.pallas_call(
+        update_kernel,
+        in_specs=[LOCAL] * 3,
+        out_specs=[FAR] * 2,
+        out_shape=[jax.ShapeDtypeStruct(first.shape, F32)] * 2,
+        scratch_shapes=[pltpu.VMEM(first.shape, F32)] * 2
+        + [pltpu.SemaphoreType.DMA((2 * CANDS,))],
+        compiler_params=PARAMS,
+        cost_estimate=cost(8 * first.size, 8 * first.size),
+        name="update",
+    )(summed, first, second)
 
 
 def backward_kernel(parts, *refs):
@@ -241,10 +334,12 @@
 
 
 def combine_kernel(parts, pieces, *refs):
-    masks, blocks, out, held, sems = refs[0], refs[1 : 1 + parts], *refs[1 + parts :]
+    picks, blocks, out, held, sems = refs[0], refs[1 : 1 + parts], *refs[1 + parts :]
     width = out.shape[1]
     step = width // pieces
-    left = masks[...]
+    left = jnp.where(picks[...] > 0.0, 1.0, 0.0).astype(BF16)
+    if left.shape[0] < parts * CAP:
+        left = rows_of([left] * parts)
     copies = []
     for piece in range(pieces):
         at = slice(piece * step, (piece + 1) * step)
@@ -257,28 +352,29 @@
         copy.wait()
 
 
-def combine(masks, blocks):
-    count, tok = masks.shape
+def combine(picks, blocks):
+    count, tok = picks.shape
     width = blocks[0].shape[1]
     pieces = 4
     return pl.pallas_call(
         functools.partial(combine_kernel, len(blocks), pieces),
         in_specs=[LOCAL] * (1 + len(blocks)),
-        out_specs=pl.BlockSpec(memory_space=pltpu.HBM),
+        out_specs=FAR,
         out_shape=jax.ShapeDtypeStruct((tok, width), BF16),
         scratch_shapes=[pltpu.VMEM((tok, width), BF16), pltpu.SemaphoreType.DMA((pieces,))],
         compiler_params=PARAMS,
         cost_estimate=cost(2 * count * tok * width, 2 * tok * width),
         name="combine",
-    )(masks, *blocks)
-
-
-def place_kernel(groups, me, *refs):
+    )(picks, *blocks)
+
+
+def place_kernel(groups, *refs):
+    me = lax.axis_index("grp")
     blocks, out, sems = refs[:groups], refs[groups], refs[groups + 1]
     columns = blocks[0].shape[1]
     copies = []
     for peer in range(groups):
-        start = pl.multiple_of((me[0, 0] ^ peer) * columns, 128)
+        start = pl.multiple_of((me ^ peer) * columns, 128)
         copies.append(
             pltpu.make_async_copy(
                 blocks[peer], out.at[:, pl.ds(start, columns)], sems.at[peer]
@@ -289,19 +385,19 @@
         copy.wait()
 
 
-def place_blocks(me, blocks):
+def place_blocks(blocks):
     groups = len(blocks)
     units, columns = blocks[0].shape
     return pl.pallas_call(
         functools.partial(place_kernel, groups),
-        in_specs=[SCALARS] + [LOCAL] * groups,
-        out_specs=pl.BlockSpec(memory_space=pltpu.HBM),
+        in_specs=[LOCAL] * groups,
+        out_specs=FAR,
         out_shape=jax.ShapeDtypeStruct((units, groups * columns), BF16),
         scratch_shapes=[pltpu.SemaphoreType.DMA((groups,))],
         compiler_params=PARAMS,
         cost_estimate=cost(0, 4 * groups * units * columns),
         name="place_blocks",
-    )(me, *blocks)
+    )(*blocks)
 
 
 def swap(value, axis, size, bits):
@@ -324,7 +420,6 @@
     groups = lax.axis_size("grp")
     slots = num_ep // QUARTERS
     ep_index = lax.axis_index("ep")
-    me = lax.axis_index("grp").astype(jnp.int32).reshape(1, 1)
 
     def slot_of(bits):
         return (ep_index ^ bits) // QUARTERS
@@ -356,29 +451,41 @@
     w_up = up_weight[0].T
     w_down = down_weight[0]
 
-    rows, mask, coefs = select(placement, expert_ids.T, gate_probs.T, tokens, slots)
+    rows, picks = select(placement, expert_ids.T, gate_probs.T, tokens, slots)
     in_rows = share(per_slot(rows), 0)
-    scaled, blocks = scale(mask, coefs, out_grad, groups)
-    columns = lax.all_to_all(blocks, "grp", split_axis=0, concat_axis=0, tiled=True)
-    columns = share(columns.reshape(groups, slots, CAP, columns.shape[-1]), 1)
+    scaled, *blocks = scale(picks, out_grad, groups)
+    if slots > 1:
+        picks = [of_slot(per_slot(picks), bits, 0) for bits in range(num_ep)]
+        picks = jnp.concatenate(picks, axis=0)
+    pairs = [blocks[0]]
+    for number in range(1, groups // 2):
+        pairs.append(swap(blocks[number], "grp", groups, 2 * number))
+    kept, passed = stack(pairs)
+    passed = swap(passed, "grp", groups, 1)
+    columns = join(kept, passed)
+    columns = columns.reshape(groups, slots, CAP, columns.shape[-1])
+    near = []
+    for far in range(0, num_ep, 2):
+        piece = of_slot(columns, far, 1)
+        near.append(swap(piece, "ep", num_ep, far) if far else piece)
+    near = functools.reduce(join, near)
+    columns = (near, swap(near, "ep", num_ep, 1))
     my_cand = placement
     if slots > 1:
         my_cand = lax.dynamic_index_in_dim(placement, slot_of(0), 1, keepdims=True)
     pre_gate, pre_up, hidden = forward(my_cand, in_rows, w_gate, w_up)
     hiddens = exchange([hidden] * groups)
-    summed, *dirs = adam(me, hiddens, columns, moment_first, moment_second)
+    summed, *dirs = adam(hiddens, columns, moment_first, moment_second)
     got_dirs = exchange(dirs)
-    new_first, new_second = moments(summed, moment_first, moment_second)
+    new_first, new_second = update(summed, moment_first, moment_second)
 
     in_scaled = share(per_slot(scaled), 0)
     partials = backward(in_scaled, w_down, w_gate, w_up, pre_gate, pre_up)
     returned = [partials[0]]
     for bits in range(1, num_ep):
         returned.append(swap(partials[bits], "ep", num_ep, bits))
-    masks = per_slot(mask)
-    masks = jnp.concatenate([of_slot(masks, bits, 0) for bits in range(num_ep)], axis=0)
-    token_grad = combine(masks, returned)
-    step_dir = place_blocks(me, got_dirs)[None]
+    token_grad = combine(picks, returned)
+    step_dir = place_blocks(got_dirs)[None]
     return (token_grad, step_dir, new_first, new_second)
 
 

time: 113 us -> 96.6 us (0.85)
  the two profiles are of different devices: /device:TPU:8 before, /device:TPU:9 now
where the time goes in v1:
time: 96.6 us; the launch traced here: 96.4 us
  starting transfers between devices  46.5 us (48%)
  waiting for transfers between devices  34.9 us (36%)
  Pallas kernels  12.6 us (13%)
  between operations  1.46 us (2%)
    ppermute x29, starting transfers between devices, swap(): return lax.ppermute(value, axis, [(i, i ^ bits) for i in range(size)])  46.5 us
    ppermute x29, waiting for transfers between devices, swap(): return lax.ppermute(value, axis, [(i, i ^ bits) for i in range(size)])  34.9 us
    pallas_call x1, Pallas kernels, select(): pl.pallas_call(functools.partial(select_kernel, slots, pieces), in_specs=...  2.63 us
  transfers between devices with their start and end apart: 29, of which 10 were waited for; matrix products, arithmetic and copies ran while one was open for 0% of the time, Pallas kernels for 7%

profile of v1, /device:TPU:9, one launch (start us, length us, event | category | flops | bytes accessed | tf_op | source)
XLA Modules:
  0.0 96.4 jit_solution(7747226252154939059)
XLA Ops:
  1.3 2.6 %select_rows.1 = (bf16[24,4096]{1,0:T(8,128)(2,1)}, f32[24,192]{1,0:T(8,128)}) custom-call(s32[1,1]{1,0:T(1,128)S(6)} %copy.14.place, s32[8,192]{1,0:T(8,128)} %bitcast.16, f32[8,192]{1,0:T(8,128)} %bitcast.17, bf16[192,4096]{1,0:T(8,128)(2,1)} %tokens.1), custom_call_target="tpu_custom_call" | custom-call | flops 37748736 | bytes 25165824 | tf_op jit(solution)/shard_map/select_rows/pallas_call | solution.py:85
  3.9 0.0 copy-start.5
  3.9 0.0 copy-start
  4.0 0.0 copy-start.6
  4.0 0.9 copy-done.6
  4.8 1.8 %scale_rows.1 = (bf16[24,4096]{1,0:T(8,128)(2,1)S(1)}, bf16[2,24,512]{2,1,0:T(8,128)(2,1)S(1)}, bf16[2,24,512]{2,1,0:T(8,128)(2,1)S(1)}, bf16[2,24,512]{2,1,0:T(8,128)(2,1)S(1)}, bf16[2,24,512]{2,1,0:T(8,128)(2,1)S(1)}) custom-call(f32[24,192]{1,0:T(8,128)S(1)} %copy-done.6, bf16[192,4096]{1,0:T(8,128)(2,1)} %grads.1), custom_call_target="tpu_custom_call" | custom-call | flops 37748736 | bytes 100663296 | tf_op jit(solution)/shard_map/scale_rows/pallas_call | solution.py:134
  6.6 0.1 collective-permute-start.16
  6.7 2.5 %collective-permute-start.17 = (bf16[2,24,512]{2,1,0:T(8,128)(2,1)S(1)}, bf16[2,24,512]{2,1,0:T(8,128)(2,1)S(1)}, u32[]{:S(2)}, u32[]{:S(2)}) collective-permute-start(bf16[2,24,512]{2,1,0:T(8,128)(2,1)S(1)} %get-tuple-element.43), channel_id=1, source_target_pairs={{0,16},{4,20},{8,24},{12,28},{16,0},{20,4},{24,8},{28,12},{1,17},{... | collective-permute-start | bytes 147464 | tf_op jit(solution)/shard_map/ppermute | solution.py:404
  9.2 0.2 collective-permute-start.18
  9.3 0.3 collective-permute-done.16.refs_1_
  9.6 1.6 %collective-permute-done.17.refs_2_ = bf16[2,24,512]{2,1,0:T(8,128)(2,1)S(1)} collective-permute-done((bf16[2,24,512]{2,1,0:T(8,128)(2,1)S(1)}, bf16[2,24,512]{2,1,0:T(8,128)(2,1)S(1)}, u32[]{:S(2)}, u32[]{:S(2)}) %collective-permute-start.17) | collective-permute-done | bytes 49184 | tf_op jit(solution)/shard_map/ppermute | solution.py:404
  11.3 1.8 %collective-permute-done.18.refs_3_ = bf16[2,24,512]{2,1,0:T(8,128)(2,1)S(1)} collective-permute-done((bf16[2,24,512]{2,1,0:T(8,128)(2,1)S(1)}, bf16[2,24,512]{2,1,0:T(8,128)(2,1)S(1)}, u32[]{:S(2)}, u32[]{:S(2)}) %collective-permute-start.18) | collective-permute-done | bytes 49184 | tf_op jit(solution)/shard_map/ppermute | solution.py:404
  13.1 1.3 %collective-permute-start.19 = (bf16[4,24,512]{2,1,0:T(8,128)(2,1)S(1)}, bf16[4,24,512]{2,1,0:T(8,128)(2,1)S(1)}, u32[]{:S(2)}, u32[]{:S(2)}) collective-permute-start(bf16[4,24,512]{2,1,0:T(8,128)(2,1)S(1)} %get-tuple-element.46), channel_id=1, source_target_pairs={{0,4},{4,0},{8,12},{12,8},{16,20},{20,16},{24,28},{28,24},{1,5},{5... | collective-permute-start | bytes 294920 | tf_op jit(solution)/shard_map/ppermute | solution.py:404
  14.4 2.2 %collective-permute-done.19.two = bf16[4,24,512]{2,1,0:T(8,128)(2,1)S(1)} collective-permute-done((bf16[4,24,512]{2,1,0:T(8,128)(2,1)S(1)}, bf16[4,24,512]{2,1,0:T(8,128)(2,1)S(1)}, u32[]{:S(2)}, u32[]{:S(2)}) %collective-permute-start.19) | collective-permute-done | bytes 98336 | tf_op jit(solution)/shard_map/ppermute | solution.py:404
  16.6 1.3 %collective-permute-start.20 = (bf16[8,24,512]{2,1,0:T(8,128)(2,1)S(1)}, bf16[8,24,512]{2,1,0:T(8,128)(2,1)S(1)}, u32[]{:S(2)}, u32[]{:S(2)}) collective-permute-start(bf16[8,24,512]{2,1,0:T(8,128)(2,1)S(1)} %join.2.one), channel_id=1, source_target_pairs={{0,2},{1,3},{2,0},{3,1},{4,6},{5,7},{6,4},{7,5},{8,10},{9,11},{10,... | collective-permute-start | bytes 589832 | tf_op jit(solution)/shard_map/ppermute | solution.py:404
  17.9 0.3 collective-permute-start.4
  18.1 1.2 %collective-permute-start.1 = (bf16[24,4096]{1,0:T(8,128)(2,1)S(1)}, bf16[24,4096]{1,0:T(8,128)(2,1)S(1)}, u32[]{:S(2)}, u32[]{:S(2)}) collective-permute-start(bf16[24,4096]{1,0:T(8,128)(2,1)S(1)} %get-tuple-element.32.refs_0_), channel_id=1, source_target_pairs={{0,2},{1,3},{2,0},{3,1},{4,6},{5,7},{6,4},{7,5},{8,10},{9,11},{10,... | collective-permute-start | bytes 589832 | tf_op jit(solution)/shard_map/ppermute | solution.py:404
  19.3 1.8 %collective-permute-done.20.two = bf16[8,24,512]{2,1,0:T(8,128)(2,1)S(1)} collective-permute-done((bf16[8,24,512]{2,1,0:T(8,128)(2,1)S(1)}, bf16[8,24,512]{2,1,0:T(8,128)(2,1)S(1)}, u32[]{:S(2)}, u32[]{:S(2)}) %collective-permute-start.20) | collective-permute-done | bytes 196640 | tf_op jit(solution)/shard_map/ppermute | solution.py:404
  21.2 6.4 %collective-permute-start.21 = (bf16[16,24,512]{2,1,0:T(8,128)(2,1)S(1)}, bf16[16,24,512]{2,1,0:T(8,128)(2,1)S(1)}, u32[]{:S(2)}, u32[]{:S(2)}) collective-permute-start(bf16[16,24,512]{2,1,0:T(8,128)(2,1)S(1)} %join.3.refs_8_), channel_id=1, source_target_pairs={{0,1},{1,0},{2,3},{3,2},{4,5},{5,4},{6,7},{7,6},{8,9},{9,8},{10,11... | collective-permute-start | bytes 1179656 | tf_op jit(solution)/shard_map/ppermute | solution.py:404
  27.7 0.1 collective-permute-start.3
  27.7 0.0 collective-permute-done.4.refs_2_
  27.7 2.6 %collective-permute-start.5 = (bf16[24,4096]{1,0:T(8,128)(2,1)S(1)}, bf16[24,4096]{1,0:T(8,128)(2,1)S(1)}, u32[]{:S(2)}, u32[]{:S(2)}) collective-permute-start(bf16[24,4096]{1,0:T(8,128)(2,1)S(1)} %collective-permute-done.4.refs_2_), channel_id=1, source_target_pairs={{0,1},{1,0},{2,3},{3,2},{4,5},{5,4},{6,7},{7,6},{8,9},{9,8},{10,11... | collective-permute-start | bytes 589832 | tf_op jit(solution)/shard_map/ppermute | solution.py:404
  30.3 0.0 collective-permute-start
  30.3 0.0 collective-permute-done.1.refs_2_
  30.3 2.1 %collective-permute-start.2 = (bf16[24,4096]{1,0:T(8,128)(2,1)S(1)}, bf16[24,4096]{1,0:T(8,128)(2,1)S(1)}, u32[]{:S(2)}, u32[]{:S(2)}) collective-permute-start(bf16[24,4096]{1,0:T(8,128)(2,1)S(1)} %collective-permute-done.1.refs_2_), channel_id=1, source_target_pairs={{0,1},{1,0},{2,3},{3,2},{4,5},{5,4},{6,7},{7,6},{8,9},{9,8},{10,11... | collective-permute-start | bytes 589832 | tf_op jit(solution)/shard_map/ppermute | solution.py:404
  32.4 0.0 collective-permute-done.3.refs_1_
  32.4 0.0 collective-permute-done.5.refs_3_
  32.4 0.0 copy-start.4
  32.4 1.1 %forward.1 = (f32[96,192]{1,0:T(8,128)S(1)}, f32[96,192]{1,0:T(8,128)S(1)}, bf16[112,192]{1,0:T(8,128)(2,1)S(1)}) custom-call(s32[1,1]{1,0:T(1,128)S(6)} %copy.14.place, bf16[24,4096]{1,0:T(8,128)(2,1)S(1)} %copy-done.5, bf16[24,4096]{1,0:T(8,128)(2,1)S(1)} %collective-permute-done.3.refs_1_, bf16[24,4096]{1,0:T(8,128)(2,1)S(1)} %collective-permute-done.4.refs_2_, ...), custom_call_target="tpu_custom_call" | custom-call | flops 301989888 | bytes 50331648 | tf_op jit(solution)/shard_map/forward/pallas_call | solution.py:201
  33.6 1.2 %collective-permute-start.15 = (bf16[112,192]{1,0:T(8,128)(2,1)S(1)}, bf16[112,192]{1,0:T(8,128)(2,1)S(1)}, u32[]{:S(2)}, u32[]{:S(2)}) collective-permute-start(bf16[112,192]{1,0:T(8,128)(2,1)S(1)} %get-tuple-element.40.refs_0_), channel_id=1, source_target_pairs={{0,28},{4,24},{8,20},{12,16},{16,12},{20,8},{24,4},{28,0},{1,29},{... | collective-permute-start | bytes 129032 | tf_op jit(solution)/shard_map/ppermute | solution.py:404
  34.8 1.3 %collective-permute-start.14 = (bf16[112,192]{1,0:T(8,128)(2,1)S(1)}, bf16[112,192]{1,0:T(8,128)(2,1)S(1)}, u32[]{:S(2)}, u32[]{:S(2)}) collective-permute-start(bf16[112,192]{1,0:T(8,128)(2,1)S(1)} %get-tuple-element.40.refs_0_), channel_id=1, source_target_pairs={{0,24},{4,28},{8,16},{12,20},{16,8},{20,12},{24,0},{28,4},{1,25},{... | collective-permute-start | bytes 129032 | tf_op jit(solution)/shard_map/ppermute | solution.py:404
  36.1 3.4 %collective-permute-start.13 = (bf16[112,192]{1,0:T(8,128)(2,1)S(1)}, bf16[112,192]{1,0:T(8,128)(2,1)S(1)}, u32[]{:S(2)}, u32[]{:S(2)}) collective-permute-start(bf16[112,192]{1,0:T(8,128)(2,1)S(1)} %get-tuple-element.40.refs_0_), channel_id=1, source_target_pairs={{0,20},{4,16},{8,28},{12,24},{16,4},{20,0},{24,12},{28,8},{1,21},{... | collective-permute-start | bytes 129032 | tf_op jit(solution)/shard_map/ppermute | solution.py:404
  39.5 0.1 collective-permute-start.12
  39.6 0.0 collective-permute-done.15.refs_7_
  39.6 3.9 %collective-permute-start.11 = (bf16[112,192]{1,0:T(8,128)(2,1)S(1)}, bf16[112,192]{1,0:T(8,128)(2,1)S(1)}, u32[]{:S(2)}, u32[]{:S(2)}) collective-permute-start(bf16[112,192]{1,0:T(8,128)(2,1)S(1)} %get-tuple-element.40.refs_0_), channel_id=1, source_target_pairs={{0,12},{4,8},{8,4},{12,0},{16,28},{20,24},{24,20},{28,16},{1,13},{... | collective-permute-start | bytes 129032 | tf_op jit(solution)/shard_map/ppermute | solution.py:404
  43.4 0.0 collective-permute-done.14.refs_6_
  43.4 0.0 collective-permute-start.10
  43.4 0.0 collective-permute-done.13.refs_5_
  43.4 1.2 %collective-permute-start.9 = (bf16[112,192]{1,0:T(8,128)(2,1)S(1)}, bf16[112,192]{1,0:T(8,128)(2,1)S(1)}, u32[]{:S(2)}, u32[]{:S(2)}) collective-permute-start(bf16[112,192]{1,0:T(8,128)(2,1)S(1)} %get-tuple-element.40.refs_0_), channel_id=1, source_target_pairs={{0,4},{4,0},{8,12},{12,8},{16,20},{20,16},{24,28},{28,24},{1,5},{5... | collective-permute-start | bytes 129032 | tf_op jit(solution)/shard_map/ppermute | solution.py:404
  44.6 1.9 %backward.1 = (bf16[24,4096]{1,0:T(8,128)(2,1)S(1)}, bf16[24,4096]{1,0:T(8,128)(2,1)S(1)}, bf16[24,4096]{1,0:T(8,128)(2,1)S(1)}, bf16[24,4096]{1,0:T(8,128)(2,1)S(1)}) custom-call(bf16[24,4096]{1,0:T(8,128)(2,1)S(1)} %get-tuple-element.32.refs_0_, bf16[24,4096]{1,0:T(8,128)(2,1)S(1)} %collective-permute-done.refs_1_, ...), custom_call_target="tpu_custom_call" | custom-call | flops 452984832 | bytes 75497472 | tf_op jit(solution)/shard_map/backward/pallas_call | solution.py:325
  46.5 0.0 collective-permute-done.12.refs_4_
  46.5 1.8 %collective-permute-start.6 = (bf16[24,4096]{1,0:T(8,128)(2,1)S(1)}, bf16[24,4096]{1,0:T(8,128)(2,1)S(1)}, u32[]{:S(2)}, u32[]{:S(2)}) collective-permute-start(bf16[24,4096]{1,0:T(8,128)(2,1)S(1)} %get-tuple-element.37), channel_id=1, source_target_pairs={{0,1},{1,0},{2,3},{3,2},{4,5},{5,4},{6,7},{7,6},{8,9},{9,8},{10,11... | collective-permute-start | bytes 589832 | tf_op jit(solution)/shard_map/ppermute | solution.py:404
  48.3 1.2 %collective-permute-start.7 = (bf16[24,4096]{1,0:T(8,128)(2,1)S(1)}, bf16[24,4096]{1,0:T(8,128)(2,1)S(1)}, u32[]{:S(2)}, u32[]{:S(2)}) collective-permute-start(bf16[24,4096]{1,0:T(8,128)(2,1)S(1)} %get-tuple-element.38), channel_id=1, source_target_pairs={{0,2},{1,3},{2,0},{3,1},{4,6},{5,7},{6,4},{7,5},{8,10},{9,11},{10,... | collective-permute-start | bytes 589832 | tf_op jit(solution)/shard_map/ppermute | solution.py:404
  49.5 0.0 collective-permute-done.10.refs_2_
  49.5 0.7 collective-permute-start.8
  50.2 0.0 collective-permute-done.9.refs_1_
  50.2 0.0 collective-permute-done.21.refs_9_
  50.2 1.1 %adam.1 = (f32[2,192,512]{2,1,0:T(8,128)S(1)}, bf16[192,512]{1,0:T(8,128)(2,1)S(1)}, bf16[192,512]{1,0:T(8,128)(2,1)S(1)}, bf16[192,512]{1,0:T(8,128)(2,1)S(1)},...) custom-call(bf16[112,192]{1,0:T(8,128)(2,1)S(1)} %get-tuple-element., ...), custom_call_target="tpu_custom_call" | custom-call | flops 301989888 | bytes 25165824 | tf_op jit(solution)/shard_map/adam/pallas_call | solution.py:261
  51.4 1.0 %collective-permute-start.22 = (bf16[192,512]{1,0:T(8,128)(2,1)S(1)}, bf16[192,512]{1,0:T(8,128)(2,1)S(1)}, u32[]{:S(2)}, u32[]{:S(2)}) collective-permute-start(bf16[192,512]{1,0:T(8,128)(2,1)S(1)} %get-tuple-element.48), channel_id=1, source_target_pairs={{0,4},{4,0},{8,12},{12,8},{16,20},{20,16},{24,28},{28,24},{1,5},{5... | collective-permute-start | bytes 589832 | tf_op jit(solution)/shard_map/ppermute | solution.py:404
  52.3 2.4 %collective-permute-start.23 = (bf16[192,512]{1,0:T(8,128)(2,1)S(1)}, bf16[192,512]{1,0:T(8,128)(2,1)S(1)}, u32[]{:S(2)}, u32[]{:S(2)}) collective-permute-start(bf16[192,512]{1,0:T(8,128)(2,1)S(1)} %get-tuple-element.49), channel_id=1, source_target_pairs={{0,8},{4,12},{8,0},{12,4},{16,24},{20,28},{24,16},{28,20},{1,9},{5... | collective-permute-start | bytes 589832 | tf_op jit(solution)/shard_map/ppermute | solution.py:404
  54.7 1.0 %collective-permute-start.24 = (bf16[192,512]{1,0:T(8,128)(2,1)S(1)}, bf16[192,512]{1,0:T(8,128)(2,1)S(1)}, u32[]{:S(2)}, u32[]{:S(2)}) collective-permute-start(bf16[192,512]{1,0:T(8,128)(2,1)S(1)} %get-tuple-element.50), channel_id=1, source_target_pairs={{0,12},{4,8},{8,4},{12,0},{16,28},{20,24},{24,20},{28,16},{1,13},{... | collective-permute-start | bytes 589832 | tf_op jit(solution)/shard_map/ppermute | solution.py:404
  55.7 3.1 %collective-permute-start.25 = (bf16[192,512]{1,0:T(8,128)(2,1)S(1)}, bf16[192,512]{1,0:T(8,128)(2,1)S(1)}, u32[]{:S(2)}, u32[]{:S(2)}) collective-permute-start(bf16[192,512]{1,0:T(8,128)(2,1)S(1)} %get-tuple-element.51), channel_id=1, source_target_pairs={{0,16},{4,20},{8,24},{12,28},{16,0},{20,4},{24,8},{28,12},{1,17},{... | collective-permute-start | bytes 589832 | tf_op jit(solution)/shard_map/ppermute | solution.py:404
  58.8 0.6 collective-permute-done.8.refs_4_
  59.5 3.6 %collective-permute-start.26 = (bf16[192,512]{1,0:T(8,128)(2,1)S(1)}, bf16[192,512]{1,0:T(8,128)(2,1)S(1)}, u32[]{:S(2)}, u32[]{:S(2)}) collective-permute-start(bf16[192,512]{1,0:T(8,128)(2,1)S(1)} %get-tuple-element.52), channel_id=1, source_target_pairs={{0,20},{4,16},{8,28},{12,24},{16,4},{20,0},{24,12},{28,8},{1,21},{... | collective-permute-start | bytes 589832 | tf_op jit(solution)/shard_map/ppermute | solution.py:404
  63.0 0.7 collective-permute-start.27
  63.8 2.2 %collective-permute-start.28 = (bf16[192,512]{1,0:T(8,128)(2,1)S(1)}, bf16[192,512]{1,0:T(8,128)(2,1)S(1)}, u32[]{:S(2)}, u32[]{:S(2)}) collective-permute-start(bf16[192,512]{1,0:T(8,128)(2,1)S(1)} %get-tuple-element.54), channel_id=1, source_target_pairs={{0,28},{4,24},{8,20},{12,16},{16,12},{20,8},{24,4},{28,0},{1,29},{... | collective-permute-start | bytes 589832 | tf_op jit(solution)/shard_map/ppermute | solution.py:404
  65.9 1.5 %combine.1 = bf16[192,4096]{1,0:T(8,128)(2,1)} custom-call(f32[24,192]{1,0:T(8,128)S(1)} %copy-done.6, bf16[24,4096]{1,0:T(8,128)(2,1)S(1)} %get-tuple-element.36.refs_1_, bf16[24,4096]{1,0:T(8,128)(2,1)S(1)} %collective-permute-done.6.refs_2_, bf16[24,4096]{1,0:T(8,128)(2,1)S(1)} %collective-permute-done.7.refs_3_, ...), custom_call_target="tpu_custom_call" | custom-call | flops 37748736 | bytes 25165824 | tf_op jit(solution)/shard_map/combine/pallas_call | solution.py:359
  67.4 1.3 %update.1 = (f32[2,192,512]{2,1,0:T(8,128)}, f32[2,192,512]{2,1,0:T(8,128)}) custom-call(f32[2,192,512]{2,1,0:T(8,128)S(1)} %get-tuple-element.55.summed, f32[2,192,512]{2,1,0:T(8,128)S(1)} %copy-done.2, f32[2,192,512]{2,1,0:T(8,128)S(1)} %copy-done.3), custom_call_target="tpu_custom_call" | custom-call | flops 1572864 | bytes 25165824 | tf_op jit(solution)/shard_map/update/pallas_call | solution.py:288
  68.7 0.0 collective-permute-done.24.refs_3_
  68.7 0.1 collective-permute-done.25.refs_4_
  68.8 15.4 %collective-permute-done.26.refs_5_ = bf16[192,512]{1,0:T(8,128)(2,1)S(1)} collective-permute-done((bf16[192,512]{1,0:T(8,128)(2,1)S(1)}, bf16[192,512]{1,0:T(8,128)(2,1)S(1)}, u32[]{:S(2)}, u32[]{:S(2)}) %collective-permute-start.26) | collective-permute-done | bytes 196640 | tf_op jit(solution)/shard_map/ppermute | solution.py:404
  84.2 5.7 %collective-permute-done.27.refs_6_ = bf16[192,512]{1,0:T(8,128)(2,1)S(1)} collective-permute-done((bf16[192,512]{1,0:T(8,128)(2,1)S(1)}, bf16[192,512]{1,0:T(8,128)(2,1)S(1)}, u32[]{:S(2)}, u32[]{:S(2)}) %collective-permute-start.27) | collective-permute-done | bytes 196640 | tf_op jit(solution)/shard_map/ppermute | solution.py:404
  89.9 5.3 %collective-permute-done.28.refs_7_ = bf16[192,512]{1,0:T(8,128)(2,1)S(1)} collective-permute-done((bf16[192,512]{1,0:T(8,128)(2,1)S(1)}, bf16[192,512]{1,0:T(8,128)(2,1)S(1)}, u32[]{:S(2)}, u32[]{:S(2)}) %collective-permute-start.28) | collective-permute-done | bytes 196640 | tf_op jit(solution)/shard_map/ppermute | solution.py:404
  95.2 1.2 %place_blocks.1 = bf16[192,4096]{1,0:T(8,128)(2,1)} custom-call(bf16[192,512]{1,0:T(8,128)(2,1)S(1)} %get-tuple-element.47.refs_0_, bf16[192,512]{1,0:T(8,128)(2,1)S(1)} %collective-permute-done.22.refs_1_, bf16[192,512]{1,0:T(8,128)(2,1)S(1)} %collective-permute-done.23.refs_2_, bf16[192,512]{1,0:T(8,128)(2,1)S(1)} %collective-permute-done.24.refs_3_, ...), custom_call_target="tpu_custom_call" | custom-call | bytes 50331648 | tf_op jit(solution)/shard_map/place_blocks/pallas_call | solution.py:391
  (19 shorter events, 0.1 us)
Async XLA Ops:
  1.3 31.1 %copy-start.1 = (bf16[1,4096,192]{1,2,0:T(8,128)(2,1)S(1)}, bf16[1,4096,192]{1,2,0:T(8,128)(2,1)}, u32[]{:S(2)}) copy-start(bf16[1,4096,192]{1,2,0:T(8,128)(2,1)} %param.15) | copy-start | bytes 4718596
  3.9 13.9 %copy-start.5 = (bf16[24,4096]{1,0:T(8,128)(2,1)S(1)}, bf16[24,4096]{1,0:T(8,128)(2,1)}, u32[]{:S(2)}) copy-start(bf16[24,4096]{1,0:T(8,128)(2,1)} %get-tuple-element.33.refs_0_) | copy-start | bytes 589828
  3.9 28.5 %copy-start = (bf16[1,4096,192]{1,2,0:T(8,128)(2,1)S(1)}, bf16[1,4096,192]{1,2,0:T(8,128)(2,1)}, u32[]{:S(2)}) copy-start(bf16[1,4096,192]{1,2,0:T(8,128)(2,1)} %param.14) | copy-start | bytes 4718596
  4.0 0.9 copy-start.6
  6.6 3.0 %collective-permute-start.16 = (bf16[2,24,512]{2,1,0:T(8,128)(2,1)S(1)}, bf16[2,24,512]{2,1,0:T(8,128)(2,1)S(1)}, u32[]{:S(2)}, u32[]{:S(2)}) collective-permute-start(bf16[2,24,512]{2,1,0:T(8,128)(2,1)S(1)} %get-tuple-element.42), channel_id=1, source_target_pairs={{0,8},{4,12},{8,0},{12,4},{16,24},{20,28},{24,16},{28,20},{1,9},{5... | collective-permute-start | bytes 147464 | tf_op jit(solution)/shard_map/ppermute | solution.py:404
  6.7 4.6 %collective-permute-start.17 = (bf16[2,24,512]{2,1,0:T(8,128)(2,1)S(1)}, bf16[2,24,512]{2,1,0:T(8,128)(2,1)S(1)}, u32[]{:S(2)}, u32[]{:S(2)}) collective-permute-start(bf16[2,24,512]{2,1,0:T(8,128)(2,1)S(1)} %get-tuple-element.43), channel_id=1, source_target_pairs={{0,16},{4,20},{8,24},{12,28},{16,0},{20,4},{24,8},{28,12},{1,17},{... | collective-permute-start | bytes 147464 | tf_op jit(solution)/shard_map/ppermute | solution.py:404
  9.2 3.9 %collective-permute-start.18 = (bf16[2,24,512]{2,1,0:T(8,128)(2,1)S(1)}, bf16[2,24,512]{2,1,0:T(8,128)(2,1)S(1)}, u32[]{:S(2)}, u32[]{:S(2)}) collective-permute-start(bf16[2,24,512]{2,1,0:T(8,128)(2,1)S(1)} %get-tuple-element.44), channel_id=1, source_target_pairs={{0,24},{4,28},{8,16},{12,20},{16,8},{20,12},{24,0},{28,4},{1,25},{... | collective-permute-start | bytes 147464 | tf_op jit(solution)/shard_map/ppermute | solution.py:404
  13.1 3.5 %collective-permute-start.19 = (bf16[4,24,512]{2,1,0:T(8,128)(2,1)S(1)}, bf16[4,24,512]{2,1,0:T(8,128)(2,1)S(1)}, u32[]{:S(2)}, u32[]{:S(2)}) collective-permute-start(bf16[4,24,512]{2,1,0:T(8,128)(2,1)S(1)} %get-tuple-element.46), channel_id=1, source_target_pairs={{0,4},{4,0},{8,12},{12,8},{16,20},{20,16},{24,28},{28,24},{1,5},{5... | collective-permute-start | bytes 294920 | tf_op jit(solution)/shard_map/ppermute | solution.py:404
  16.6 4.6 %collective-permute-start.20 = (bf16[8,24,512]{2,1,0:T(8,128)(2,1)S(1)}, bf16[8,24,512]{2,1,0:T(8,128)(2,1)S(1)}, u32[]{:S(2)}, u32[]{:S(2)}) collective-permute-start(bf16[8,24,512]{2,1,0:T(8,128)(2,1)S(1)} %join.2.one), channel_id=1, source_target_pairs={{0,2},{1,3},{2,0},{3,1},{4,6},{5,7},{6,4},{7,5},{8,10},{9,11},{10,... | collective-permute-start | bytes 589832 | tf_op jit(solution)/shard_map/ppermute | solution.py:404
  17.9 9.9 %collective-permute-start.4 = (bf16[24,4096]{1,0:T(8,128)(2,1)S(1)}, bf16[24,4096]{1,0:T(8,128)(2,1)S(1)}, u32[]{:S(2)}, u32[]{:S(2)}) collective-permute-start(bf16[24,4096]{1,0:T(8,128)(2,1)S(1)} %copy-done.5), channel_id=1, source_target_pairs={{0,2},{1,3},{2,0},{3,1},{4,6},{5,7},{6,4},{7,5},{8,10},{9,11},{10,... | collective-permute-start | bytes 589832 | tf_op jit(solution)/shard_map/ppermute | solution.py:404
  18.1 12.2 %collective-permute-start.1 = (bf16[24,4096]{1,0:T(8,128)(2,1)S(1)}, bf16[24,4096]{1,0:T(8,128)(2,1)S(1)}, u32[]{:S(2)}, u32[]{:S(2)}) collective-permute-start(bf16[24,4096]{1,0:T(8,128)(2,1)S(1)} %get-tuple-element.32.refs_0_), channel_id=1, source_target_pairs={{0,2},{1,3},{2,0},{3,1},{4,6},{5,7},{6,4},{7,5},{8,10},{9,11},{10,... | collective-permute-start | bytes 589832 | tf_op jit(solution)/shard_map/ppermute | solution.py:404
  21.2 29.0 %collective-permute-start.21 = (bf16[16,24,512]{2,1,0:T(8,128)(2,1)S(1)}, bf16[16,24,512]{2,1,0:T(8,128)(2,1)S(1)}, u32[]{:S(2)}, u32[]{:S(2)}) collective-permute-start(bf16[16,24,512]{2,1,0:T(8,128)(2,1)S(1)} %join.3.refs_8_), channel_id=1, source_target_pairs={{0,1},{1,0},{2,3},{3,2},{4,5},{5,4},{6,7},{7,6},{8,9},{9,8},{10,11... | collective-permute-start | bytes 1179656 | tf_op jit(solution)/shard_map/ppermute | solution.py:404
  27.7 4.8 %collective-permute-start.3 = (bf16[24,4096]{1,0:T(8,128)(2,1)S(1)}, bf16[24,4096]{1,0:T(8,128)(2,1)S(1)}, u32[]{:S(2)}, u32[]{:S(2)}) collective-permute-start(bf16[24,4096]{1,0:T(8,128)(2,1)S(1)} %copy-done.5), channel_id=1, source_target_pairs={{0,1},{1,0},{2,3},{3,2},{4,5},{5,4},{6,7},{7,6},{8,9},{9,8},{10,11... | collective-permute-start | bytes 589832 | tf_op jit(solution)/shard_map/ppermute | solution.py:404
  27.7 4.7 %collective-permute-start.5 = (bf16[24,4096]{1,0:T(8,128)(2,1)S(1)}, bf16[24,4096]{1,0:T(8,128)(2,1)S(1)}, u32[]{:S(2)}, u32[]{:S(2)}) collective-permute-start(bf16[24,4096]{1,0:T(8,128)(2,1)S(1)} %collective-permute-done.4.refs_2_), channel_id=1, source_target_pairs={{0,1},{1,0},{2,3},{3,2},{4,5},{5,4},{6,7},{7,6},{8,9},{9,8},{10,11... | collective-permute-start | bytes 589832 | tf_op jit(solution)/shard_map/ppermute | solution.py:404
  30.3 5.8 %collective-permute-start = (bf16[24,4096]{1,0:T(8,128)(2,1)S(1)}, bf16[24,4096]{1,0:T(8,128)(2,1)S(1)}, u32[]{:S(2)}, u32[]{:S(2)}) collective-permute-start(bf16[24,4096]{1,0:T(8,128)(2,1)S(1)} %get-tuple-element.32.refs_0_), channel_id=1, source_target_pairs={{0,1},{1,0},{2,3},{3,2},{4,5},{5,4},{6,7},{7,6},{8,9},{9,8},{10,11... | collective-permute-start | bytes 589832 | tf_op jit(solution)/shard_map/ppermute | solution.py:404
  30.3 9.1 %collective-permute-start.2 = (bf16[24,4096]{1,0:T(8,128)(2,1)S(1)}, bf16[24,4096]{1,0:T(8,128)(2,1)S(1)}, u32[]{:S(2)}, u32[]{:S(2)}) collective-permute-start(bf16[24,4096]{1,0:T(8,128)(2,1)S(1)} %collective-permute-done.1.refs_2_), channel_id=1, source_target_pairs={{0,1},{1,0},{2,3},{3,2},{4,5},{5,4},{6,7},{7,6},{8,9},{9,8},{10,11... | collective-permute-start | bytes 589832 | tf_op jit(solution)/shard_map/ppermute | solution.py:404
  32.4 12.2 %copy-start.4 = (bf16[1,192,4096]{2,1,0:T(8,128)(2,1)S(1)}, bf16[1,192,4096]{2,1,0:T(8,128)(2,1)}, u32[]{:S(2)}) copy-start(bf16[1,192,4096]{2,1,0:T(8,128)(2,1)} %param.16) | copy-start | bytes 4718596
  33.6 6.0 %collective-permute-start.15 = (bf16[112,192]{1,0:T(8,128)(2,1)S(1)}, bf16[112,192]{1,0:T(8,128)(2,1)S(1)}, u32[]{:S(2)}, u32[]{:S(2)}) collective-permute-start(bf16[112,192]{1,0:T(8,128)(2,1)S(1)} %get-tuple-element.40.refs_0_), channel_id=1, source_target_pairs={{0,28},{4,24},{8,20},{12,16},{16,12},{20,8},{24,4},{28,0},{1,29},{... | collective-permute-start | bytes 129032 | tf_op jit(solution)/shard_map/ppermute | solution.py:404
  34.8 8.7 %collective-permute-start.14 = (bf16[112,192]{1,0:T(8,128)(2,1)S(1)}, bf16[112,192]{1,0:T(8,128)(2,1)S(1)}, u32[]{:S(2)}, u32[]{:S(2)}) collective-permute-start(bf16[112,192]{1,0:T(8,128)(2,1)S(1)} %get-tuple-element.40.refs_0_), channel_id=1, source_target_pairs={{0,24},{4,28},{8,16},{12,20},{16,8},{20,12},{24,0},{28,4},{1,25},{... | collective-permute-start | bytes 129032 | tf_op jit(solution)/shard_map/ppermute | solution.py:404
  36.1 7.3 %collective-permute-start.13 = (bf16[112,192]{1,0:T(8,128)(2,1)S(1)}, bf16[112,192]{1,0:T(8,128)(2,1)S(1)}, u32[]{:S(2)}, u32[]{:S(2)}) collective-permute-start(bf16[112,192]{1,0:T(8,128)(2,1)S(1)} %get-tuple-element.40.refs_0_), channel_id=1, source_target_pairs={{0,20},{4,16},{8,28},{12,24},{16,4},{20,0},{24,12},{28,8},{1,21},{... | collective-permute-start | bytes 129032 | tf_op jit(solution)/shard_map/ppermute | solution.py:404
  39.5 7.1 %collective-permute-start.12 = (bf16[112,192]{1,0:T(8,128)(2,1)S(1)}, bf16[112,192]{1,0:T(8,128)(2,1)S(1)}, u32[]{:S(2)}, u32[]{:S(2)}) collective-permute-start(bf16[112,192]{1,0:T(8,128)(2,1)S(1)} %get-tuple-element.40.refs_0_), channel_id=1, source_target_pairs={{0,16},{4,20},{8,24},{12,28},{16,0},{20,4},{24,8},{28,12},{1,17},{... | collective-permute-start | bytes 129032 | tf_op jit(solution)/shard_map/ppermute | solution.py:404
  39.6 8.7 %collective-permute-start.11 = (bf16[112,192]{1,0:T(8,128)(2,1)S(1)}, bf16[112,192]{1,0:T(8,128)(2,1)S(1)}, u32[]{:S(2)}, u32[]{:S(2)}) collective-permute-start(bf16[112,192]{1,0:T(8,128)(2,1)S(1)} %get-tuple-element.40.refs_0_), channel_id=1, source_target_pairs={{0,12},{4,8},{8,4},{12,0},{16,28},{20,24},{24,20},{28,16},{1,13},{... | collective-permute-start | bytes 129032 | tf_op jit(solution)/shard_map/ppermute | solution.py:404
  43.4 6.1 %collective-permute-start.10 = (bf16[112,192]{1,0:T(8,128)(2,1)S(1)}, bf16[112,192]{1,0:T(8,128)(2,1)S(1)}, u32[]{:S(2)}, u32[]{:S(2)}) collective-permute-start(bf16[112,192]{1,0:T(8,128)(2,1)S(1)} %get-tuple-element.40.refs_0_), channel_id=1, source_target_pairs={{0,8},{4,12},{8,0},{12,4},{16,24},{20,28},{24,16},{28,20},{1,9},{5... | collective-permute-start | bytes 129032 | tf_op jit(solution)/shard_map/ppermute | solution.py:404
  43.4 6.8 %collective-permute-start.9 = (bf16[112,192]{1,0:T(8,128)(2,1)S(1)}, bf16[112,192]{1,0:T(8,128)(2,1)S(1)}, u32[]{:S(2)}, u32[]{:S(2)}) collective-permute-start(bf16[112,192]{1,0:T(8,128)(2,1)S(1)} %get-tuple-element.40.refs_0_), channel_id=1, source_target_pairs={{0,4},{4,0},{8,12},{12,8},{16,20},{20,16},{24,28},{28,24},{1,5},{5... | collective-permute-start | bytes 129032 | tf_op jit(solution)/shard_map/ppermute | solution.py:404
  44.6 5.6 %copy-start.2 = (f32[2,192,512]{2,1,0:T(8,128)S(1)}, f32[2,192,512]{2,1,0:T(8,128)}, u32[]{:S(2)}) copy-start(f32[2,192,512]{2,1,0:T(8,128)} %first.1) | copy-start | bytes 2359300
  44.6 5.6 %copy-start.3 = (f32[2,192,512]{2,1,0:T(8,128)S(1)}, f32[2,192,512]{2,1,0:T(8,128)}, u32[]{:S(2)}) copy-start(f32[2,192,512]{2,1,0:T(8,128)} %second.1) | copy-start | bytes 2359300
  46.5 8.2 %collective-permute-start.6 = (bf16[24,4096]{1,0:T(8,128)(2,1)S(1)}, bf16[24,4096]{1,0:T(8,128)(2,1)S(1)}, u32[]{:S(2)}, u32[]{:S(2)}) collective-permute-start(bf16[24,4096]{1,0:T(8,128)(2,1)S(1)} %get-tuple-element.37), channel_id=1, source_target_pairs={{0,1},{1,0},{2,3},{3,2},{4,5},{5,4},{6,7},{7,6},{8,9},{9,8},{10,11... | collective-permute-start | bytes 589832 | tf_op jit(solution)/shard_map/ppermute | solution.py:404
  48.3 7.4 %collective-permute-start.7 = (bf16[24,4096]{1,0:T(8,128)(2,1)S(1)}, bf16[24,4096]{1,0:T(8,128)(2,1)S(1)}, u32[]{:S(2)}, u32[]{:S(2)}) collective-permute-start(bf16[24,4096]{1,0:T(8,128)(2,1)S(1)} %get-tuple-element.38), channel_id=1, source_target_pairs={{0,2},{1,3},{2,0},{3,1},{4,6},{5,7},{6,4},{7,5},{8,10},{9,11},{10,... | collective-permute-start | bytes 589832 | tf_op jit(solution)/shard_map/ppermute | solution.py:404
  49.5 9.9 %collective-permute-start.8 = (bf16[24,4096]{1,0:T(8,128)(2,1)S(1)}, bf16[24,4096]{1,0:T(8,128)(2,1)S(1)}, u32[]{:S(2)}, u32[]{:S(2)}) collective-permute-start(bf16[24,4096]{1,0:T(8,128)(2,1)S(1)} %get-tuple-element.39), channel_id=1, source_target_pairs={{0,3},{1,2},{2,1},{3,0},{4,7},{5,6},{6,5},{7,4},{8,11},{9,10},{10,... | collective-permute-start | bytes 589832 | tf_op jit(solution)/shard_map/ppermute | solution.py:404
  51.4 11.7 %collective-permute-start.22 = (bf16[192,512]{1,0:T(8,128)(2,1)S(1)}, bf16[192,512]{1,0:T(8,128)(2,1)S(1)}, u32[]{:S(2)}, u32[]{:S(2)}) collective-permute-start(bf16[192,512]{1,0:T(8,128)(2,1)S(1)} %get-tuple-element.48), channel_id=1, source_target_pairs={{0,4},{4,0},{8,12},{12,8},{16,20},{20,16},{24,28},{28,24},{1,5},{5... | collective-permute-start | bytes 589832 | tf_op jit(solution)/shard_map/ppermute | solution.py:404
  52.3 11.4 %collective-permute-start.23 = (bf16[192,512]{1,0:T(8,128)(2,1)S(1)}, bf16[192,512]{1,0:T(8,128)(2,1)S(1)}, u32[]{:S(2)}, u32[]{:S(2)}) collective-permute-start(bf16[192,512]{1,0:T(8,128)(2,1)S(1)} %get-tuple-element.49), channel_id=1, source_target_pairs={{0,8},{4,12},{8,0},{12,4},{16,24},{20,28},{24,16},{28,20},{1,9},{5... | collective-permute-start | bytes 589832 | tf_op jit(solution)/shard_map/ppermute | solution.py:404
  54.7 14.0 %collective-permute-start.24 = (bf16[192,512]{1,0:T(8,128)(2,1)S(1)}, bf16[192,512]{1,0:T(8,128)(2,1)S(1)}, u32[]{:S(2)}, u32[]{:S(2)}) collective-permute-start(bf16[192,512]{1,0:T(8,128)(2,1)S(1)} %get-tuple-element.50), channel_id=1, source_target_pairs={{0,12},{4,8},{8,4},{12,0},{16,28},{20,24},{24,20},{28,16},{1,13},{... | collective-permute-start | bytes 589832 | tf_op jit(solution)/shard_map/ppermute | solution.py:404
  55.7 13.1 %collective-permute-start.25 = (bf16[192,512]{1,0:T(8,128)(2,1)S(1)}, bf16[192,512]{1,0:T(8,128)(2,1)S(1)}, u32[]{:S(2)}, u32[]{:S(2)}) collective-permute-start(bf16[192,512]{1,0:T(8,128)(2,1)S(1)} %get-tuple-element.51), channel_id=1, source_target_pairs={{0,16},{4,20},{8,24},{12,28},{16,0},{20,4},{24,8},{28,12},{1,17},{... | collective-permute-start | bytes 589832 | tf_op jit(solution)/shard_map/ppermute | solution.py:404
  59.5 24.8 %collective-permute-start.26 = (bf16[192,512]{1,0:T(8,128)(2,1)S(1)}, bf16[192,512]{1,0:T(8,128)(2,1)S(1)}, u32[]{:S(2)}, u32[]{:S(2)}) collective-permute-start(bf16[192,512]{1,0:T(8,128)(2,1)S(1)} %get-tuple-element.52), channel_id=1, source_target_pairs={{0,20},{4,16},{8,28},{12,24},{16,4},{20,0},{24,12},{28,8},{1,21},{... | collective-permute-start | bytes 589832 | tf_op jit(solution)/shard_map/ppermute | solution.py:404
  63.0 26.9 %collective-permute-start.27 = (bf16[192,512]{1,0:T(8,128)(2,1)S(1)}, bf16[192,512]{1,0:T(8,128)(2,1)S(1)}, u32[]{:S(2)}, u32[]{:S(2)}) collective-permute-start(bf16[192,512]{1,0:T(8,128)(2,1)S(1)} %get-tuple-element.53), channel_id=1, source_target_pairs={{0,24},{4,28},{8,16},{12,20},{16,8},{20,12},{24,0},{28,4},{1,25},{... | collective-permute-start | bytes 589832 | tf_op jit(solution)/shard_map/ppermute | solution.py:404
  63.8 31.4 %collective-permute-start.28 = (bf16[192,512]{1,0:T(8,128)(2,1)S(1)}, bf16[192,512]{1,0:T(8,128)(2,1)S(1)}, u32[]{:S(2)}, u32[]{:S(2)}) collective-permute-start(bf16[192,512]{1,0:T(8,128)(2,1)S(1)} %get-tuple-element.54), channel_id=1, source_target_pairs={{0,28},{4,24},{8,20},{12,16},{16,12},{20,8},{24,4},{28,0},{1,29},{... | collective-permute-start | bytes 589832 | tf_op jit(solution)/shard_map/ppermute | solution.py:404

commit v2 on v1

--- a/solution.py
+++ b/solution.py
@@ -239,12 +239,16 @@
         summed[cand] = grad
         one, two = moments(grad, first[cand], second[cand])
         dir_list.append(one / first_fix / (jnp.sqrt(two / second_fix) + adam_eps))
+    both = dirs[groups]
+    split = dir_list[0].shape[0] - both.shape[1]
+    for cand in range(CANDS):
+        both[cand] = dir_list[cand][split:].astype(BF16)
     for peer in range(groups):
         tag = hiddens[peer][count : count + TAG, :].astype(F32)[0:1, 0:1]
         out = dir_list[0]
         for cand in range(1, CANDS):
             out = jnp.where(tag == float(cand), dir_list[cand], out)
-        dirs[peer][...] = out.astype(BF16)
+        dirs[peer][...] = out[: dirs[peer].shape[0]].astype(BF16)
 
 
 def moments(gradient, first_moment, second):
@@ -257,17 +261,44 @@
     groups = len(hiddens)
     parts = 2 * blocks[0].shape[0] // groups
     units, columns = first.shape[1:]
+    split = units // 2
     rows = groups * parts * CAP
     return pl.pallas_call(
         functools.partial(adam_kernel, groups, parts),
         in_specs=[LOCAL] * (groups + 4),
-        out_specs=[LOCAL] * (1 + groups),
+        out_specs=[LOCAL] * (2 + groups),
         out_shape=[jax.ShapeDtypeStruct(first.shape, F32)]
-        + [jax.ShapeDtypeStruct((units, columns), BF16)] * groups,
+        + [jax.ShapeDtypeStruct((units, columns), BF16)] * (groups // 2)
+        + [jax.ShapeDtypeStruct((split, columns), BF16)] * (groups // 2)
+        + [jax.ShapeDtypeStruct((CANDS, units - split, columns), BF16)],
         compiler_params=PARAMS,
         cost_estimate=cost(2 * CANDS * rows * units * columns, 8 * first.size),
         name="adam",
     )(*hiddens, *blocks, first, second)
+
+
+def choose_kernel(half, *refs):
+    hiddens, both, outs = refs[:half], refs[half], refs[half + 1 :]
+    for peer in range(half):
+        count = hiddens[peer].shape[0] - TAG
+        tag = hiddens[peer][count : count + TAG, :].astype(F32)[0:1, 0:1]
+        out = both[0].astype(F32)
+        for cand in range(1, CANDS):
+            out = jnp.where(tag == float(cand), both[cand].astype(F32), out)
+        outs[peer][...] = out.astype(BF16)
+
+
+def choose(hiddens, both):
+    half = len(hiddens)
+    return pl.pallas_call(
+        functools.partial(choose_kernel, half),
+        in_specs=[LOCAL] * (half + 1),
+        out_specs=[LOCAL] * half,
+        out_shape=[jax.ShapeDtypeStruct(both.shape[1:], BF16)] * half,
+        compiler_params=PARAMS,
+        cost_estimate=cost(both.size, 2 * half * both.size),
+        name="choose",
+    )(*hiddens, both)
 
 
 def update_kernel(summed, first, second, new_first, new_second, one_out, two_out, sems):
@@ -370,30 +401,30 @@
 
 def place_kernel(groups, *refs):
     me = lax.axis_index("grp")
-    blocks, out, sems = refs[:groups], refs[groups], refs[groups + 1]
-    columns = blocks[0].shape[1]
+    half = groups // 2
+    blocks, (out, sems) = refs[: groups + half], refs[groups + half :]
+    units, columns = blocks[0].shape
     copies = []
-    for peer in range(groups):
+    for number, block in enumerate(blocks):
+        rows = block.shape[0]
+        peer = number if number < groups else number - half
         start = pl.multiple_of((me ^ peer) * columns, 128)
-        copies.append(
-            pltpu.make_async_copy(
-                blocks[peer], out.at[:, pl.ds(start, columns)], sems.at[peer]
-            )
-        )
+        at = pl.ds(0 if number < groups else units - rows, rows)
+        target = out.at[at, pl.ds(start, columns)]
+        copies.append(pltpu.make_async_copy(block, target, sems.at[number]))
         copies[-1].start()
     for copy in copies:
         copy.wait()
 
 
-def place_blocks(blocks):
-    groups = len(blocks)
+def place_blocks(groups, blocks):
     units, columns = blocks[0].shape
     return pl.pallas_call(
         functools.partial(place_kernel, groups),
-        in_specs=[LOCAL] * groups,
+        in_specs=[LOCAL] * len(blocks),
         out_specs=FAR,
         out_shape=jax.ShapeDtypeStruct((units, groups * columns), BF16),
-        scratch_shapes=[pltpu.SemaphoreType.DMA((groups,))],
+        scratch_shapes=[pltpu.SemaphoreType.DMA((len(blocks),))],
         compiler_params=PARAMS,
         cost_estimate=cost(0, 4 * groups * units * columns),
         name="place_blocks",
@@ -440,7 +471,7 @@
 
     def exchange(values):
         got = [values[0]]
-        for bits in range(1, groups):
+        for bits in range(1, len(values)):
             got.append(swap(values[bits], "grp", groups, bits))
         return got
 
@@ -475,8 +506,11 @@
         my_cand = lax.dynamic_index_in_dim(placement, slot_of(0), 1, keepdims=True)
     pre_gate, pre_up, hidden = forward(my_cand, in_rows, w_gate, w_up)
     hiddens = exchange([hidden] * groups)
-    summed, *dirs = adam(hiddens, columns, moment_first, moment_second)
+    summed, *dirs, both = adam(hiddens, columns, moment_first, moment_second)
     got_dirs = exchange(dirs)
+    both = swap(both, "grp", groups, groups // 2)
+    dirs = choose(hiddens[: groups // 2], both)
+    got_dirs = got_dirs + exchange(dirs)
     new_first, new_second = update(summed, moment_first, moment_second)
 
     in_scaled = share(per_slot(scaled), 0)
@@ -485,7 +519,7 @@
     for bits in range(1, num_ep):
         returned.append(swap(partials[bits], "ep", num_ep, bits))
     token_grad = combine(picks, returned)
-    step_dir = place_blocks(got_dirs)[None]
+    step_dir = place_blocks(groups, got_dirs)[None]
     return (token_grad, step_dir, new_first, new_second)
 
 

time: 96.6 us -> 98.3 us (1.018)
  the two profiles are of different devices: /device:TPU:9 before, /device:TPU:0 now
where the time goes in v2:
time: 98.3 us; the launch traced here: 98.1 us
  waiting for transfers between devices  43 us (44%)
  starting transfers between devices  40.1 us (41%)
  Pallas kernels  12.7 us (13%)
  between operations  1.5 us (2%)
    ppermute x33, waiting for transfers between devices, swap(): return lax.ppermute(value, axis, [(i, i ^ bits) for i in range(size)])  43 us
    ppermute x33, starting transfers between devices, swap(): return lax.ppermute(value, axis, [(i, i ^ bits) for i in range(size)])  40.1 us
    pallas_call x1, Pallas kernels, select(): pl.pallas_call(functools.partial(select_kernel, slots, pieces), in_specs=...  2.63 us
  transfers between devices with their start and end apart: 33, of which 15 were waited for; matrix products, arithmetic and copies ran while one was open for 0% of the time, Pallas kernels for 7%

profile of v2, /device:TPU:0, one launch (start us, length us, event | category | flops | bytes accessed | tf_op | source)
XLA Modules:
  0.0 98.1 jit_solution(2688544473131735273)
XLA Ops:
  1.3 2.6 %select_rows.1 = (bf16[24,4096]{1,0:T(8,128)(2,1)}, f32[24,192]{1,0:T(8,128)}) custom-call(s32[1,1]{1,0:T(1,128)S(6)} %copy.14.place, s32[8,192]{1,0:T(8,128)} %bitcast.16, f32[8,192]{1,0:T(8,128)} %bitcast.17, bf16[192,4096]{1,0:T(8,128)(2,1)} %tokens.1), custom_call_target="tpu_custom_call" | custom-call | flops 37748736 | bytes 25165824 | tf_op jit(solution)/shard_map/select_rows/pallas_call | solution.py:85
  3.9 0.0 copy-start.5
  3.9 0.0 copy-start
  4.0 0.0 copy-start.6
  4.0 0.9 copy-done.6
  4.8 1.8 %scale_rows.1 = (bf16[24,4096]{1,0:T(8,128)(2,1)S(1)}, bf16[2,24,512]{2,1,0:T(8,128)(2,1)S(1)}, bf16[2,24,512]{2,1,0:T(8,128)(2,1)S(1)}, bf16[2,24,512]{2,1,0:T(8,128)(2,1)S(1)}, bf16[2,24,512]{2,1,0:T(8,128)(2,1)S(1)}) custom-call(f32[24,192]{1,0:T(8,128)S(1)} %copy-done.6, bf16[192,4096]{1,0:T(8,128)(2,1)} %grads.1), custom_call_target="tpu_custom_call" | custom-call | flops 37748736 | bytes 100663296 | tf_op jit(solution)/shard_map/scale_rows/pallas_call | solution.py:134
  6.6 3.1 %collective-permute-start.16 = (bf16[2,24,512]{2,1,0:T(8,128)(2,1)S(1)}, bf16[2,24,512]{2,1,0:T(8,128)(2,1)S(1)}, u32[]{:S(2)}, u32[]{:S(2)}) collective-permute-start(bf16[2,24,512]{2,1,0:T(8,128)(2,1)S(1)} %get-tuple-element.47), channel_id=1, source_target_pairs={{0,8},{4,12},{8,0},{12,4},{16,24},{20,28},{24,16},{28,20},{1,9},{5... | collective-permute-start | bytes 147464 | tf_op jit(solution)/shard_map/ppermute | solution.py:435
  9.7 2.6 %collective-permute-start.17 = (bf16[2,24,512]{2,1,0:T(8,128)(2,1)S(1)}, bf16[2,24,512]{2,1,0:T(8,128)(2,1)S(1)}, u32[]{:S(2)}, u32[]{:S(2)}) collective-permute-start(bf16[2,24,512]{2,1,0:T(8,128)(2,1)S(1)} %get-tuple-element.48), channel_id=1, source_target_pairs={{0,16},{4,20},{8,24},{12,28},{16,0},{20,4},{24,8},{28,12},{1,17},{... | collective-permute-start | bytes 147464 | tf_op jit(solution)/shard_map/ppermute | solution.py:435
  12.3 0.0 collective-permute-start.18
  12.3 3.3 %collective-permute-done.17.refs_2_ = bf16[2,24,512]{2,1,0:T(8,128)(2,1)S(1)} collective-permute-done((bf16[2,24,512]{2,1,0:T(8,128)(2,1)S(1)}, bf16[2,24,512]{2,1,0:T(8,128)(2,1)S(1)}, u32[]{:S(2)}, u32[]{:S(2)}) %collective-permute-start.17) | collective-permute-done | bytes 49184 | tf_op jit(solution)/shard_map/ppermute | solution.py:435
  15.7 2.6 %collective-permute-done.18.refs_3_ = bf16[2,24,512]{2,1,0:T(8,128)(2,1)S(1)} collective-permute-done((bf16[2,24,512]{2,1,0:T(8,128)(2,1)S(1)}, bf16[2,24,512]{2,1,0:T(8,128)(2,1)S(1)}, u32[]{:S(2)}, u32[]{:S(2)}) %collective-permute-start.18) | collective-permute-done | bytes 49184 | tf_op jit(solution)/shard_map/ppermute | solution.py:435
  18.2 1.6 %collective-permute-start.19 = (bf16[4,24,512]{2,1,0:T(8,128)(2,1)S(1)}, bf16[4,24,512]{2,1,0:T(8,128)(2,1)S(1)}, u32[]{:S(2)}, u32[]{:S(2)}) collective-permute-start(bf16[4,24,512]{2,1,0:T(8,128)(2,1)S(1)} %get-tuple-element.51), channel_id=1, source_target_pairs={{0,4},{4,0},{8,12},{12,8},{16,20},{20,16},{24,28},{28,24},{1,5},{5... | collective-permute-start | bytes 294920 | tf_op jit(solution)/shard_map/ppermute | solution.py:435
  19.8 3.1 %collective-permute-done.19.two = bf16[4,24,512]{2,1,0:T(8,128)(2,1)S(1)} collective-permute-done((bf16[4,24,512]{2,1,0:T(8,128)(2,1)S(1)}, bf16[4,24,512]{2,1,0:T(8,128)(2,1)S(1)}, u32[]{:S(2)}, u32[]{:S(2)}) %collective-permute-start.19) | collective-permute-done | bytes 98336 | tf_op jit(solution)/shard_map/ppermute | solution.py:435
  22.9 1.6 %collective-permute-start.20 = (bf16[8,24,512]{2,1,0:T(8,128)(2,1)S(1)}, bf16[8,24,512]{2,1,0:T(8,128)(2,1)S(1)}, u32[]{:S(2)}, u32[]{:S(2)}) collective-permute-start(bf16[8,24,512]{2,1,0:T(8,128)(2,1)S(1)} %join.2.one), channel_id=1, source_target_pairs={{0,2},{1,3},{2,0},{3,1},{4,6},{5,7},{6,4},{7,5},{8,10},{9,11},{10,... | collective-permute-start | bytes 589832 | tf_op jit(solution)/shard_map/ppermute | solution.py:435
  24.5 0.5 collective-permute-start.4
  25.0 1.5 %collective-permute-start.1 = (bf16[24,4096]{1,0:T(8,128)(2,1)S(1)}, bf16[24,4096]{1,0:T(8,128)(2,1)S(1)}, u32[]{:S(2)}, u32[]{:S(2)}) collective-permute-start(bf16[24,4096]{1,0:T(8,128)(2,1)S(1)} %get-tuple-element.37.refs_0_), channel_id=1, source_target_pairs={{0,2},{1,3},{2,0},{3,1},{4,6},{5,7},{6,4},{7,5},{8,10},{9,11},{10,... | collective-permute-start | bytes 589832 | tf_op jit(solution)/shard_map/ppermute | solution.py:435
  26.5 4.3 %collective-permute-done.20.two = bf16[8,24,512]{2,1,0:T(8,128)(2,1)S(1)} collective-permute-done((bf16[8,24,512]{2,1,0:T(8,128)(2,1)S(1)}, bf16[8,24,512]{2,1,0:T(8,128)(2,1)S(1)}, u32[]{:S(2)}, u32[]{:S(2)}) %collective-permute-start.20) | collective-permute-done | bytes 196640 | tf_op jit(solution)/shard_map/ppermute | solution.py:435
  30.8 0.1 collective-permute-start.21
  30.9 0.5 collective-permute-start.3
  31.4 1.8 %collective-permute-done.4.refs_2_ = bf16[24,4096]{1,0:T(8,128)(2,1)S(1)} collective-permute-done((bf16[24,4096]{1,0:T(8,128)(2,1)S(1)}, bf16[24,4096]{1,0:T(8,128)(2,1)S(1)}, u32[]{:S(2)}, u32[]{:S(2)}) %collective-permute-start.4) | collective-permute-done | bytes 196640 | tf_op jit(solution)/shard_map/ppermute | solution.py:435
  33.2 0.5 collective-permute-start
  33.7 1.6 %collective-permute-done.1.refs_2_ = bf16[24,4096]{1,0:T(8,128)(2,1)S(1)} collective-permute-done((bf16[24,4096]{1,0:T(8,128)(2,1)S(1)}, bf16[24,4096]{1,0:T(8,128)(2,1)S(1)}, u32[]{:S(2)}, u32[]{:S(2)}) %collective-permute-start.1) | collective-permute-done | bytes 196640 | tf_op jit(solution)/shard_map/ppermute | solution.py:435
  35.3 0.0 collective-permute-done.3.refs_1_
  35.3 0.0 collective-permute-done.5.refs_3_
  35.3 0.0 copy-start.4
  35.4 1.1 %forward.1 = (f32[96,192]{1,0:T(8,128)S(1)}, f32[96,192]{1,0:T(8,128)S(1)}, bf16[112,192]{1,0:T(8,128)(2,1)S(1)}) custom-call(s32[1,1]{1,0:T(1,128)S(6)} %copy.14.place, bf16[24,4096]{1,0:T(8,128)(2,1)S(1)} %copy-done.5, bf16[24,4096]{1,0:T(8,128)(2,1)S(1)} %collective-permute-done.3.refs_1_, bf16[24,4096]{1,0:T(8,128)(2,1)S(1)} %collective-permute-done.4.refs_2_, ...), custom_call_target="tpu_custom_call" | custom-call | flops 301989888 | bytes 50331648 | tf_op jit(solution)/shard_map/forward/pallas_call | solution.py:201
  36.5 1.8 %collective-permute-start.15 = (bf16[112,192]{1,0:T(8,128)(2,1)S(1)}, bf16[112,192]{1,0:T(8,128)(2,1)S(1)}, u32[]{:S(2)}, u32[]{:S(2)}) collective-permute-start(bf16[112,192]{1,0:T(8,128)(2,1)S(1)} %get-tuple-element.45.refs_0_), channel_id=1, source_target_pairs={{0,28},{4,24},{8,20},{12,16},{16,12},{20,8},{24,4},{28,0},{1,29},{... | collective-permute-start | bytes 129032 | tf_op jit(solution)/shard_map/ppermute | solution.py:435
  38.3 3.0 %collective-permute-start.14 = (bf16[112,192]{1,0:T(8,128)(2,1)S(1)}, bf16[112,192]{1,0:T(8,128)(2,1)S(1)}, u32[]{:S(2)}, u32[]{:S(2)}) collective-permute-start(bf16[112,192]{1,0:T(8,128)(2,1)S(1)} %get-tuple-element.45.refs_0_), channel_id=1, source_target_pairs={{0,24},{4,28},{8,16},{12,20},{16,8},{20,12},{24,0},{28,4},{1,25},{... | collective-permute-start | bytes 129032 | tf_op jit(solution)/shard_map/ppermute | solution.py:435
  41.4 0.0 collective-permute-start.13
  41.4 0.0 collective-permute-done.2.refs_3_
  41.4 2.9 %collective-permute-start.12 = (bf16[112,192]{1,0:T(8,128)(2,1)S(1)}, bf16[112,192]{1,0:T(8,128)(2,1)S(1)}, u32[]{:S(2)}, u32[]{:S(2)}) collective-permute-start(bf16[112,192]{1,0:T(8,128)(2,1)S(1)} %get-tuple-element.45.refs_0_), channel_id=1, source_target_pairs={{0,16},{4,20},{8,24},{12,28},{16,0},{20,4},{24,8},{28,12},{1,17},{... | collective-permute-start | bytes 129032 | tf_op jit(solution)/shard_map/ppermute | solution.py:435
  44.2 0.0 copy-start.2
  44.3 0.0 copy-start.3
  44.3 1.9 %backward.1 = (bf16[24,4096]{1,0:T(8,128)(2,1)S(1)}, bf16[24,4096]{1,0:T(8,128)(2,1)S(1)}, bf16[24,4096]{1,0:T(8,128)(2,1)S(1)}, bf16[24,4096]{1,0:T(8,128)(2,1)S(1)}) custom-call(bf16[24,4096]{1,0:T(8,128)(2,1)S(1)} %get-tuple-element.37.refs_0_, bf16[24,4096]{1,0:T(8,128)(2,1)S(1)} %collective-permute-done.refs_1_, ...), custom_call_target="tpu_custom_call" | custom-call | flops 452984832 | bytes 75497472 | tf_op jit(solution)/shard_map/backward/pallas_call | solution.py:356
  46.2 0.1 collective-permute-start.6
  46.3 2.4 %collective-permute-done.13.refs_5_ = bf16[112,192]{1,0:T(8,128)(2,1)S(1)} collective-permute-done((bf16[112,192]{1,0:T(8,128)(2,1)S(1)}, bf16[112,192]{1,0:T(8,128)(2,1)S(1)}, u32[]{:S(2)}, u32[]{:S(2)}) %collective-permute-start.13) | collective-permute-done | bytes 43040 | tf_op jit(solution)/shard_map/ppermute | solution.py:435
  48.7 1.5 %collective-permute-start.7 = (bf16[24,4096]{1,0:T(8,128)(2,1)S(1)}, bf16[24,4096]{1,0:T(8,128)(2,1)S(1)}, u32[]{:S(2)}, u32[]{:S(2)}) collective-permute-start(bf16[24,4096]{1,0:T(8,128)(2,1)S(1)} %get-tuple-element.43), channel_id=1, source_target_pairs={{0,2},{1,3},{2,0},{3,1},{4,6},{5,7},{6,4},{7,5},{8,10},{9,11},{10,... | collective-permute-start | bytes 589832 | tf_op jit(solution)/shard_map/ppermute | solution.py:435
  50.2 0.0 collective-permute-done.12.refs_4_
  50.2 0.6 collective-permute-start.10
  50.8 1.4 %collective-permute-start.9 = (bf16[112,192]{1,0:T(8,128)(2,1)S(1)}, bf16[112,192]{1,0:T(8,128)(2,1)S(1)}, u32[]{:S(2)}, u32[]{:S(2)}) collective-permute-start(bf16[112,192]{1,0:T(8,128)(2,1)S(1)} %get-tuple-element.45.refs_0_), channel_id=1, source_target_pairs={{0,4},{4,0},{8,12},{12,8},{16,20},{20,16},{24,28},{28,24},{1,5},{5... | collective-permute-start | bytes 129032 | tf_op jit(solution)/shard_map/ppermute | solution.py:435
  52.2 2.2 %collective-permute-done.10.refs_2_ = bf16[112,192]{1,0:T(8,128)(2,1)S(1)} collective-permute-done((bf16[112,192]{1,0:T(8,128)(2,1)S(1)}, bf16[112,192]{1,0:T(8,128)(2,1)S(1)}, u32[]{:S(2)}, u32[]{:S(2)}) %collective-permute-start.10) | collective-permute-done | bytes 43040 | tf_op jit(solution)/shard_map/ppermute | solution.py:435
  54.4 0.0 collective-permute-start.8
  54.4 0.6 collective-permute-done.9.refs_1_
  55.0 1.1 %adam.1 = (f32[2,192,512]{2,1,0:T(8,128)S(1)}, bf16[192,512]{1,0:T(8,128)(2,1)S(1)}, bf16[192,512]{1,0:T(8,128)(2,1)S(1)}, bf16[192,512]{1,0:T(8,128)(2,1)S(1)},...) custom-call(bf16[112,192]{1,0:T(8,128)(2,1)S(1)} %get-tuple-element., ...), custom_call_target="tpu_custom_call" | custom-call | flops 301989888 | bytes 25165824 | tf_op jit(solution)/shard_map/adam/pallas_call | solution.py:266
  56.0 1.8 %collective-permute-start.29 = (bf16[2,96,512]{2,1,0:T(8,128)(2,1)S(1)}, bf16[2,96,512]{2,1,0:T(8,128)(2,1)S(1)}, u32[]{:S(2)}, u32[]{:S(2)}) collective-permute-start(bf16[2,96,512]{2,1,0:T(8,128)(2,1)S(1)} %get-tuple-element.60), channel_id=1, source_target_pairs={{0,16},{4,20},{8,24},{12,28},{16,0},{20,4},{24,8},{28,12},{1,17},{... | collective-permute-start | bytes 589832 | tf_op jit(solution)/shard_map/ppermute | solution.py:435
  57.8 1.2 %collective-permute-start.25 = (bf16[96,512]{1,0:T(8,128)(2,1)S(1)}, bf16[96,512]{1,0:T(8,128)(2,1)S(1)}, u32[]{:S(2)}, u32[]{:S(2)}) collective-permute-start(bf16[96,512]{1,0:T(8,128)(2,1)S(1)} %get-tuple-element.56), channel_id=1, source_target_pairs={{0,16},{4,20},{8,24},{12,28},{16,0},{20,4},{24,8},{28,12},{1,17},{... | collective-permute-start | bytes 294920 | tf_op jit(solution)/shard_map/ppermute | solution.py:435
  59.0 3.2 %collective-permute-start.26 = (bf16[96,512]{1,0:T(8,128)(2,1)S(1)}, bf16[96,512]{1,0:T(8,128)(2,1)S(1)}, u32[]{:S(2)}, u32[]{:S(2)}) collective-permute-start(bf16[96,512]{1,0:T(8,128)(2,1)S(1)} %get-tuple-element.57), channel_id=1, source_target_pairs={{0,20},{4,16},{8,28},{12,24},{16,4},{20,0},{24,12},{28,8},{1,21},{... | collective-permute-start | bytes 294920 | tf_op jit(solution)/shard_map/ppermute | solution.py:435
  62.2 0.0 collective-permute-start.22
  62.2 2.1 %collective-permute-start.27 = (bf16[96,512]{1,0:T(8,128)(2,1)S(1)}, bf16[96,512]{1,0:T(8,128)(2,1)S(1)}, u32[]{:S(2)}, u32[]{:S(2)}) collective-permute-start(bf16[96,512]{1,0:T(8,128)(2,1)S(1)} %get-tuple-element.58), channel_id=1, source_target_pairs={{0,24},{4,28},{8,16},{12,20},{16,8},{20,12},{24,0},{28,4},{1,25},{... | collective-permute-start | bytes 294920 | tf_op jit(solution)/shard_map/ppermute | solution.py:435
  64.3 12.3 %collective-permute-done.25.refs_4_ = bf16[96,512]{1,0:T(8,128)(2,1)S(1)} collective-permute-done((bf16[96,512]{1,0:T(8,128)(2,1)S(1)}, bf16[96,512]{1,0:T(8,128)(2,1)S(1)}, u32[]{:S(2)}, u32[]{:S(2)}) %collective-permute-start.25) | collective-permute-done | bytes 98336 | tf_op jit(solution)/shard_map/ppermute | solution.py:435
  76.6 2.5 %collective-permute-start.28 = (bf16[96,512]{1,0:T(8,128)(2,1)S(1)}, bf16[96,512]{1,0:T(8,128)(2,1)S(1)}, u32[]{:S(2)}, u32[]{:S(2)}) collective-permute-start(bf16[96,512]{1,0:T(8,128)(2,1)S(1)} %get-tuple-element.59), channel_id=1, source_target_pairs={{0,28},{4,24},{8,20},{12,16},{16,12},{20,8},{24,4},{28,0},{1,29},{... | collective-permute-start | bytes 294920 | tf_op jit(solution)/shard_map/ppermute | solution.py:435
  79.2 0.1 collective-permute-done.26.refs_5_
  79.2 2.4 %collective-permute-start.24 = (bf16[192,512]{1,0:T(8,128)(2,1)S(1)}, bf16[192,512]{1,0:T(8,128)(2,1)S(1)}, u32[]{:S(2)}, u32[]{:S(2)}) collective-permute-start(bf16[192,512]{1,0:T(8,128)(2,1)S(1)} %get-tuple-element.55), channel_id=1, source_target_pairs={{0,12},{4,8},{8,4},{12,0},{16,28},{20,24},{24,20},{28,16},{1,13},{... | collective-permute-start | bytes 589832 | tf_op jit(solution)/shard_map/ppermute | solution.py:435
  81.7 0.1 choose.1
  81.8 1.1 %collective-permute-start.30 = (bf16[96,512]{1,0:T(8,128)(2,1)S(1)}, bf16[96,512]{1,0:T(8,128)(2,1)S(1)}, u32[]{:S(2)}, u32[]{:S(2)}) collective-permute-start(bf16[96,512]{1,0:T(8,128)(2,1)S(1)} %get-tuple-element.62), channel_id=1, source_target_pairs={{0,4},{4,0},{8,12},{12,8},{16,20},{20,16},{24,28},{28,24},{1,5},{5... | collective-permute-start | bytes 294920 | tf_op jit(solution)/shard_map/ppermute | solution.py:435
  82.9 2.1 %collective-permute-done.28.refs_7_ = bf16[96,512]{1,0:T(8,128)(2,1)S(1)} collective-permute-done((bf16[96,512]{1,0:T(8,128)(2,1)S(1)}, bf16[96,512]{1,0:T(8,128)(2,1)S(1)}, u32[]{:S(2)}, u32[]{:S(2)}) %collective-permute-start.28) | collective-permute-done | bytes 98336 | tf_op jit(solution)/shard_map/ppermute | solution.py:435
  85.0 1.1 %collective-permute-start.31 = (bf16[96,512]{1,0:T(8,128)(2,1)S(1)}, bf16[96,512]{1,0:T(8,128)(2,1)S(1)}, u32[]{:S(2)}, u32[]{:S(2)}) collective-permute-start(bf16[96,512]{1,0:T(8,128)(2,1)S(1)} %get-tuple-element.63), channel_id=1, source_target_pairs={{0,8},{4,12},{8,0},{12,4},{16,24},{20,28},{24,16},{28,20},{1,9},{5... | collective-permute-start | bytes 294920 | tf_op jit(solution)/shard_map/ppermute | solution.py:435
  86.2 1.4 %collective-permute-start.32 = (bf16[96,512]{1,0:T(8,128)(2,1)S(1)}, bf16[96,512]{1,0:T(8,128)(2,1)S(1)}, u32[]{:S(2)}, u32[]{:S(2)}) collective-permute-start(bf16[96,512]{1,0:T(8,128)(2,1)S(1)} %get-tuple-element.64), channel_id=1, source_target_pairs={{0,12},{4,8},{8,4},{12,0},{16,28},{20,24},{24,20},{28,16},{1,13},{... | collective-permute-start | bytes 294920 | tf_op jit(solution)/shard_map/ppermute | solution.py:435
  87.5 1.5 %combine.1 = bf16[192,4096]{1,0:T(8,128)(2,1)} custom-call(f32[24,192]{1,0:T(8,128)S(1)} %copy-done.6, bf16[24,4096]{1,0:T(8,128)(2,1)S(1)} %get-tuple-element.41.refs_1_, bf16[24,4096]{1,0:T(8,128)(2,1)S(1)} %collective-permute-done.6.refs_2_, bf16[24,4096]{1,0:T(8,128)(2,1)S(1)} %collective-permute-done.7.refs_3_, ...), custom_call_target="tpu_custom_call" | custom-call | flops 37748736 | bytes 25165824 | tf_op jit(solution)/shard_map/combine/pallas_call | solution.py:390
  89.0 1.3 %update.1 = (f32[2,192,512]{2,1,0:T(8,128)}, f32[2,192,512]{2,1,0:T(8,128)}) custom-call(f32[2,192,512]{2,1,0:T(8,128)S(1)} %get-tuple-element.65.summed, f32[2,192,512]{2,1,0:T(8,128)S(1)} %copy-done.2, f32[2,192,512]{2,1,0:T(8,128)S(1)} %copy-done.3), custom_call_target="tpu_custom_call" | custom-call | flops 1572864 | bytes 25165824 | tf_op jit(solution)/shard_map/update/pallas_call | solution.py:319
  90.3 2.4 %collective-permute-done.24.refs_3_ = bf16[192,512]{1,0:T(8,128)(2,1)S(1)} collective-permute-done((bf16[192,512]{1,0:T(8,128)(2,1)S(1)}, bf16[192,512]{1,0:T(8,128)(2,1)S(1)}, u32[]{:S(2)}, u32[]{:S(2)}) %collective-permute-start.24) | collective-permute-done | bytes 196640 | tf_op jit(solution)/shard_map/ppermute | solution.py:435
  92.7 1.6 %collective-permute-done.31.refs_10_ = bf16[96,512]{1,0:T(8,128)(2,1)S(1)} collective-permute-done((bf16[96,512]{1,0:T(8,128)(2,1)S(1)}, bf16[96,512]{1,0:T(8,128)(2,1)S(1)}, u32[]{:S(2)}, u32[]{:S(2)}) %collective-permute-start.31) | collective-permute-done | bytes 98336 | tf_op jit(solution)/shard_map/ppermute | solution.py:435
  94.3 2.5 %collective-permute-done.32.refs_11_ = bf16[96,512]{1,0:T(8,128)(2,1)S(1)} collective-permute-done((bf16[96,512]{1,0:T(8,128)(2,1)S(1)}, bf16[96,512]{1,0:T(8,128)(2,1)S(1)}, u32[]{:S(2)}, u32[]{:S(2)}) %collective-permute-start.32) | collective-permute-done | bytes 98336 | tf_op jit(solution)/shard_map/ppermute | solution.py:435
  96.8 1.2 %place_blocks.1 = bf16[192,4096]{1,0:T(8,128)(2,1)} custom-call(bf16[192,512]{1,0:T(8,128)(2,1)S(1)} %get-tuple-element.52.refs_0_, bf16[192,512]{1,0:T(8,128)(2,1)S(1)} %collective-permute-done.22.refs_1_, bf16[192,512]{1,0:T(8,128)(2,1)S(1)} %collective-permute-done.23.refs_2_, bf16[192,512]{1,0:T(8,128)(2,1)S(1)} %collective-permute-done.24.refs_3_, ...), custom_call_target="tpu_custom_call" | custom-call | bytes 50331648 | tf_op jit(solution)/shard_map/place_blocks/pallas_call | solution.py:422
  (28 shorter events, 0.1 us)
Async XLA Ops:
  1.3 34.0 %copy-start.1 = (bf16[1,4096,192]{1,2,0:T(8,128)(2,1)S(1)}, bf16[1,4096,192]{1,2,0:T(8,128)(2,1)}, u32[]{:S(2)}) copy-start(bf16[1,4096,192]{1,2,0:T(8,128)(2,1)} %param.15) | copy-start | bytes 4718596
  3.9 20.6 %copy-start.5 = (bf16[24,4096]{1,0:T(8,128)(2,1)S(1)}, bf16[24,4096]{1,0:T(8,128)(2,1)}, u32[]{:S(2)}) copy-start(bf16[24,4096]{1,0:T(8,128)(2,1)} %get-tuple-element.38.refs_0_) | copy-start | bytes 589828
  3.9 31.4 %copy-start = (bf16[1,4096,192]{1,2,0:T(8,128)(2,1)S(1)}, bf16[1,4096,192]{1,2,0:T(8,128)(2,1)}, u32[]{:S(2)}) copy-start(bf16[1,4096,192]{1,2,0:T(8,128)(2,1)} %param.14) | copy-start | bytes 4718596
  4.0 0.9 copy-start.6
  6.6 5.7 %collective-permute-start.16 = (bf16[2,24,512]{2,1,0:T(8,128)(2,1)S(1)}, bf16[2,24,512]{2,1,0:T(8,128)(2,1)S(1)}, u32[]{:S(2)}, u32[]{:S(2)}) collective-permute-start(bf16[2,24,512]{2,1,0:T(8,128)(2,1)S(1)} %get-tuple-element.47), channel_id=1, source_target_pairs={{0,8},{4,12},{8,0},{12,4},{16,24},{20,28},{24,16},{28,20},{1,9},{5... | collective-permute-start | bytes 147464 | tf_op jit(solution)/shard_map/ppermute | solution.py:435
  9.7 5.9 %collective-permute-start.17 = (bf16[2,24,512]{2,1,0:T(8,128)(2,1)S(1)}, bf16[2,24,512]{2,1,0:T(8,128)(2,1)S(1)}, u32[]{:S(2)}, u32[]{:S(2)}) collective-permute-start(bf16[2,24,512]{2,1,0:T(8,128)(2,1)S(1)} %get-tuple-element.48), channel_id=1, source_target_pairs={{0,16},{4,20},{8,24},{12,28},{16,0},{20,4},{24,8},{28,12},{1,17},{... | collective-permute-start | bytes 147464 | tf_op jit(solution)/shard_map/ppermute | solution.py:435
  12.3 5.9 %collective-permute-start.18 = (bf16[2,24,512]{2,1,0:T(8,128)(2,1)S(1)}, bf16[2,24,512]{2,1,0:T(8,128)(2,1)S(1)}, u32[]{:S(2)}, u32[]{:S(2)}) collective-permute-start(bf16[2,24,512]{2,1,0:T(8,128)(2,1)S(1)} %get-tuple-element.49), channel_id=1, source_target_pairs={{0,24},{4,28},{8,16},{12,20},{16,8},{20,12},{24,0},{28,4},{1,25},{... | collective-permute-start | bytes 147464 | tf_op jit(solution)/shard_map/ppermute | solution.py:435
  18.2 4.7 %collective-permute-start.19 = (bf16[4,24,512]{2,1,0:T(8,128)(2,1)S(1)}, bf16[4,24,512]{2,1,0:T(8,128)(2,1)S(1)}, u32[]{:S(2)}, u32[]{:S(2)}) collective-permute-start(bf16[4,24,512]{2,1,0:T(8,128)(2,1)S(1)} %get-tuple-element.51), channel_id=1, source_target_pairs={{0,4},{4,0},{8,12},{12,8},{16,20},{20,16},{24,28},{28,24},{1,5},{5... | collective-permute-start | bytes 294920 | tf_op jit(solution)/shard_map/ppermute | solution.py:435
  22.9 7.8 %collective-permute-start.20 = (bf16[8,24,512]{2,1,0:T(8,128)(2,1)S(1)}, bf16[8,24,512]{2,1,0:T(8,128)(2,1)S(1)}, u32[]{:S(2)}, u32[]{:S(2)}) collective-permute-start(bf16[8,24,512]{2,1,0:T(8,128)(2,1)S(1)} %join.2.one), channel_id=1, source_target_pairs={{0,2},{1,3},{2,0},{3,1},{4,6},{5,7},{6,4},{7,5},{8,10},{9,11},{10,... | collective-permute-start | bytes 589832 | tf_op jit(solution)/shard_map/ppermute | solution.py:435
  24.5 8.7 %collective-permute-start.4 = (bf16[24,4096]{1,0:T(8,128)(2,1)S(1)}, bf16[24,4096]{1,0:T(8,128)(2,1)S(1)}, u32[]{:S(2)}, u32[]{:S(2)}) collective-permute-start(bf16[24,4096]{1,0:T(8,128)(2,1)S(1)} %copy-done.5), channel_id=1, source_target_pairs={{0,2},{1,3},{2,0},{3,1},{4,6},{5,7},{6,4},{7,5},{8,10},{9,11},{10,... | collective-permute-start | bytes 589832 | tf_op jit(solution)/shard_map/ppermute | solution.py:435
  25.0 10.3 %collective-permute-start.1 = (bf16[24,4096]{1,0:T(8,128)(2,1)S(1)}, bf16[24,4096]{1,0:T(8,128)(2,1)S(1)}, u32[]{:S(2)}, u32[]{:S(2)}) collective-permute-start(bf16[24,4096]{1,0:T(8,128)(2,1)S(1)} %get-tuple-element.37.refs_0_), channel_id=1, source_target_pairs={{0,2},{1,3},{2,0},{3,1},{4,6},{5,7},{6,4},{7,5},{8,10},{9,11},{10,... | collective-permute-start | bytes 589832 | tf_op jit(solution)/shard_map/ppermute | solution.py:435
  30.8 24.2 %collective-permute-start.21 = (bf16[16,24,512]{2,1,0:T(8,128)(2,1)S(1)}, bf16[16,24,512]{2,1,0:T(8,128)(2,1)S(1)}, u32[]{:S(2)}, u32[]{:S(2)}) collective-permute-start(bf16[16,24,512]{2,1,0:T(8,128)(2,1)S(1)} %join.3.refs_8_), channel_id=1, source_target_pairs={{0,1},{1,0},{2,3},{3,2},{4,5},{5,4},{6,7},{7,6},{8,9},{9,8},{10,11... | collective-permute-start | bytes 1179656 | tf_op jit(solution)/shard_map/ppermute | solution.py:435
  30.9 4.4 %collective-permute-start.3 = (bf16[24,4096]{1,0:T(8,128)(2,1)S(1)}, bf16[24,4096]{1,0:T(8,128)(2,1)S(1)}, u32[]{:S(2)}, u32[]{:S(2)}) collective-permute-start(bf16[24,4096]{1,0:T(8,128)(2,1)S(1)} %copy-done.5), channel_id=1, source_target_pairs={{0,1},{1,0},{2,3},{3,2},{4,5},{5,4},{6,7},{7,6},{8,9},{9,8},{10,11... | collective-permute-start | bytes 589832 | tf_op jit(solution)/shard_map/ppermute | solution.py:435
  33.2 2.1 %collective-permute-start.5 = (bf16[24,4096]{1,0:T(8,128)(2,1)S(1)}, bf16[24,4096]{1,0:T(8,128)(2,1)S(1)}, u32[]{:S(2)}, u32[]{:S(2)}) collective-permute-start(bf16[24,4096]{1,0:T(8,128)(2,1)S(1)} %collective-permute-done.4.refs_2_), channel_id=1, source_target_pairs={{0,1},{1,0},{2,3},{3,2},{4,5},{5,4},{6,7},{7,6},{8,9},{9,8},{10,11... | collective-permute-start | bytes 589832 | tf_op jit(solution)/shard_map/ppermute | solution.py:435
  33.2 8.2 %collective-permute-start = (bf16[24,4096]{1,0:T(8,128)(2,1)S(1)}, bf16[24,4096]{1,0:T(8,128)(2,1)S(1)}, u32[]{:S(2)}, u32[]{:S(2)}) collective-permute-start(bf16[24,4096]{1,0:T(8,128)(2,1)S(1)} %get-tuple-element.37.refs_0_), channel_id=1, source_target_pairs={{0,1},{1,0},{2,3},{3,2},{4,5},{5,4},{6,7},{7,6},{8,9},{9,8},{10,11... | collective-permute-start | bytes 589832 | tf_op jit(solution)/shard_map/ppermute | solution.py:435
  35.3 6.1 %collective-permute-start.2 = (bf16[24,4096]{1,0:T(8,128)(2,1)S(1)}, bf16[24,4096]{1,0:T(8,128)(2,1)S(1)}, u32[]{:S(2)}, u32[]{:S(2)}) collective-permute-start(bf16[24,4096]{1,0:T(8,128)(2,1)S(1)} %collective-permute-done.1.refs_2_), channel_id=1, source_target_pairs={{0,1},{1,0},{2,3},{3,2},{4,5},{5,4},{6,7},{7,6},{8,9},{9,8},{10,11... | collective-permute-start | bytes 589832 | tf_op jit(solution)/shard_map/ppermute | solution.py:435
  35.3 8.9 %copy-start.4 = (bf16[1,192,4096]{2,1,0:T(8,128)(2,1)S(1)}, bf16[1,192,4096]{2,1,0:T(8,128)(2,1)}, u32[]{:S(2)}) copy-start(bf16[1,192,4096]{2,1,0:T(8,128)(2,1)} %param.16) | copy-start | bytes 4718596
  36.5 7.7 %collective-permute-start.15 = (bf16[112,192]{1,0:T(8,128)(2,1)S(1)}, bf16[112,192]{1,0:T(8,128)(2,1)S(1)}, u32[]{:S(2)}, u32[]{:S(2)}) collective-permute-start(bf16[112,192]{1,0:T(8,128)(2,1)S(1)} %get-tuple-element.45.refs_0_), channel_id=1, source_target_pairs={{0,28},{4,24},{8,20},{12,16},{16,12},{20,8},{24,4},{28,0},{1,29},{... | collective-permute-start | bytes 129032 | tf_op jit(solution)/shard_map/ppermute | solution.py:435
  38.3 7.8 %collective-permute-start.14 = (bf16[112,192]{1,0:T(8,128)(2,1)S(1)}, bf16[112,192]{1,0:T(8,128)(2,1)S(1)}, u32[]{:S(2)}, u32[]{:S(2)}) collective-permute-start(bf16[112,192]{1,0:T(8,128)(2,1)S(1)} %get-tuple-element.45.refs_0_), channel_id=1, source_target_pairs={{0,24},{4,28},{8,16},{12,20},{16,8},{20,12},{24,0},{28,4},{1,25},{... | collective-permute-start | bytes 129032 | tf_op jit(solution)/shard_map/ppermute | solution.py:435
  41.4 7.3 %collective-permute-start.13 = (bf16[112,192]{1,0:T(8,128)(2,1)S(1)}, bf16[112,192]{1,0:T(8,128)(2,1)S(1)}, u32[]{:S(2)}, u32[]{:S(2)}) collective-permute-start(bf16[112,192]{1,0:T(8,128)(2,1)S(1)} %get-tuple-element.45.refs_0_), channel_id=1, source_target_pairs={{0,20},{4,16},{8,28},{12,24},{16,4},{20,0},{24,12},{28,8},{1,21},{... | collective-permute-start | bytes 129032 | tf_op jit(solution)/shard_map/ppermute | solution.py:435
  41.4 8.8 %collective-permute-start.12 = (bf16[112,192]{1,0:T(8,128)(2,1)S(1)}, bf16[112,192]{1,0:T(8,128)(2,1)S(1)}, u32[]{:S(2)}, u32[]{:S(2)}) collective-permute-start(bf16[112,192]{1,0:T(8,128)(2,1)S(1)} %get-tuple-element.45.refs_0_), channel_id=1, source_target_pairs={{0,16},{4,20},{8,24},{12,28},{16,0},{20,4},{24,8},{28,12},{1,17},{... | collective-permute-start | bytes 129032 | tf_op jit(solution)/shard_map/ppermute | solution.py:435
  44.2 6.6 %collective-permute-start.11 = (bf16[112,192]{1,0:T(8,128)(2,1)S(1)}, bf16[112,192]{1,0:T(8,128)(2,1)S(1)}, u32[]{:S(2)}, u32[]{:S(2)}) collective-permute-start(bf16[112,192]{1,0:T(8,128)(2,1)S(1)} %get-tuple-element.45.refs_0_), channel_id=1, source_target_pairs={{0,12},{4,8},{8,4},{12,0},{16,28},{20,24},{24,20},{28,16},{1,13},{... | collective-permute-start | bytes 129032 | tf_op jit(solution)/shard_map/ppermute | solution.py:435
  44.2 10.7 %copy-start.2 = (f32[2,192,512]{2,1,0:T(8,128)S(1)}, f32[2,192,512]{2,1,0:T(8,128)}, u32[]{:S(2)}) copy-start(f32[2,192,512]{2,1,0:T(8,128)} %first.1) | copy-start | bytes 2359300
  44.3 10.7 %copy-start.3 = (f32[2,192,512]{2,1,0:T(8,128)S(1)}, f32[2,192,512]{2,1,0:T(8,128)}, u32[]{:S(2)}) copy-start(f32[2,192,512]{2,1,0:T(8,128)} %second.1) | copy-start | bytes 2359300
  46.2 12.9 %collective-permute-start.6 = (bf16[24,4096]{1,0:T(8,128)(2,1)S(1)}, bf16[24,4096]{1,0:T(8,128)(2,1)S(1)}, u32[]{:S(2)}, u32[]{:S(2)}) collective-permute-start(bf16[24,4096]{1,0:T(8,128)(2,1)S(1)} %get-tuple-element.42), channel_id=1, source_target_pairs={{0,1},{1,0},{2,3},{3,2},{4,5},{5,4},{6,7},{7,6},{8,9},{9,8},{10,11... | collective-permute-start | bytes 589832 | tf_op jit(solution)/shard_map/ppermute | solution.py:435
  48.7 13.5 %collective-permute-start.7 = (bf16[24,4096]{1,0:T(8,128)(2,1)S(1)}, bf16[24,4096]{1,0:T(8,128)(2,1)S(1)}, u32[]{:S(2)}, u32[]{:S(2)}) collective-permute-start(bf16[24,4096]{1,0:T(8,128)(2,1)S(1)} %get-tuple-element.43), channel_id=1, source_target_pairs={{0,2},{1,3},{2,0},{3,1},{4,6},{5,7},{6,4},{7,5},{8,10},{9,11},{10,... | collective-permute-start | bytes 589832 | tf_op jit(solution)/shard_map/ppermute | solution.py:435
  50.2 4.2 %collective-permute-start.10 = (bf16[112,192]{1,0:T(8,128)(2,1)S(1)}, bf16[112,192]{1,0:T(8,128)(2,1)S(1)}, u32[]{:S(2)}, u32[]{:S(2)}) collective-permute-start(bf16[112,192]{1,0:T(8,128)(2,1)S(1)} %get-tuple-element.45.refs_0_), channel_id=1, source_target_pairs={{0,8},{4,12},{8,0},{12,4},{16,24},{20,28},{24,16},{28,20},{1,9},{5... | collective-permute-start | bytes 129032 | tf_op jit(solution)/shard_map/ppermute | solution.py:435
  50.8 4.2 %collective-permute-start.9 = (bf16[112,192]{1,0:T(8,128)(2,1)S(1)}, bf16[112,192]{1,0:T(8,128)(2,1)S(1)}, u32[]{:S(2)}, u32[]{:S(2)}) collective-permute-start(bf16[112,192]{1,0:T(8,128)(2,1)S(1)} %get-tuple-element.45.refs_0_), channel_id=1, source_target_pairs={{0,4},{4,0},{8,12},{12,8},{16,20},{20,16},{24,28},{28,24},{1,5},{5... | collective-permute-start | bytes 129032 | tf_op jit(solution)/shard_map/ppermute | solution.py:435
  54.4 7.8 %collective-permute-start.8 = (bf16[24,4096]{1,0:T(8,128)(2,1)S(1)}, bf16[24,4096]{1,0:T(8,128)(2,1)S(1)}, u32[]{:S(2)}, u32[]{:S(2)}) collective-permute-start(bf16[24,4096]{1,0:T(8,128)(2,1)S(1)} %get-tuple-element.44), channel_id=1, source_target_pairs={{0,3},{1,2},{2,1},{3,0},{4,7},{5,6},{6,5},{7,4},{8,11},{9,10},{10,... | collective-permute-start | bytes 589832 | tf_op jit(solution)/shard_map/ppermute | solution.py:435
  56.0 23.2 %collective-permute-start.29 = (bf16[2,96,512]{2,1,0:T(8,128)(2,1)S(1)}, bf16[2,96,512]{2,1,0:T(8,128)(2,1)S(1)}, u32[]{:S(2)}, u32[]{:S(2)}) collective-permute-start(bf16[2,96,512]{2,1,0:T(8,128)(2,1)S(1)} %get-tuple-element.60), channel_id=1, source_target_pairs={{0,16},{4,20},{8,24},{12,28},{16,0},{20,4},{24,8},{28,12},{1,17},{... | collective-permute-start | bytes 589832 | tf_op jit(solution)/shard_map/ppermute | solution.py:435
  57.8 18.8 %collective-permute-start.25 = (bf16[96,512]{1,0:T(8,128)(2,1)S(1)}, bf16[96,512]{1,0:T(8,128)(2,1)S(1)}, u32[]{:S(2)}, u32[]{:S(2)}) collective-permute-start(bf16[96,512]{1,0:T(8,128)(2,1)S(1)} %get-tuple-element.56), channel_id=1, source_target_pairs={{0,16},{4,20},{8,24},{12,28},{16,0},{20,4},{24,8},{28,12},{1,17},{... | collective-permute-start | bytes 294920 | tf_op jit(solution)/shard_map/ppermute | solution.py:435
  59.0 20.2 %collective-permute-start.26 = (bf16[96,512]{1,0:T(8,128)(2,1)S(1)}, bf16[96,512]{1,0:T(8,128)(2,1)S(1)}, u32[]{:S(2)}, u32[]{:S(2)}) collective-permute-start(bf16[96,512]{1,0:T(8,128)(2,1)S(1)} %get-tuple-element.57), channel_id=1, source_target_pairs={{0,20},{4,16},{8,28},{12,24},{16,4},{20,0},{24,12},{28,8},{1,21},{... | collective-permute-start | bytes 294920 | tf_op jit(solution)/shard_map/ppermute | solution.py:435
  62.2 24.0 %collective-permute-start.22 = (bf16[192,512]{1,0:T(8,128)(2,1)S(1)}, bf16[192,512]{1,0:T(8,128)(2,1)S(1)}, u32[]{:S(2)}, u32[]{:S(2)}) collective-permute-start(bf16[192,512]{1,0:T(8,128)(2,1)S(1)} %get-tuple-element.53), channel_id=1, source_target_pairs={{0,4},{4,0},{8,12},{12,8},{16,20},{20,16},{24,28},{28,24},{1,5},{5... | collective-permute-start | bytes 589832 | tf_op jit(solution)/shard_map/ppermute | solution.py:435
  62.2 19.6 %collective-permute-start.27 = (bf16[96,512]{1,0:T(8,128)(2,1)S(1)}, bf16[96,512]{1,0:T(8,128)(2,1)S(1)}, u32[]{:S(2)}, u32[]{:S(2)}) collective-permute-start(bf16[96,512]{1,0:T(8,128)(2,1)S(1)} %get-tuple-element.58), channel_id=1, source_target_pairs={{0,24},{4,28},{8,16},{12,20},{16,8},{20,12},{24,0},{28,4},{1,25},{... | collective-permute-start | bytes 294920 | tf_op jit(solution)/shard_map/ppermute | solution.py:435
  76.6 8.4 %collective-permute-start.28 = (bf16[96,512]{1,0:T(8,128)(2,1)S(1)}, bf16[96,512]{1,0:T(8,128)(2,1)S(1)}, u32[]{:S(2)}, u32[]{:S(2)}) collective-permute-start(bf16[96,512]{1,0:T(8,128)(2,1)S(1)} %get-tuple-element.59), channel_id=1, source_target_pairs={{0,28},{4,24},{8,20},{12,16},{16,12},{20,8},{24,4},{28,0},{1,29},{... | collective-permute-start | bytes 294920 | tf_op jit(solution)/shard_map/ppermute | solution.py:435
  79.2 11.1 %collective-permute-start.23 = (bf16[192,512]{1,0:T(8,128)(2,1)S(1)}, bf16[192,512]{1,0:T(8,128)(2,1)S(1)}, u32[]{:S(2)}, u32[]{:S(2)}) collective-permute-start(bf16[192,512]{1,0:T(8,128)(2,1)S(1)} %get-tuple-element.54), channel_id=1, source_target_pairs={{0,8},{4,12},{8,0},{12,4},{16,24},{20,28},{24,16},{28,20},{1,9},{5... | collective-permute-start | bytes 589832 | tf_op jit(solution)/shard_map/ppermute | solution.py:435
  79.2 13.5 %collective-permute-start.24 = (bf16[192,512]{1,0:T(8,128)(2,1)S(1)}, bf16[192,512]{1,0:T(8,128)(2,1)S(1)}, u32[]{:S(2)}, u32[]{:S(2)}) collective-permute-start(bf16[192,512]{1,0:T(8,128)(2,1)S(1)} %get-tuple-element.55), channel_id=1, source_target_pairs={{0,12},{4,8},{8,4},{12,0},{16,28},{20,24},{24,20},{28,16},{1,13},{... | collective-permute-start | bytes 589832 | tf_op jit(solution)/shard_map/ppermute | solution.py:435
  81.8 10.9 %collective-permute-start.30 = (bf16[96,512]{1,0:T(8,128)(2,1)S(1)}, bf16[96,512]{1,0:T(8,128)(2,1)S(1)}, u32[]{:S(2)}, u32[]{:S(2)}) collective-permute-start(bf16[96,512]{1,0:T(8,128)(2,1)S(1)} %get-tuple-element.62), channel_id=1, source_target_pairs={{0,4},{4,0},{8,12},{12,8},{16,20},{20,16},{24,28},{28,24},{1,5},{5... | collective-permute-start | bytes 294920 | tf_op jit(solution)/shard_map/ppermute | solution.py:435
  85.0 9.3 %collective-permute-start.31 = (bf16[96,512]{1,0:T(8,128)(2,1)S(1)}, bf16[96,512]{1,0:T(8,128)(2,1)S(1)}, u32[]{:S(2)}, u32[]{:S(2)}) collective-permute-start(bf16[96,512]{1,0:T(8,128)(2,1)S(1)} %get-tuple-element.63), channel_id=1, source_target_pairs={{0,8},{4,12},{8,0},{12,4},{16,24},{20,28},{24,16},{28,20},{1,9},{5... | collective-permute-start | bytes 294920 | tf_op jit(solution)/shard_map/ppermute | solution.py:435
  86.2 10.7 %collective-permute-start.32 = (bf16[96,512]{1,0:T(8,128)(2,1)S(1)}, bf16[96,512]{1,0:T(8,128)(2,1)S(1)}, u32[]{:S(2)}, u32[]{:S(2)}) collective-permute-start(bf16[96,512]{1,0:T(8,128)(2,1)S(1)} %get-tuple-element.64), channel_id=1, source_target_pairs={{0,12},{4,8},{8,4},{12,0},{16,28},{20,24},{24,20},{28,16},{1,13},{... | collective-permute-start | bytes 294920 | tf_op jit(solution)/shard_map/ppermute | solution.py:435

commit v3 on v2

--- a/solution.py
+++ b/solution.py
@@ -163,6 +163,23 @@
     )(*pairs)
 
 
+def pile_kernel(count, *refs):
+    for number in range(count):
+        refs[count][number] = refs[number][...]
+
+
+def pile(blocks):
+    return pl.pallas_call(
+        functools.partial(pile_kernel, len(blocks)),
+        in_specs=[LOCAL] * len(blocks),
+        out_specs=LOCAL,
+        out_shape=jax.ShapeDtypeStruct((len(blocks),) + blocks[0].shape, BF16),
+        compiler_params=PARAMS,
+        cost_estimate=cost(0, 4 * len(blocks) * blocks[0].size),
+        name="pile",
+    )(*blocks)
+
+
 def join_kernel(one, two, out):
     count = one.shape[0]
     out[0:count] = one[...]
@@ -215,7 +232,7 @@
 
 def adam_kernel(groups, parts, *refs):
     half = groups // 2
-    hiddens, refs = refs[:groups], refs[groups:]
+    hiddens, refs = [refs[p % 2].at[p // 2] for p in range(groups)], refs[2:]
     near, other, first, second, summed = refs[:5]
     dirs = refs[5:]
     count = parts * CAP
@@ -258,14 +275,14 @@
 
 
 def adam(hiddens, blocks, first, second):
-    groups = len(hiddens)
+    groups = 2 * hiddens[0].shape[0]
     parts = 2 * blocks[0].shape[0] // groups
     units, columns = first.shape[1:]
     split = units // 2
     rows = groups * parts * CAP
     return pl.pallas_call(
         functools.partial(adam_kernel, groups, parts),
-        in_specs=[LOCAL] * (groups + 4),
+        in_specs=[LOCAL] * 6,
         out_specs=[LOCAL] * (2 + groups),
         out_shape=[jax.ShapeDtypeStruct(first.shape, F32)]
         + [jax.ShapeDtypeStruct((units, columns), BF16)] * (groups // 2)
@@ -278,7 +295,7 @@
 
 
 def choose_kernel(half, *refs):
-    hiddens, both, outs = refs[:half], refs[half], refs[half + 1 :]
+    hiddens, both, outs = [refs[p % 2].at[p // 2] for p in range(half)], refs[2], refs[3:]
     for peer in range(half):
         count = hiddens[peer].shape[0] - TAG
         tag = hiddens[peer][count : count + TAG, :].astype(F32)[0:1, 0:1]
@@ -289,10 +306,10 @@
 
 
 def choose(hiddens, both):
-    half = len(hiddens)
+    half = hiddens[0].shape[0]
     return pl.pallas_call(
         functools.partial(choose_kernel, half),
-        in_specs=[LOCAL] * (half + 1),
+        in_specs=[LOCAL] * 3,
         out_specs=[LOCAL] * half,
         out_shape=[jax.ShapeDtypeStruct(both.shape[1:], BF16)] * half,
         compiler_params=PARAMS,
@@ -505,11 +522,15 @@
     if slots > 1:
         my_cand = lax.dynamic_index_in_dim(placement, slot_of(0), 1, keepdims=True)
     pre_gate, pre_up, hidden = forward(my_cand, in_rows, w_gate, w_up)
-    hiddens = exchange([hidden] * groups)
+    hiddens = [hidden]
+    for bits in range(2, groups, 2):
+        hiddens.append(swap(hidden, "grp", groups, bits))
+    hiddens = pile(hiddens)
+    hiddens = (hiddens, swap(hiddens, "grp", groups, 1))
     summed, *dirs, both = adam(hiddens, columns, moment_first, moment_second)
     got_dirs = exchange(dirs)
     both = swap(both, "grp", groups, groups // 2)
-    dirs = choose(hiddens[: groups // 2], both)
+    dirs = choose(hiddens, both)
     got_dirs = got_dirs + exchange(dirs)
     new_first, new_second = update(summed, moment_first, moment_second)
 

time: 98.3 us -> 93.4 us (0.950)
  starting transfers between devices: 40.1 us -> 28.6 us
  waiting for transfers between devices: 43 us -> 49.5 us
    ppermute x33 -> x30, starting transfers between devices: 40.1 us -> 28.6 us  [swap(): return lax.ppermute(value, axis, [(i, i ^ bits) for i in range(size)])]
    ppermute x33 -> x30, waiting for transfers between devices: 43 us -> 49.5 us  [swap(): return lax.ppermute(value, axis, [(i, i ^ bits) for i in range(size)])]
  transfers between devices with their start and end apart: 33 -> 30, of which waited for: 15 -> 18; matrix products, arithmetic and copies ran while one was open for 0% -> 0% of each run, Pallas kernels for 7% -> 8%
where the time goes in v3:
time: 93.4 us; the launch traced here: 93.2 us
  waiting for transfers between devices  49.5 us (53%)
  starting transfers between devices  28.6 us (31%)
  Pallas kernels  12.7 us (14%)
  between operations  1.5 us (2%)
    ppermute x30, waiting for transfers between devices, swap(): return lax.ppermute(value, axis, [(i, i ^ bits) for i in range(size)])  49.5 us
    ppermute x30, starting transfers between devices, swap(): return lax.ppermute(value, axis, [(i, i ^ bits) for i in range(size)])  28.6 us
    pallas_call x1, Pallas kernels, select(): pl.pallas_call(functools.partial(select_kernel, slots, pieces), in_specs=...  2.63 us
    pallas_call x1, Pallas kernels, backward(): pl.pallas_call(functools.partial(backward_kernel, parts), in_specs=[LOCAL...  1.9 us
  transfers between devices with their start and end apart: 30, of which 18 were waited for; matrix products, arithmetic and copies ran while one was open for 0% of the time, Pallas kernels for 8%

profile of v3, /device:TPU:0, one launch (start us, length us, event | category | flops | bytes accessed | tf_op | source)
XLA Modules:
  0.0 93.2 jit_solution(12856304501442079433)
XLA Ops:
  1.3 2.6 %select_rows.1 = (bf16[24,4096]{1,0:T(8,128)(2,1)}, f32[24,192]{1,0:T(8,128)}) custom-call(s32[1,1]{1,0:T(1,128)S(6)} %copy.14.place, s32[8,192]{1,0:T(8,128)} %bitcast.16, f32[8,192]{1,0:T(8,128)} %bitcast.17, bf16[192,4096]{1,0:T(8,128)(2,1)} %tokens.1), custom_call_target="tpu_custom_call" | custom-call | flops 37748736 | bytes 25165824 | tf_op jit(solution)/shard_map/select_rows/pallas_call | solution.py:85
  3.9 0.0 copy-start.5
  3.9 0.0 copy-start
  4.0 0.0 copy-start.6
  4.0 0.9 copy-done.6
  4.8 1.8 %scale_rows.1 = (bf16[24,4096]{1,0:T(8,128)(2,1)S(1)}, bf16[2,24,512]{2,1,0:T(8,128)(2,1)S(1)}, bf16[2,24,512]{2,1,0:T(8,128)(2,1)S(1)}, bf16[2,24,512]{2,1,0:T(8,128)(2,1)S(1)}, bf16[2,24,512]{2,1,0:T(8,128)(2,1)S(1)}) custom-call(f32[24,192]{1,0:T(8,128)S(1)} %copy-done.6, bf16[192,4096]{1,0:T(8,128)(2,1)} %grads.1), custom_call_target="tpu_custom_call" | custom-call | flops 37748736 | bytes 100663296 | tf_op jit(solution)/shard_map/scale_rows/pallas_call | solution.py:134
  6.6 3.1 %collective-permute-start.13 = (bf16[2,24,512]{2,1,0:T(8,128)(2,1)S(1)}, bf16[2,24,512]{2,1,0:T(8,128)(2,1)S(1)}, u32[]{:S(2)}, u32[]{:S(2)}) collective-permute-start(bf16[2,24,512]{2,1,0:T(8,128)(2,1)S(1)} %get-tuple-element.47), channel_id=1, source_target_pairs={{0,8},{4,12},{8,0},{12,4},{16,24},{20,28},{24,16},{28,20},{1,9},{5... | collective-permute-start | bytes 147464 | tf_op jit(solution)/shard_map/ppermute | solution.py:452
  9.7 2.6 %collective-permute-start.14 = (bf16[2,24,512]{2,1,0:T(8,128)(2,1)S(1)}, bf16[2,24,512]{2,1,0:T(8,128)(2,1)S(1)}, u32[]{:S(2)}, u32[]{:S(2)}) collective-permute-start(bf16[2,24,512]{2,1,0:T(8,128)(2,1)S(1)} %get-tuple-element.48), channel_id=1, source_target_pairs={{0,16},{4,20},{8,24},{12,28},{16,0},{20,4},{24,8},{28,12},{1,17},{... | collective-permute-start | bytes 147464 | tf_op jit(solution)/shard_map/ppermute | solution.py:452
  12.3 0.0 collective-permute-start.15
  12.3 3.3 %collective-permute-done.14.refs_2_ = bf16[2,24,512]{2,1,0:T(8,128)(2,1)S(1)} collective-permute-done((bf16[2,24,512]{2,1,0:T(8,128)(2,1)S(1)}, bf16[2,24,512]{2,1,0:T(8,128)(2,1)S(1)}, u32[]{:S(2)}, u32[]{:S(2)}) %collective-permute-start.14) | collective-permute-done | bytes 49184 | tf_op jit(solution)/shard_map/ppermute | solution.py:452
  15.7 2.6 %collective-permute-done.15.refs_3_ = bf16[2,24,512]{2,1,0:T(8,128)(2,1)S(1)} collective-permute-done((bf16[2,24,512]{2,1,0:T(8,128)(2,1)S(1)}, bf16[2,24,512]{2,1,0:T(8,128)(2,1)S(1)}, u32[]{:S(2)}, u32[]{:S(2)}) %collective-permute-start.15) | collective-permute-done | bytes 49184 | tf_op jit(solution)/shard_map/ppermute | solution.py:452
  18.2 1.6 %collective-permute-start.16 = (bf16[4,24,512]{2,1,0:T(8,128)(2,1)S(1)}, bf16[4,24,512]{2,1,0:T(8,128)(2,1)S(1)}, u32[]{:S(2)}, u32[]{:S(2)}) collective-permute-start(bf16[4,24,512]{2,1,0:T(8,128)(2,1)S(1)} %get-tuple-element.51), channel_id=1, source_target_pairs={{0,4},{4,0},{8,12},{12,8},{16,20},{20,16},{24,28},{28,24},{1,5},{5... | collective-permute-start | bytes 294920 | tf_op jit(solution)/shard_map/ppermute | solution.py:452
  19.8 1.5 %collective-permute-start.4 = (bf16[24,4096]{1,0:T(8,128)(2,1)S(1)}, bf16[24,4096]{1,0:T(8,128)(2,1)S(1)}, u32[]{:S(2)}, u32[]{:S(2)}) collective-permute-start(bf16[24,4096]{1,0:T(8,128)(2,1)S(1)} %copy-done.5), channel_id=1, source_target_pairs={{0,2},{1,3},{2,0},{3,1},{4,6},{5,7},{6,4},{7,5},{8,10},{9,11},{10,... | collective-permute-start | bytes 589832 | tf_op jit(solution)/shard_map/ppermute | solution.py:452
  21.3 1.6 %collective-permute-done.16.two = bf16[4,24,512]{2,1,0:T(8,128)(2,1)S(1)} collective-permute-done((bf16[4,24,512]{2,1,0:T(8,128)(2,1)S(1)}, bf16[4,24,512]{2,1,0:T(8,128)(2,1)S(1)}, u32[]{:S(2)}, u32[]{:S(2)}) %collective-permute-start.16) | collective-permute-done | bytes 98336 | tf_op jit(solution)/shard_map/ppermute | solution.py:452
  22.9 1.6 %collective-permute-start.17 = (bf16[8,24,512]{2,1,0:T(8,128)(2,1)S(1)}, bf16[8,24,512]{2,1,0:T(8,128)(2,1)S(1)}, u32[]{:S(2)}, u32[]{:S(2)}) collective-permute-start(bf16[8,24,512]{2,1,0:T(8,128)(2,1)S(1)} %join.2.one), channel_id=1, source_target_pairs={{0,2},{1,3},{2,0},{3,1},{4,6},{5,7},{6,4},{7,5},{8,10},{9,11},{10,... | collective-permute-start | bytes 589832 | tf_op jit(solution)/shard_map/ppermute | solution.py:452
  24.5 0.5 collective-permute-start.1
  25.0 2.6 %collective-permute-done.4.refs_2_ = bf16[24,4096]{1,0:T(8,128)(2,1)S(1)} collective-permute-done((bf16[24,4096]{1,0:T(8,128)(2,1)S(1)}, bf16[24,4096]{1,0:T(8,128)(2,1)S(1)}, u32[]{:S(2)}, u32[]{:S(2)}) %collective-permute-start.4) | collective-permute-done | bytes 196640 | tf_op jit(solution)/shard_map/ppermute | solution.py:452
  27.6 3.5 %collective-permute-done.17.two = bf16[8,24,512]{2,1,0:T(8,128)(2,1)S(1)} collective-permute-done((bf16[8,24,512]{2,1,0:T(8,128)(2,1)S(1)}, bf16[8,24,512]{2,1,0:T(8,128)(2,1)S(1)}, u32[]{:S(2)}, u32[]{:S(2)}) %collective-permute-start.17) | collective-permute-done | bytes 196640 | tf_op jit(solution)/shard_map/ppermute | solution.py:452
  31.1 0.1 collective-permute-start.18
  31.2 0.5 collective-permute-start
  31.7 1.5 %collective-permute-done.1.refs_2_ = bf16[24,4096]{1,0:T(8,128)(2,1)S(1)} collective-permute-done((bf16[24,4096]{1,0:T(8,128)(2,1)S(1)}, bf16[24,4096]{1,0:T(8,128)(2,1)S(1)}, u32[]{:S(2)}, u32[]{:S(2)}) %collective-permute-start.1) | collective-permute-done | bytes 196640 | tf_op jit(solution)/shard_map/ppermute | solution.py:452
  33.2 0.0 copy-start.4
  33.2 1.2 %forward.1 = (f32[96,192]{1,0:T(8,128)S(1)}, f32[96,192]{1,0:T(8,128)S(1)}, bf16[112,192]{1,0:T(8,128)(2,1)S(1)}) custom-call(s32[1,1]{1,0:T(1,128)S(6)} %copy.14.place, bf16[24,4096]{1,0:T(8,128)(2,1)S(1)} %copy-done.5, bf16[24,4096]{1,0:T(8,128)(2,1)S(1)} %collective-permute-done.3.refs_1_, bf16[24,4096]{1,0:T(8,128)(2,1)S(1)} %collective-permute-done.4.refs_2_, ...), custom_call_target="tpu_custom_call" | custom-call | flops 301989888 | bytes 50331648 | tf_op jit(solution)/shard_map/forward/pallas_call | solution.py:218
  34.4 0.9 collective-permute-start.11
  35.3 0.1 collective-permute-start.10
  35.4 5.7 %collective-permute-done.11.refs_3_ = bf16[112,192]{1,0:T(8,128)(2,1)S(1)} collective-permute-done((bf16[112,192]{1,0:T(8,128)(2,1)S(1)}, bf16[112,192]{1,0:T(8,128)(2,1)S(1)}, u32[]{:S(2)}, u32[]{:S(2)}) %collective-permute-start.11) | collective-permute-done | bytes 43040 | tf_op jit(solution)/shard_map/ppermute | solution.py:452
  41.2 1.5 %collective-permute-done.10.refs_2_ = bf16[112,192]{1,0:T(8,128)(2,1)S(1)} collective-permute-done((bf16[112,192]{1,0:T(8,128)(2,1)S(1)}, bf16[112,192]{1,0:T(8,128)(2,1)S(1)}, u32[]{:S(2)}, u32[]{:S(2)}) %collective-permute-start.10) | collective-permute-done | bytes 43040 | tf_op jit(solution)/shard_map/ppermute | solution.py:452
  42.7 2.7 %collective-permute-done.9.refs_1_ = bf16[112,192]{1,0:T(8,128)(2,1)S(1)} collective-permute-done((bf16[112,192]{1,0:T(8,128)(2,1)S(1)}, bf16[112,192]{1,0:T(8,128)(2,1)S(1)}, u32[]{:S(2)}, u32[]{:S(2)}) %collective-permute-start.9) | collective-permute-done | bytes 43040 | tf_op jit(solution)/shard_map/ppermute | solution.py:452
  45.4 1.3 %collective-permute-start.12 = (bf16[4,112,192]{2,1,0:T(8,128)(2,1)S(1)}, bf16[4,112,192]{2,1,0:T(8,128)(2,1)S(1)}, u32[]{:S(2)}, u32[]{:S(2)}) collective-permute-start(bf16[4,112,192]{2,1,0:T(8,128)(2,1)S(1)} %pile.1.refs_0_), channel_id=1, source_target_pairs={{0,4},{4,0},{8,12},{12,8},{16,20},{20,16},{24,28},{28,24},{1,5},{5... | collective-permute-start | bytes 516104 | tf_op jit(solution)/shard_map/ppermute | solution.py:452
  46.7 0.0 copy-start.2
  46.7 0.0 copy-start.3
  46.7 1.9 %backward.1 = (bf16[24,4096]{1,0:T(8,128)(2,1)S(1)}, bf16[24,4096]{1,0:T(8,128)(2,1)S(1)}, bf16[24,4096]{1,0:T(8,128)(2,1)S(1)}, bf16[24,4096]{1,0:T(8,128)(2,1)S(1)}) custom-call(bf16[24,4096]{1,0:T(8,128)(2,1)S(1)} %get-tuple-element.37.refs_0_, bf16[24,4096]{1,0:T(8,128)(2,1)S(1)} %collective-permute-done.refs_1_, ...), custom_call_target="tpu_custom_call" | custom-call | flops 452984832 | bytes 75497472 | tf_op jit(solution)/shard_map/backward/pallas_call | solution.py:373
  48.6 0.1 collective-permute-start.6
  48.7 1.6 %collective-permute-start.7 = (bf16[24,4096]{1,0:T(8,128)(2,1)S(1)}, bf16[24,4096]{1,0:T(8,128)(2,1)S(1)}, u32[]{:S(2)}, u32[]{:S(2)}) collective-permute-start(bf16[24,4096]{1,0:T(8,128)(2,1)S(1)} %get-tuple-element.43), channel_id=1, source_target_pairs={{0,2},{1,3},{2,0},{3,1},{4,6},{5,7},{6,4},{7,5},{8,10},{9,11},{10,... | collective-permute-start | bytes 589832 | tf_op jit(solution)/shard_map/ppermute | solution.py:452
  50.2 0.3 collective-permute-start.8
  50.5 0.9 collective-permute-done.12.refs_1_
  51.5 1.1 %adam.1 = (f32[2,192,512]{2,1,0:T(8,128)S(1)}, bf16[192,512]{1,0:T(8,128)(2,1)S(1)}, bf16[192,512]{1,0:T(8,128)(2,1)S(1)}, bf16[192,512]{1,0:T(8,128)(2,1)S(1)},...) custom-call(bf16[4,112,192]{2,1,0:T(8,128)(2,1)S(1)} %pile.1.refs_0_, ...), custom_call_target="tpu_custom_call" | custom-call | flops 301989888 | bytes 25165824 | tf_op jit(solution)/shard_map/adam/pallas_call | solution.py:283
  52.5 0.1 collective-permute-start.26
  52.6 2.9 %collective-permute-start.22 = (bf16[96,512]{1,0:T(8,128)(2,1)S(1)}, bf16[96,512]{1,0:T(8,128)(2,1)S(1)}, u32[]{:S(2)}, u32[]{:S(2)}) collective-permute-start(bf16[96,512]{1,0:T(8,128)(2,1)S(1)} %get-tuple-element.56), channel_id=1, source_target_pairs={{0,16},{4,20},{8,24},{12,28},{16,0},{20,4},{24,8},{28,12},{1,17},{... | collective-permute-start | bytes 294920 | tf_op jit(solution)/shard_map/ppermute | solution.py:452
  55.5 0.0 collective-permute-done.6.refs_2_
  55.5 0.7 collective-permute-start.23
  56.3 0.3 collective-permute-done.7.refs_3_
  56.5 0.8 collective-permute-start.19
  57.3 2.3 %collective-permute-done.8.refs_4_ = bf16[24,4096]{1,0:T(8,128)(2,1)S(1)} collective-permute-done((bf16[24,4096]{1,0:T(8,128)(2,1)S(1)}, bf16[24,4096]{1,0:T(8,128)(2,1)S(1)}, u32[]{:S(2)}, u32[]{:S(2)}) %collective-permute-start.8) | collective-permute-done | bytes 196640 | tf_op jit(solution)/shard_map/ppermute | solution.py:452
  59.6 0.6 collective-permute-start.24
  60.3 11.6 %collective-permute-done.22.refs_4_ = bf16[96,512]{1,0:T(8,128)(2,1)S(1)} collective-permute-done((bf16[96,512]{1,0:T(8,128)(2,1)S(1)}, bf16[96,512]{1,0:T(8,128)(2,1)S(1)}, u32[]{:S(2)}, u32[]{:S(2)}) %collective-permute-start.22) | collective-permute-done | bytes 98336 | tf_op jit(solution)/shard_map/ppermute | solution.py:452
  71.9 2.0 %collective-permute-start.25 = (bf16[96,512]{1,0:T(8,128)(2,1)S(1)}, bf16[96,512]{1,0:T(8,128)(2,1)S(1)}, u32[]{:S(2)}, u32[]{:S(2)}) collective-permute-start(bf16[96,512]{1,0:T(8,128)(2,1)S(1)} %get-tuple-element.59), channel_id=1, source_target_pairs={{0,28},{4,24},{8,20},{12,16},{16,12},{20,8},{24,4},{28,0},{1,29},{... | collective-permute-start | bytes 294920 | tf_op jit(solution)/shard_map/ppermute | solution.py:452
  73.9 0.4 collective-permute-done.23.refs_5_
  74.3 2.7 %collective-permute-start.21 = (bf16[192,512]{1,0:T(8,128)(2,1)S(1)}, bf16[192,512]{1,0:T(8,128)(2,1)S(1)}, u32[]{:S(2)}, u32[]{:S(2)}) collective-permute-start(bf16[192,512]{1,0:T(8,128)(2,1)S(1)} %get-tuple-element.55), channel_id=1, source_target_pairs={{0,12},{4,8},{8,4},{12,0},{16,28},{20,24},{24,20},{28,16},{1,13},{... | collective-permute-start | bytes 589832 | tf_op jit(solution)/shard_map/ppermute | solution.py:452
  76.9 0.1 choose.1
  77.1 0.0 collective-permute-done.24.refs_6_
  77.1 0.9 collective-permute-start.27
  77.9 2.3 %collective-permute-done.25.refs_7_ = bf16[96,512]{1,0:T(8,128)(2,1)S(1)} collective-permute-done((bf16[96,512]{1,0:T(8,128)(2,1)S(1)}, bf16[96,512]{1,0:T(8,128)(2,1)S(1)}, u32[]{:S(2)}, u32[]{:S(2)}) %collective-permute-start.25) | collective-permute-done | bytes 98336 | tf_op jit(solution)/shard_map/ppermute | solution.py:452
  80.3 0.9 collective-permute-start.28
  81.1 0.0 collective-permute-done.19.refs_1_
  81.1 1.4 %collective-permute-start.29 = (bf16[96,512]{1,0:T(8,128)(2,1)S(1)}, bf16[96,512]{1,0:T(8,128)(2,1)S(1)}, u32[]{:S(2)}, u32[]{:S(2)}) collective-permute-start(bf16[96,512]{1,0:T(8,128)(2,1)S(1)} %get-tuple-element.64), channel_id=1, source_target_pairs={{0,12},{4,8},{8,4},{12,0},{16,28},{20,24},{24,20},{28,16},{1,13},{... | collective-permute-start | bytes 294920 | tf_op jit(solution)/shard_map/ppermute | solution.py:452
  82.5 1.5 %combine.1 = bf16[192,4096]{1,0:T(8,128)(2,1)} custom-call(f32[24,192]{1,0:T(8,128)S(1)} %copy-done.6, bf16[24,4096]{1,0:T(8,128)(2,1)S(1)} %get-tuple-element.41.refs_1_, bf16[24,4096]{1,0:T(8,128)(2,1)S(1)} %collective-permute-done.6.refs_2_, bf16[24,4096]{1,0:T(8,128)(2,1)S(1)} %collective-permute-done.7.refs_3_, ...), custom_call_target="tpu_custom_call" | custom-call | flops 37748736 | bytes 25165824 | tf_op jit(solution)/shard_map/combine/pallas_call | solution.py:407
  84.0 1.3 %update.1 = (f32[2,192,512]{2,1,0:T(8,128)}, f32[2,192,512]{2,1,0:T(8,128)}) custom-call(f32[2,192,512]{2,1,0:T(8,128)S(1)} %get-tuple-element.65.summed, f32[2,192,512]{2,1,0:T(8,128)S(1)} %copy-done.2, f32[2,192,512]{2,1,0:T(8,128)S(1)} %copy-done.3), custom_call_target="tpu_custom_call" | custom-call | flops 1572864 | bytes 25165824 | tf_op jit(solution)/shard_map/update/pallas_call | solution.py:336
  85.3 0.0 collective-permute-done.20.refs_2_
  85.3 2.5 %collective-permute-done.21.refs_3_ = bf16[192,512]{1,0:T(8,128)(2,1)S(1)} collective-permute-done((bf16[192,512]{1,0:T(8,128)(2,1)S(1)}, bf16[192,512]{1,0:T(8,128)(2,1)S(1)}, u32[]{:S(2)}, u32[]{:S(2)}) %collective-permute-start.21) | collective-permute-done | bytes 196640 | tf_op jit(solution)/shard_map/ppermute | solution.py:452
  87.8 0.0 collective-permute-done.27.refs_9_
  87.8 1.4 %collective-permute-done.28.refs_10_ = bf16[96,512]{1,0:T(8,128)(2,1)S(1)} collective-permute-done((bf16[96,512]{1,0:T(8,128)(2,1)S(1)}, bf16[96,512]{1,0:T(8,128)(2,1)S(1)}, u32[]{:S(2)}, u32[]{:S(2)}) %collective-permute-start.28) | collective-permute-done | bytes 98336 | tf_op jit(solution)/shard_map/ppermute | solution.py:452
  89.3 2.7 %collective-permute-done.29.refs_11_ = bf16[96,512]{1,0:T(8,128)(2,1)S(1)} collective-permute-done((bf16[96,512]{1,0:T(8,128)(2,1)S(1)}, bf16[96,512]{1,0:T(8,128)(2,1)S(1)}, u32[]{:S(2)}, u32[]{:S(2)}) %collective-permute-start.29) | collective-permute-done | bytes 98336 | tf_op jit(solution)/shard_map/ppermute | solution.py:452
  92.0 1.2 %place_blocks.1 = bf16[192,4096]{1,0:T(8,128)(2,1)} custom-call(bf16[192,512]{1,0:T(8,128)(2,1)S(1)} %get-tuple-element.52.refs_0_, bf16[192,512]{1,0:T(8,128)(2,1)S(1)} %collective-permute-done.19.refs_1_, bf16[192,512]{1,0:T(8,128)(2,1)S(1)} %collective-permute-done.20.refs_2_, bf16[192,512]{1,0:T(8,128)(2,1)S(1)} %collective-permute-done.21.refs_3_, ...), custom_call_target="tpu_custom_call" | custom-call | bytes 50331648 | tf_op jit(solution)/shard_map/place_blocks/pallas_call | solution.py:439
  (23 shorter events, 0.1 us)
Async XLA Ops:
  1.3 31.9 %copy-start.1 = (bf16[1,4096,192]{1,2,0:T(8,128)(2,1)S(1)}, bf16[1,4096,192]{1,2,0:T(8,128)(2,1)}, u32[]{:S(2)}) copy-start(bf16[1,4096,192]{1,2,0:T(8,128)(2,1)} %param.15) | copy-start | bytes 4718596
  3.9 15.9 %copy-start.5 = (bf16[24,4096]{1,0:T(8,128)(2,1)S(1)}, bf16[24,4096]{1,0:T(8,128)(2,1)}, u32[]{:S(2)}) copy-start(bf16[24,4096]{1,0:T(8,128)(2,1)} %get-tuple-element.38.refs_0_) | copy-start | bytes 589828
  3.9 29.3 %copy-start = (bf16[1,4096,192]{1,2,0:T(8,128)(2,1)S(1)}, bf16[1,4096,192]{1,2,0:T(8,128)(2,1)}, u32[]{:S(2)}) copy-start(bf16[1,4096,192]{1,2,0:T(8,128)(2,1)} %param.14) | copy-start | bytes 4718596
  4.0 0.9 copy-start.6
  6.6 5.7 %collective-permute-start.13 = (bf16[2,24,512]{2,1,0:T(8,128)(2,1)S(1)}, bf16[2,24,512]{2,1,0:T(8,128)(2,1)S(1)}, u32[]{:S(2)}, u32[]{:S(2)}) collective-permute-start(bf16[2,24,512]{2,1,0:T(8,128)(2,1)S(1)} %get-tuple-element.47), channel_id=1, source_target_pairs={{0,8},{4,12},{8,0},{12,4},{16,24},{20,28},{24,16},{28,20},{1,9},{5... | collective-permute-start | bytes 147464 | tf_op jit(solution)/shard_map/ppermute | solution.py:452
  9.7 5.9 %collective-permute-start.14 = (bf16[2,24,512]{2,1,0:T(8,128)(2,1)S(1)}, bf16[2,24,512]{2,1,0:T(8,128)(2,1)S(1)}, u32[]{:S(2)}, u32[]{:S(2)}) collective-permute-start(bf16[2,24,512]{2,1,0:T(8,128)(2,1)S(1)} %get-tuple-element.48), channel_id=1, source_target_pairs={{0,16},{4,20},{8,24},{12,28},{16,0},{20,4},{24,8},{28,12},{1,17},{... | collective-permute-start | bytes 147464 | tf_op jit(solution)/shard_map/ppermute | solution.py:452
  12.3 5.9 %collective-permute-start.15 = (bf16[2,24,512]{2,1,0:T(8,128)(2,1)S(1)}, bf16[2,24,512]{2,1,0:T(8,128)(2,1)S(1)}, u32[]{:S(2)}, u32[]{:S(2)}) collective-permute-start(bf16[2,24,512]{2,1,0:T(8,128)(2,1)S(1)} %get-tuple-element.49), channel_id=1, source_target_pairs={{0,24},{4,28},{8,16},{12,20},{16,8},{20,12},{24,0},{28,4},{1,25},{... | collective-permute-start | bytes 147464 | tf_op jit(solution)/shard_map/ppermute | solution.py:452
  18.2 4.7 %collective-permute-start.16 = (bf16[4,24,512]{2,1,0:T(8,128)(2,1)S(1)}, bf16[4,24,512]{2,1,0:T(8,128)(2,1)S(1)}, u32[]{:S(2)}, u32[]{:S(2)}) collective-permute-start(bf16[4,24,512]{2,1,0:T(8,128)(2,1)S(1)} %get-tuple-element.51), channel_id=1, source_target_pairs={{0,4},{4,0},{8,12},{12,8},{16,20},{20,16},{24,28},{28,24},{1,5},{5... | collective-permute-start | bytes 294920 | tf_op jit(solution)/shard_map/ppermute | solution.py:452
  19.8 7.8 %collective-permute-start.4 = (bf16[24,4096]{1,0:T(8,128)(2,1)S(1)}, bf16[24,4096]{1,0:T(8,128)(2,1)S(1)}, u32[]{:S(2)}, u32[]{:S(2)}) collective-permute-start(bf16[24,4096]{1,0:T(8,128)(2,1)S(1)} %copy-done.5), channel_id=1, source_target_pairs={{0,2},{1,3},{2,0},{3,1},{4,6},{5,7},{6,4},{7,5},{8,10},{9,11},{10,... | collective-permute-start | bytes 589832 | tf_op jit(solution)/shard_map/ppermute | solution.py:452
  22.9 8.2 %collective-permute-start.17 = (bf16[8,24,512]{2,1,0:T(8,128)(2,1)S(1)}, bf16[8,24,512]{2,1,0:T(8,128)(2,1)S(1)}, u32[]{:S(2)}, u32[]{:S(2)}) collective-permute-start(bf16[8,24,512]{2,1,0:T(8,128)(2,1)S(1)} %join.2.one), channel_id=1, source_target_pairs={{0,2},{1,3},{2,0},{3,1},{4,6},{5,7},{6,4},{7,5},{8,10},{9,11},{10,... | collective-permute-start | bytes 589832 | tf_op jit(solution)/shard_map/ppermute | solution.py:452
  24.5 8.7 %collective-permute-start.1 = (bf16[24,4096]{1,0:T(8,128)(2,1)S(1)}, bf16[24,4096]{1,0:T(8,128)(2,1)S(1)}, u32[]{:S(2)}, u32[]{:S(2)}) collective-permute-start(bf16[24,4096]{1,0:T(8,128)(2,1)S(1)} %get-tuple-element.37.refs_0_), channel_id=1, source_target_pairs={{0,2},{1,3},{2,0},{3,1},{4,6},{5,7},{6,4},{7,5},{8,10},{9,11},{10,... | collective-permute-start | bytes 589832 | tf_op jit(solution)/shard_map/ppermute | solution.py:452
  25.0 8.2 %collective-permute-start.3 = (bf16[24,4096]{1,0:T(8,128)(2,1)S(1)}, bf16[24,4096]{1,0:T(8,128)(2,1)S(1)}, u32[]{:S(2)}, u32[]{:S(2)}) collective-permute-start(bf16[24,4096]{1,0:T(8,128)(2,1)S(1)} %copy-done.5), channel_id=1, source_target_pairs={{0,1},{1,0},{2,3},{3,2},{4,5},{5,4},{6,7},{7,6},{8,9},{9,8},{10,11... | collective-permute-start | bytes 589832 | tf_op jit(solution)/shard_map/ppermute | solution.py:452
  27.6 5.6 %collective-permute-start.5 = (bf16[24,4096]{1,0:T(8,128)(2,1)S(1)}, bf16[24,4096]{1,0:T(8,128)(2,1)S(1)}, u32[]{:S(2)}, u32[]{:S(2)}) collective-permute-start(bf16[24,4096]{1,0:T(8,128)(2,1)S(1)} %collective-permute-done.4.refs_2_), channel_id=1, source_target_pairs={{0,1},{1,0},{2,3},{3,2},{4,5},{5,4},{6,7},{7,6},{8,9},{9,8},{10,11... | collective-permute-start | bytes 589832 | tf_op jit(solution)/shard_map/ppermute | solution.py:452
  31.1 20.3 %collective-permute-start.18 = (bf16[16,24,512]{2,1,0:T(8,128)(2,1)S(1)}, bf16[16,24,512]{2,1,0:T(8,128)(2,1)S(1)}, u32[]{:S(2)}, u32[]{:S(2)}) collective-permute-start(bf16[16,24,512]{2,1,0:T(8,128)(2,1)S(1)} %join.3.refs_2_), channel_id=1, source_target_pairs={{0,1},{1,0},{2,3},{3,2},{4,5},{5,4},{6,7},{7,6},{8,9},{9,8},{10,11... | collective-permute-start | bytes 1179656 | tf_op jit(solution)/shard_map/ppermute | solution.py:452
  31.2 15.4 %collective-permute-start = (bf16[24,4096]{1,0:T(8,128)(2,1)S(1)}, bf16[24,4096]{1,0:T(8,128)(2,1)S(1)}, u32[]{:S(2)}, u32[]{:S(2)}) collective-permute-start(bf16[24,4096]{1,0:T(8,128)(2,1)S(1)} %get-tuple-element.37.refs_0_), channel_id=1, source_target_pairs={{0,1},{1,0},{2,3},{3,2},{4,5},{5,4},{6,7},{7,6},{8,9},{9,8},{10,11... | collective-permute-start | bytes 589832 | tf_op jit(solution)/shard_map/ppermute | solution.py:452
  33.2 13.4 %collective-permute-start.2 = (bf16[24,4096]{1,0:T(8,128)(2,1)S(1)}, bf16[24,4096]{1,0:T(8,128)(2,1)S(1)}, u32[]{:S(2)}, u32[]{:S(2)}) collective-permute-start(bf16[24,4096]{1,0:T(8,128)(2,1)S(1)} %collective-permute-done.1.refs_2_), channel_id=1, source_target_pairs={{0,1},{1,0},{2,3},{3,2},{4,5},{5,4},{6,7},{7,6},{8,9},{9,8},{10,11... | collective-permute-start | bytes 589832 | tf_op jit(solution)/shard_map/ppermute | solution.py:452
  33.2 13.4 %copy-start.4 = (bf16[1,192,4096]{2,1,0:T(8,128)(2,1)S(1)}, bf16[1,192,4096]{2,1,0:T(8,128)(2,1)}, u32[]{:S(2)}) copy-start(bf16[1,192,4096]{2,1,0:T(8,128)(2,1)} %param.16) | copy-start | bytes 4718596
  34.4 6.8 %collective-permute-start.11 = (bf16[112,192]{1,0:T(8,128)(2,1)S(1)}, bf16[112,192]{1,0:T(8,128)(2,1)S(1)}, u32[]{:S(2)}, u32[]{:S(2)}) collective-permute-start(bf16[112,192]{1,0:T(8,128)(2,1)S(1)} %get-tuple-element.45.refs_0_), channel_id=1, source_target_pairs={{0,24},{4,28},{8,16},{12,20},{16,8},{20,12},{24,0},{28,4},{1,25},{... | collective-permute-start | bytes 129032 | tf_op jit(solution)/shard_map/ppermute | solution.py:452
  35.3 7.4 %collective-permute-start.10 = (bf16[112,192]{1,0:T(8,128)(2,1)S(1)}, bf16[112,192]{1,0:T(8,128)(2,1)S(1)}, u32[]{:S(2)}, u32[]{:S(2)}) collective-permute-start(bf16[112,192]{1,0:T(8,128)(2,1)S(1)} %get-tuple-element.45.refs_0_), channel_id=1, source_target_pairs={{0,16},{4,20},{8,24},{12,28},{16,0},{20,4},{24,8},{28,12},{1,17},{... | collective-permute-start | bytes 129032 | tf_op jit(solution)/shard_map/ppermute | solution.py:452
  41.2 4.2 %collective-permute-start.9 = (bf16[112,192]{1,0:T(8,128)(2,1)S(1)}, bf16[112,192]{1,0:T(8,128)(2,1)S(1)}, u32[]{:S(2)}, u32[]{:S(2)}) collective-permute-start(bf16[112,192]{1,0:T(8,128)(2,1)S(1)} %get-tuple-element.45.refs_0_), channel_id=1, source_target_pairs={{0,8},{4,12},{8,0},{12,4},{16,24},{20,28},{24,16},{28,20},{1,9},{5... | collective-permute-start | bytes 129032 | tf_op jit(solution)/shard_map/ppermute | solution.py:452
  45.4 6.1 %collective-permute-start.12 = (bf16[4,112,192]{2,1,0:T(8,128)(2,1)S(1)}, bf16[4,112,192]{2,1,0:T(8,128)(2,1)S(1)}, u32[]{:S(2)}, u32[]{:S(2)}) collective-permute-start(bf16[4,112,192]{2,1,0:T(8,128)(2,1)S(1)} %pile.1.refs_0_), channel_id=1, source_target_pairs={{0,4},{4,0},{8,12},{12,8},{16,20},{20,16},{24,28},{28,24},{1,5},{5... | collective-permute-start | bytes 516104 | tf_op jit(solution)/shard_map/ppermute | solution.py:452
  46.7 4.8 %copy-start.2 = (f32[2,192,512]{2,1,0:T(8,128)S(1)}, f32[2,192,512]{2,1,0:T(8,128)}, u32[]{:S(2)}) copy-start(f32[2,192,512]{2,1,0:T(8,128)} %first.1) | copy-start | bytes 2359300
  46.7 4.8 %copy-start.3 = (f32[2,192,512]{2,1,0:T(8,128)S(1)}, f32[2,192,512]{2,1,0:T(8,128)}, u32[]{:S(2)}) copy-start(f32[2,192,512]{2,1,0:T(8,128)} %second.1) | copy-start | bytes 2359300
  48.6 6.9 %collective-permute-start.6 = (bf16[24,4096]{1,0:T(8,128)(2,1)S(1)}, bf16[24,4096]{1,0:T(8,128)(2,1)S(1)}, u32[]{:S(2)}, u32[]{:S(2)}) collective-permute-start(bf16[24,4096]{1,0:T(8,128)(2,1)S(1)} %get-tuple-element.42), channel_id=1, source_target_pairs={{0,1},{1,0},{2,3},{3,2},{4,5},{5,4},{6,7},{7,6},{8,9},{9,8},{10,11... | collective-permute-start | bytes 589832 | tf_op jit(solution)/shard_map/ppermute | solution.py:452
  48.7 7.8 %collective-permute-start.7 = (bf16[24,4096]{1,0:T(8,128)(2,1)S(1)}, bf16[24,4096]{1,0:T(8,128)(2,1)S(1)}, u32[]{:S(2)}, u32[]{:S(2)}) collective-permute-start(bf16[24,4096]{1,0:T(8,128)(2,1)S(1)} %get-tuple-element.43), channel_id=1, source_target_pairs={{0,2},{1,3},{2,0},{3,1},{4,6},{5,7},{6,4},{7,5},{8,10},{9,11},{10,... | collective-permute-start | bytes 589832 | tf_op jit(solution)/shard_map/ppermute | solution.py:452
  50.2 9.4 %collective-permute-start.8 = (bf16[24,4096]{1,0:T(8,128)(2,1)S(1)}, bf16[24,4096]{1,0:T(8,128)(2,1)S(1)}, u32[]{:S(2)}, u32[]{:S(2)}) collective-permute-start(bf16[24,4096]{1,0:T(8,128)(2,1)S(1)} %get-tuple-element.44), channel_id=1, source_target_pairs={{0,3},{1,2},{2,1},{3,0},{4,7},{5,6},{6,5},{7,4},{8,11},{9,10},{10,... | collective-permute-start | bytes 589832 | tf_op jit(solution)/shard_map/ppermute | solution.py:452
  52.5 21.7 %collective-permute-start.26 = (bf16[2,96,512]{2,1,0:T(8,128)(2,1)S(1)}, bf16[2,96,512]{2,1,0:T(8,128)(2,1)S(1)}, u32[]{:S(2)}, u32[]{:S(2)}) collective-permute-start(bf16[2,96,512]{2,1,0:T(8,128)(2,1)S(1)} %get-tuple-element.60), channel_id=1, source_target_pairs={{0,16},{4,20},{8,24},{12,28},{16,0},{20,4},{24,8},{28,12},{1,17},{... | collective-permute-start | bytes 589832 | tf_op jit(solution)/shard_map/ppermute | solution.py:452
  52.6 19.3 %collective-permute-start.22 = (bf16[96,512]{1,0:T(8,128)(2,1)S(1)}, bf16[96,512]{1,0:T(8,128)(2,1)S(1)}, u32[]{:S(2)}, u32[]{:S(2)}) collective-permute-start(bf16[96,512]{1,0:T(8,128)(2,1)S(1)} %get-tuple-element.56), channel_id=1, source_target_pairs={{0,16},{4,20},{8,24},{12,28},{16,0},{20,4},{24,8},{28,12},{1,17},{... | collective-permute-start | bytes 294920 | tf_op jit(solution)/shard_map/ppermute | solution.py:452
  55.5 18.7 %collective-permute-start.23 = (bf16[96,512]{1,0:T(8,128)(2,1)S(1)}, bf16[96,512]{1,0:T(8,128)(2,1)S(1)}, u32[]{:S(2)}, u32[]{:S(2)}) collective-permute-start(bf16[96,512]{1,0:T(8,128)(2,1)S(1)} %get-tuple-element.57), channel_id=1, source_target_pairs={{0,20},{4,16},{8,28},{12,24},{16,4},{20,0},{24,12},{28,8},{1,21},{... | collective-permute-start | bytes 294920 | tf_op jit(solution)/shard_map/ppermute | solution.py:452
  56.5 24.6 %collective-permute-start.19 = (bf16[192,512]{1,0:T(8,128)(2,1)S(1)}, bf16[192,512]{1,0:T(8,128)(2,1)S(1)}, u32[]{:S(2)}, u32[]{:S(2)}) collective-permute-start(bf16[192,512]{1,0:T(8,128)(2,1)S(1)} %get-tuple-element.53), channel_id=1, source_target_pairs={{0,4},{4,0},{8,12},{12,8},{16,20},{20,16},{24,28},{28,24},{1,5},{5... | collective-permute-start | bytes 589832 | tf_op jit(solution)/shard_map/ppermute | solution.py:452
  59.6 17.4 %collective-permute-start.24 = (bf16[96,512]{1,0:T(8,128)(2,1)S(1)}, bf16[96,512]{1,0:T(8,128)(2,1)S(1)}, u32[]{:S(2)}, u32[]{:S(2)}) collective-permute-start(bf16[96,512]{1,0:T(8,128)(2,1)S(1)} %get-tuple-element.58), channel_id=1, source_target_pairs={{0,24},{4,28},{8,16},{12,20},{16,8},{20,12},{24,0},{28,4},{1,25},{... | collective-permute-start | bytes 294920 | tf_op jit(solution)/shard_map/ppermute | solution.py:452
  71.9 8.4 %collective-permute-start.25 = (bf16[96,512]{1,0:T(8,128)(2,1)S(1)}, bf16[96,512]{1,0:T(8,128)(2,1)S(1)}, u32[]{:S(2)}, u32[]{:S(2)}) collective-permute-start(bf16[96,512]{1,0:T(8,128)(2,1)S(1)} %get-tuple-element.59), channel_id=1, source_target_pairs={{0,28},{4,24},{8,20},{12,16},{16,12},{20,8},{24,4},{28,0},{1,29},{... | collective-permute-start | bytes 294920 | tf_op jit(solution)/shard_map/ppermute | solution.py:452
  74.3 11.0 %collective-permute-start.20 = (bf16[192,512]{1,0:T(8,128)(2,1)S(1)}, bf16[192,512]{1,0:T(8,128)(2,1)S(1)}, u32[]{:S(2)}, u32[]{:S(2)}) collective-permute-start(bf16[192,512]{1,0:T(8,128)(2,1)S(1)} %get-tuple-element.54), channel_id=1, source_target_pairs={{0,8},{4,12},{8,0},{12,4},{16,24},{20,28},{24,16},{28,20},{1,9},{5... | collective-permute-start | bytes 589832 | tf_op jit(solution)/shard_map/ppermute | solution.py:452
  74.3 13.6 %collective-permute-start.21 = (bf16[192,512]{1,0:T(8,128)(2,1)S(1)}, bf16[192,512]{1,0:T(8,128)(2,1)S(1)}, u32[]{:S(2)}, u32[]{:S(2)}) collective-permute-start(bf16[192,512]{1,0:T(8,128)(2,1)S(1)} %get-tuple-element.55), channel_id=1, source_target_pairs={{0,12},{4,8},{8,4},{12,0},{16,28},{20,24},{24,20},{28,16},{1,13},{... | collective-permute-start | bytes 589832 | tf_op jit(solution)/shard_map/ppermute | solution.py:452
  77.1 10.8 %collective-permute-start.27 = (bf16[96,512]{1,0:T(8,128)(2,1)S(1)}, bf16[96,512]{1,0:T(8,128)(2,1)S(1)}, u32[]{:S(2)}, u32[]{:S(2)}) collective-permute-start(bf16[96,512]{1,0:T(8,128)(2,1)S(1)} %get-tuple-element.62), channel_id=1, source_target_pairs={{0,4},{4,0},{8,12},{12,8},{16,20},{20,16},{24,28},{28,24},{1,5},{5... | collective-permute-start | bytes 294920 | tf_op jit(solution)/shard_map/ppermute | solution.py:452
  80.3 9.0 %collective-permute-start.28 = (bf16[96,512]{1,0:T(8,128)(2,1)S(1)}, bf16[96,512]{1,0:T(8,128)(2,1)S(1)}, u32[]{:S(2)}, u32[]{:S(2)}) collective-permute-start(bf16[96,512]{1,0:T(8,128)(2,1)S(1)} %get-tuple-element.63), channel_id=1, source_target_pairs={{0,8},{4,12},{8,0},{12,4},{16,24},{20,28},{24,16},{28,20},{1,9},{5... | collective-permute-start | bytes 294920 | tf_op jit(solution)/shard_map/ppermute | solution.py:452
  81.1 10.8 %collective-permute-start.29 = (bf16[96,512]{1,0:T(8,128)(2,1)S(1)}, bf16[96,512]{1,0:T(8,128)(2,1)S(1)}, u32[]{:S(2)}, u32[]{:S(2)}) collective-permute-start(bf16[96,512]{1,0:T(8,128)(2,1)S(1)} %get-tuple-element.64), channel_id=1, source_target_pairs={{0,12},{4,8},{8,4},{12,0},{16,28},{20,24},{24,20},{28,16},{1,13},{... | collective-permute-start | bytes 294920 | tf_op jit(solution)/shard_map/ppermute | solution.py:452

commit v4 on v3

--- a/solution.py
+++ b/solution.py
@@ -12,7 +12,7 @@
 QUARTERS = 4
 CANDS = 2
 CAP = 24
-TAG = 16
+TAG = 8
 
 
 beta_one = 0.9
@@ -416,17 +416,16 @@
     )(picks, *blocks)
 
 
-def place_kernel(groups, *refs):
+def place_kernel(peers, fold, *refs):
     me = lax.axis_index("grp")
-    half = groups // 2
-    blocks, (out, sems) = refs[: groups + half], refs[groups + half :]
-    units, columns = blocks[0].shape
+    count = len(peers)
+    blocks, (out, sems) = refs[:count], refs[-2:]
+    columns = blocks[0].shape[1]
     copies = []
     for number, block in enumerate(blocks):
         rows = block.shape[0]
-        peer = number if number < groups else number - half
-        start = pl.multiple_of((me ^ peer) * columns, 128)
-        at = pl.ds(0 if number < groups else units - rows, rows)
+        start = pl.multiple_of((me ^ peers[number]) * columns, 128)
+        at = pl.ds(out.shape[0] - rows if fold else 0, rows)
         target = out.at[at, pl.ds(start, columns)]
         copies.append(pltpu.make_async_copy(block, target, sems.at[number]))
         copies[-1].start()
@@ -434,18 +433,20 @@
         copy.wait()
 
 
-def place_blocks(groups, blocks):
-    units, columns = blocks[0].shape
-    return pl.pallas_call(
-        functools.partial(place_kernel, groups),
-        in_specs=[LOCAL] * len(blocks),
+def place_blocks(peers, blocks, shape, placed=None):
+    fold = placed is not None
+    count = len(blocks)
+    return pl.pallas_call(
+        functools.partial(place_kernel, peers, fold),
+        in_specs=[LOCAL] * count + [FAR] * fold,
         out_specs=FAR,
-        out_shape=jax.ShapeDtypeStruct((units, groups * columns), BF16),
-        scratch_shapes=[pltpu.SemaphoreType.DMA((len(blocks),))],
-        compiler_params=PARAMS,
-        cost_estimate=cost(0, 4 * groups * units * columns),
-        name="place_blocks",
-    )(*blocks)
+        out_shape=jax.ShapeDtypeStruct(shape, BF16),
+        scratch_shapes=[pltpu.SemaphoreType.DMA((count,))],
+        input_output_aliases={count: 0} if fold else {},
+        compiler_params=PARAMS,
+        cost_estimate=cost(0, 4 * shape[0] * shape[1]),
+        name="place_last" if fold else "place_first",
+    )(*blocks, *([placed] if fold else []))
 
 
 def swap(value, axis, size, bits):
@@ -531,7 +532,7 @@
     got_dirs = exchange(dirs)
     both = swap(both, "grp", groups, groups // 2)
     dirs = choose(hiddens, both)
-    got_dirs = got_dirs + exchange(dirs)
+    passed_dirs = exchange(dirs)
     new_first, new_second = update(summed, moment_first, moment_second)
 
     in_scaled = share(per_slot(scaled), 0)
@@ -540,7 +541,11 @@
     for bits in range(1, num_ep):
         returned.append(swap(partials[bits], "ep", num_ep, bits))
     token_grad = combine(picks, returned)
-    step_dir = place_blocks(groups, got_dirs)[None]
+    units, columns = got_dirs[0].shape
+    shape = (units, groups * columns)
+    peers = list(range(groups))
+    placed = place_blocks(peers, got_dirs, shape)
+    step_dir = place_blocks(peers[groups // 2 :], passed_dirs, shape, placed)[None]
     return (token_grad, step_dir, new_first, new_second)
 
 

time: 93.4 us -> 89.9 us (0.963)
  waiting for transfers between devices: 49.5 us -> 44.4 us
  starting transfers between devices: 28.6 us -> 29.7 us
    ppermute x30, waiting for transfers between devices: 49.5 us -> 44.4 us  [swap(): return lax.ppermute(value, axis, [(i, i ^ bits) for i in range(size)])]
    ppermute x30, starting transfers between devices: 28.6 us -> 29.7 us  [swap(): return lax.ppermute(value, axis, [(i, i ^ bits) for i in range(size)])]
  transfers between devices with their start and end apart: 30 -> 30, of which waited for: 18 -> 16; matrix products, arithmetic and copies ran while one was open for 0% -> 0% of each run, Pallas kernels for 8% -> 9%
where the time goes in v4:
time: 89.9 us; the launch traced here: 89.7 us
  waiting for transfers between devices  44.4 us (49%)
  starting transfers between devices  29.7 us (33%)
  Pallas kernels  13.3 us (15%)
  between operations  1.52 us (2%)
  local copies, waits for them, and re-layouts  0.9 us (1%)
    ppermute x30, waiting for transfers between devices, swap(): return lax.ppermute(value, axis, [(i, i ^ bits) for i in range(size)])  44.4 us
    ppermute x30, starting transfers between devices, swap(): return lax.ppermute(value, axis, [(i, i ^ bits) for i in range(size)])  29.7 us
    pallas_call x1, Pallas kernels, select(): pl.pallas_call(functools.partial(select_kernel, slots, pieces), in_specs=...  2.63 us
    pallas_call x1, Pallas kernels, backward(): pl.pallas_call(functools.partial(backward_kernel, parts), in_specs=[LOCAL...  1.9 us
    pallas_call x2, Pallas kernels, place_blocks(): pl.pallas_call(functools.partial(place_kernel, peers, fold), in_specs=[LO...  1.85 us
  transfers between devices with their start and end apart: 30, of which 16 were waited for; matrix products, arithmetic and copies ran while one was open for 0% of the time, Pallas kernels for 9%

profile of v4, /device:TPU:0, one launch (start us, length us, event | category | flops | bytes accessed | tf_op | source)
XLA Modules:
  0.0 89.7 jit_solution(10627516065004484062)
XLA Ops:
  1.3 2.6 %select_rows.1 = (bf16[24,4096]{1,0:T(8,128)(2,1)}, f32[24,192]{1,0:T(8,128)}) custom-call(s32[1,1]{1,0:T(1,128)S(6)} %copy.16.place, s32[8,192]{1,0:T(8,128)} %bitcast.16, f32[8,192]{1,0:T(8,128)} %bitcast.17, bf16[192,4096]{1,0:T(8,128)(2,1)} %tokens.1), custom_call_target="tpu_custom_call" | custom-call | flops 37748736 | bytes 25165824 | tf_op jit(solution)/shard_map/select_rows/pallas_call | solution.py:85
  3.9 0.0 copy-start.5
  3.9 0.0 copy-start
  4.0 0.0 copy-start.6
  4.0 0.9 copy-done.6
  4.8 1.8 %scale_rows.1 = (bf16[24,4096]{1,0:T(8,128)(2,1)S(1)}, bf16[2,24,512]{2,1,0:T(8,128)(2,1)S(1)}, bf16[2,24,512]{2,1,0:T(8,128)(2,1)S(1)}, bf16[2,24,512]{2,1,0:T(8,128)(2,1)S(1)}, bf16[2,24,512]{2,1,0:T(8,128)(2,1)S(1)}) custom-call(f32[24,192]{1,0:T(8,128)S(1)} %copy-done.6, bf16[192,4096]{1,0:T(8,128)(2,1)} %grads.1), custom_call_target="tpu_custom_call" | custom-call | flops 37748736 | bytes 100663296 | tf_op jit(solution)/shard_map/scale_rows/pallas_call | solution.py:134
  6.6 3.1 %collective-permute-start.13 = (bf16[2,24,512]{2,1,0:T(8,128)(2,1)S(1)}, bf16[2,24,512]{2,1,0:T(8,128)(2,1)S(1)}, u32[]{:S(2)}, u32[]{:S(2)}) collective-permute-start(bf16[2,24,512]{2,1,0:T(8,128)(2,1)S(1)} %get-tuple-element.47), channel_id=1, source_target_pairs={{0,8},{4,12},{8,0},{12,4},{16,24},{20,28},{24,16},{28,20},{1,9},{5... | collective-permute-start | bytes 147464 | tf_op jit(solution)/shard_map/ppermute | solution.py:453
  9.7 2.6 %collective-permute-start.14 = (bf16[2,24,512]{2,1,0:T(8,128)(2,1)S(1)}, bf16[2,24,512]{2,1,0:T(8,128)(2,1)S(1)}, u32[]{:S(2)}, u32[]{:S(2)}) collective-permute-start(bf16[2,24,512]{2,1,0:T(8,128)(2,1)S(1)} %get-tuple-element.48), channel_id=1, source_target_pairs={{0,16},{4,20},{8,24},{12,28},{16,0},{20,4},{24,8},{28,12},{1,17},{... | collective-permute-start | bytes 147464 | tf_op jit(solution)/shard_map/ppermute | solution.py:453
  12.3 0.0 collective-permute-start.15
  12.3 3.3 %collective-permute-done.14.refs_2_ = bf16[2,24,512]{2,1,0:T(8,128)(2,1)S(1)} collective-permute-done((bf16[2,24,512]{2,1,0:T(8,128)(2,1)S(1)}, bf16[2,24,512]{2,1,0:T(8,128)(2,1)S(1)}, u32[]{:S(2)}, u32[]{:S(2)}) %collective-permute-start.14) | collective-permute-done | bytes 49184 | tf_op jit(solution)/shard_map/ppermute | solution.py:453
  15.7 2.6 %collective-permute-done.15.refs_3_ = bf16[2,24,512]{2,1,0:T(8,128)(2,1)S(1)} collective-permute-done((bf16[2,24,512]{2,1,0:T(8,128)(2,1)S(1)}, bf16[2,24,512]{2,1,0:T(8,128)(2,1)S(1)}, u32[]{:S(2)}, u32[]{:S(2)}) %collective-permute-start.15) | collective-permute-done | bytes 49184 | tf_op jit(solution)/shard_map/ppermute | solution.py:453
  18.2 1.6 %collective-permute-start.16 = (bf16[4,24,512]{2,1,0:T(8,128)(2,1)S(1)}, bf16[4,24,512]{2,1,0:T(8,128)(2,1)S(1)}, u32[]{:S(2)}, u32[]{:S(2)}) collective-permute-start(bf16[4,24,512]{2,1,0:T(8,128)(2,1)S(1)} %get-tuple-element.51), channel_id=1, source_target_pairs={{0,4},{4,0},{8,12},{12,8},{16,20},{20,16},{24,28},{28,24},{1,5},{5... | collective-permute-start | bytes 294920 | tf_op jit(solution)/shard_map/ppermute | solution.py:453
  19.8 1.5 %collective-permute-start.4 = (bf16[24,4096]{1,0:T(8,128)(2,1)S(1)}, bf16[24,4096]{1,0:T(8,128)(2,1)S(1)}, u32[]{:S(2)}, u32[]{:S(2)}) collective-permute-start(bf16[24,4096]{1,0:T(8,128)(2,1)S(1)} %copy-done.5), channel_id=1, source_target_pairs={{0,2},{1,3},{2,0},{3,1},{4,6},{5,7},{6,4},{7,5},{8,10},{9,11},{10,... | collective-permute-start | bytes 589832 | tf_op jit(solution)/shard_map/ppermute | solution.py:453
  21.3 1.6 %collective-permute-done.16.two = bf16[4,24,512]{2,1,0:T(8,128)(2,1)S(1)} collective-permute-done((bf16[4,24,512]{2,1,0:T(8,128)(2,1)S(1)}, bf16[4,24,512]{2,1,0:T(8,128)(2,1)S(1)}, u32[]{:S(2)}, u32[]{:S(2)}) %collective-permute-start.16) | collective-permute-done | bytes 98336 | tf_op jit(solution)/shard_map/ppermute | solution.py:453
  22.9 1.6 %collective-permute-start.17 = (bf16[8,24,512]{2,1,0:T(8,128)(2,1)S(1)}, bf16[8,24,512]{2,1,0:T(8,128)(2,1)S(1)}, u32[]{:S(2)}, u32[]{:S(2)}) collective-permute-start(bf16[8,24,512]{2,1,0:T(8,128)(2,1)S(1)} %join.2.one), channel_id=1, source_target_pairs={{0,2},{1,3},{2,0},{3,1},{4,6},{5,7},{6,4},{7,5},{8,10},{9,11},{10,... | collective-permute-start | bytes 589832 | tf_op jit(solution)/shard_map/ppermute | solution.py:453
  24.5 0.5 collective-permute-start.1
  25.0 2.6 %collective-permute-done.4.refs_2_ = bf16[24,4096]{1,0:T(8,128)(2,1)S(1)} collective-permute-done((bf16[24,4096]{1,0:T(8,128)(2,1)S(1)}, bf16[24,4096]{1,0:T(8,128)(2,1)S(1)}, u32[]{:S(2)}, u32[]{:S(2)}) %collective-permute-start.4) | collective-permute-done | bytes 196640 | tf_op jit(solution)/shard_map/ppermute | solution.py:453
  27.6 3.5 %collective-permute-done.17.two = bf16[8,24,512]{2,1,0:T(8,128)(2,1)S(1)} collective-permute-done((bf16[8,24,512]{2,1,0:T(8,128)(2,1)S(1)}, bf16[8,24,512]{2,1,0:T(8,128)(2,1)S(1)}, u32[]{:S(2)}, u32[]{:S(2)}) %collective-permute-start.17) | collective-permute-done | bytes 196640 | tf_op jit(solution)/shard_map/ppermute | solution.py:453
  31.1 0.1 collective-permute-start.18
  31.2 0.5 collective-permute-start
  31.7 1.5 %collective-permute-done.1.refs_2_ = bf16[24,4096]{1,0:T(8,128)(2,1)S(1)} collective-permute-done((bf16[24,4096]{1,0:T(8,128)(2,1)S(1)}, bf16[24,4096]{1,0:T(8,128)(2,1)S(1)}, u32[]{:S(2)}, u32[]{:S(2)}) %collective-permute-start.1) | collective-permute-done | bytes 196640 | tf_op jit(solution)/shard_map/ppermute | solution.py:453
  33.2 0.0 copy-start.4
  33.2 1.2 %forward.1 = (f32[96,192]{1,0:T(8,128)S(1)}, f32[96,192]{1,0:T(8,128)S(1)}, bf16[104,192]{1,0:T(8,128)(2,1)S(1)}) custom-call(s32[1,1]{1,0:T(1,128)S(6)} %copy.16.place, bf16[24,4096]{1,0:T(8,128)(2,1)S(1)} %copy-done.5, bf16[24,4096]{1,0:T(8,128)(2,1)S(1)} %collective-permute-done.3.refs_1_, bf16[24,4096]{1,0:T(8,128)(2,1)S(1)} %collective-permute-done.4.refs_2_, ...), custom_call_target="tpu_custom_call" | custom-call | flops 301989888 | bytes 50331648 | tf_op jit(solution)/shard_map/forward/pallas_call | solution.py:218
  34.4 0.1 collective-permute-start.10
  34.5 1.8 %collective-permute-start.11 = (bf16[104,192]{1,0:T(8,128)(2,1)S(1)}, bf16[104,192]{1,0:T(8,128)(2,1)S(1)}, u32[]{:S(2)}, u32[]{:S(2)}) collective-permute-start(bf16[104,192]{1,0:T(8,128)(2,1)S(1)} %get-tuple-element.45.refs_0_), channel_id=1, source_target_pairs={{0,24},{4,28},{8,16},{12,20},{16,8},{20,12},{24,0},{28,4},{1,25},{... | collective-permute-start | bytes 119816 | tf_op jit(solution)/shard_map/ppermute | solution.py:453
  36.3 4.9 %collective-permute-done.10.refs_2_ = bf16[104,192]{1,0:T(8,128)(2,1)S(1)} collective-permute-done((bf16[104,192]{1,0:T(8,128)(2,1)S(1)}, bf16[104,192]{1,0:T(8,128)(2,1)S(1)}, u32[]{:S(2)}, u32[]{:S(2)}) %collective-permute-start.10) | collective-permute-done | bytes 39968 | tf_op jit(solution)/shard_map/ppermute | solution.py:453
  41.2 0.0 collective-permute-start.9
  41.2 0.0 collective-permute-done.11.refs_3_
  41.2 4.1 %collective-permute-done.9.refs_1_ = bf16[104,192]{1,0:T(8,128)(2,1)S(1)} collective-permute-done((bf16[104,192]{1,0:T(8,128)(2,1)S(1)}, bf16[104,192]{1,0:T(8,128)(2,1)S(1)}, u32[]{:S(2)}, u32[]{:S(2)}) %collective-permute-start.9) | collective-permute-done | bytes 39968 | tf_op jit(solution)/shard_map/ppermute | solution.py:453
  45.4 1.3 %collective-permute-start.12 = (bf16[4,104,192]{2,1,0:T(8,128)(2,1)S(1)}, bf16[4,104,192]{2,1,0:T(8,128)(2,1)S(1)}, u32[]{:S(2)}, u32[]{:S(2)}) collective-permute-start(bf16[4,104,192]{2,1,0:T(8,128)(2,1)S(1)} %pile.1.refs_0_), channel_id=1, source_target_pairs={{0,4},{4,0},{8,12},{12,8},{16,20},{20,16},{24,28},{28,24},{1,5},{5... | collective-permute-start | bytes 479240 | tf_op jit(solution)/shard_map/ppermute | solution.py:453
  46.7 0.0 copy-start.2
  46.7 0.0 copy-start.3
  46.7 1.9 %backward.1 = (bf16[24,4096]{1,0:T(8,128)(2,1)S(1)}, bf16[24,4096]{1,0:T(8,128)(2,1)S(1)}, bf16[24,4096]{1,0:T(8,128)(2,1)S(1)}, bf16[24,4096]{1,0:T(8,128)(2,1)S(1)}) custom-call(bf16[24,4096]{1,0:T(8,128)(2,1)S(1)} %get-tuple-element.37.refs_0_, bf16[24,4096]{1,0:T(8,128)(2,1)S(1)} %collective-permute-done.refs_1_, ...), custom_call_target="tpu_custom_call" | custom-call | flops 452984832 | bytes 75497472 | tf_op jit(solution)/shard_map/backward/pallas_call | solution.py:373
  48.6 0.1 collective-permute-start.6
  48.7 1.6 %collective-permute-start.7 = (bf16[24,4096]{1,0:T(8,128)(2,1)S(1)}, bf16[24,4096]{1,0:T(8,128)(2,1)S(1)}, u32[]{:S(2)}, u32[]{:S(2)}) collective-permute-start(bf16[24,4096]{1,0:T(8,128)(2,1)S(1)} %get-tuple-element.43), channel_id=1, source_target_pairs={{0,2},{1,3},{2,0},{3,1},{4,6},{5,7},{6,4},{7,5},{8,10},{9,11},{10,... | collective-permute-start | bytes 589832 | tf_op jit(solution)/shard_map/ppermute | solution.py:453
  50.2 0.3 collective-permute-start.8
  50.5 0.8 collective-permute-done.12.refs_1_
  51.3 0.0 collective-permute-done.18.refs_3_
  51.3 1.1 %adam.1 = (f32[2,192,512]{2,1,0:T(8,128)S(1)}, bf16[192,512]{1,0:T(8,128)(2,1)S(1)}, bf16[192,512]{1,0:T(8,128)(2,1)S(1)}, bf16[192,512]{1,0:T(8,128)(2,1)S(1)},...) custom-call(bf16[4,104,192]{2,1,0:T(8,128)(2,1)S(1)} %pile.1.refs_0_, ...), custom_call_target="tpu_custom_call" | custom-call | flops 301989888 | bytes 25165824 | tf_op jit(solution)/shard_map/adam/pallas_call | solution.py:283
  52.4 0.5 collective-permute-start.19
  52.9 2.4 %collective-permute-start.26 = (bf16[96,512]{1,0:T(8,128)(2,1)S(1)}, bf16[96,512]{1,0:T(8,128)(2,1)S(1)}, u32[]{:S(2)}, u32[]{:S(2)}) collective-permute-start(bf16[96,512]{1,0:T(8,128)(2,1)S(1)} %get-tuple-element.61), channel_id=1, source_target_pairs={{0,16},{4,20},{8,24},{12,28},{16,0},{20,4},{24,8},{28,12},{1,17},{... | collective-permute-start | bytes 294920 | tf_op jit(solution)/shard_map/ppermute | solution.py:453
  55.4 1.1 %collective-permute-start.27 = (bf16[96,512]{1,0:T(8,128)(2,1)S(1)}, bf16[96,512]{1,0:T(8,128)(2,1)S(1)}, u32[]{:S(2)}, u32[]{:S(2)}) collective-permute-start(bf16[96,512]{1,0:T(8,128)(2,1)S(1)} %get-tuple-element.62), channel_id=1, source_target_pairs={{0,20},{4,16},{8,28},{12,24},{16,4},{20,0},{24,12},{28,8},{1,21},{... | collective-permute-start | bytes 294920 | tf_op jit(solution)/shard_map/ppermute | solution.py:453
  56.4 0.1 collective-permute-done.7.refs_3_
  56.5 0.8 collective-permute-start.23
  57.3 2.3 %collective-permute-done.8.refs_4_ = bf16[24,4096]{1,0:T(8,128)(2,1)S(1)} collective-permute-done((bf16[24,4096]{1,0:T(8,128)(2,1)S(1)}, bf16[24,4096]{1,0:T(8,128)(2,1)S(1)}, u32[]{:S(2)}, u32[]{:S(2)}) %collective-permute-start.8) | collective-permute-done | bytes 196640 | tf_op jit(solution)/shard_map/ppermute | solution.py:453
  59.6 0.0 collective-permute-start.24
  59.6 10.3 %collective-permute-done.26.refs_4_ = bf16[96,512]{1,0:T(8,128)(2,1)S(1)} collective-permute-done((bf16[96,512]{1,0:T(8,128)(2,1)S(1)}, bf16[96,512]{1,0:T(8,128)(2,1)S(1)}, u32[]{:S(2)}, u32[]{:S(2)}) %collective-permute-start.26) | collective-permute-done | bytes 98336 | tf_op jit(solution)/shard_map/ppermute | solution.py:453
  69.9 2.3 %collective-permute-done.27.refs_5_ = bf16[96,512]{1,0:T(8,128)(2,1)S(1)} collective-permute-done((bf16[96,512]{1,0:T(8,128)(2,1)S(1)}, bf16[96,512]{1,0:T(8,128)(2,1)S(1)}, u32[]{:S(2)}, u32[]{:S(2)}) %collective-permute-start.27) | collective-permute-done | bytes 98336 | tf_op jit(solution)/shard_map/ppermute | solution.py:453
  72.2 1.9 %collective-permute-start.28 = (bf16[96,512]{1,0:T(8,128)(2,1)S(1)}, bf16[96,512]{1,0:T(8,128)(2,1)S(1)}, u32[]{:S(2)}, u32[]{:S(2)}) collective-permute-start(bf16[96,512]{1,0:T(8,128)(2,1)S(1)} %get-tuple-element.63), channel_id=1, source_target_pairs={{0,24},{4,28},{8,16},{12,20},{16,8},{20,12},{24,0},{28,4},{1,25},{... | collective-permute-start | bytes 294920 | tf_op jit(solution)/shard_map/ppermute | solution.py:453
  74.1 0.0 collective-permute-done.19.refs_2_
  74.1 2.6 %collective-permute-start.29 = (bf16[96,512]{1,0:T(8,128)(2,1)S(1)}, bf16[96,512]{1,0:T(8,128)(2,1)S(1)}, u32[]{:S(2)}, u32[]{:S(2)}) collective-permute-start(bf16[96,512]{1,0:T(8,128)(2,1)S(1)} %get-tuple-element.64), channel_id=1, source_target_pairs={{0,28},{4,24},{8,20},{12,16},{16,12},{20,8},{24,4},{28,0},{1,29},{... | collective-permute-start | bytes 294920 | tf_op jit(solution)/shard_map/ppermute | solution.py:453
  76.7 0.1 choose.1
  76.8 2.2 %collective-permute-done.28.refs_6_ = bf16[96,512]{1,0:T(8,128)(2,1)S(1)} collective-permute-done((bf16[96,512]{1,0:T(8,128)(2,1)S(1)}, bf16[96,512]{1,0:T(8,128)(2,1)S(1)}, u32[]{:S(2)}, u32[]{:S(2)}) %collective-permute-start.28) | collective-permute-done | bytes 98336 | tf_op jit(solution)/shard_map/ppermute | solution.py:453
  79.0 1.2 %collective-permute-start.20 = (bf16[96,512]{1,0:T(8,128)(2,1)S(1)}, bf16[96,512]{1,0:T(8,128)(2,1)S(1)}, u32[]{:S(2)}, u32[]{:S(2)}) collective-permute-start(bf16[96,512]{1,0:T(8,128)(2,1)S(1)} %get-tuple-element.54), channel_id=1, source_target_pairs={{0,4},{4,0},{8,12},{12,8},{16,20},{20,16},{24,28},{28,24},{1,5},{5... | collective-permute-start | bytes 294920 | tf_op jit(solution)/shard_map/ppermute | solution.py:453
  80.2 1.4 %collective-permute-done.29.refs_7_ = bf16[96,512]{1,0:T(8,128)(2,1)S(1)} collective-permute-done((bf16[96,512]{1,0:T(8,128)(2,1)S(1)}, bf16[96,512]{1,0:T(8,128)(2,1)S(1)}, u32[]{:S(2)}, u32[]{:S(2)}) %collective-permute-start.29) | collective-permute-done | bytes 98336 | tf_op jit(solution)/shard_map/ppermute | solution.py:453
  81.6 1.9 %collective-permute-start.21 = (bf16[96,512]{1,0:T(8,128)(2,1)S(1)}, bf16[96,512]{1,0:T(8,128)(2,1)S(1)}, u32[]{:S(2)}, u32[]{:S(2)}) collective-permute-start(bf16[96,512]{1,0:T(8,128)(2,1)S(1)} %get-tuple-element.55), channel_id=1, source_target_pairs={{0,8},{4,12},{8,0},{12,4},{16,24},{20,28},{24,16},{28,20},{1,9},{5... | collective-permute-start | bytes 294920 | tf_op jit(solution)/shard_map/ppermute | solution.py:453
  83.4 0.0 collective-permute-done.23.refs_1_
  83.5 0.7 collective-permute-start.22
  84.1 1.5 %combine.1 = bf16[192,4096]{1,0:T(8,128)(2,1)} custom-call(f32[24,192]{1,0:T(8,128)S(1)} %copy-done.6, bf16[24,4096]{1,0:T(8,128)(2,1)S(1)} %get-tuple-element.41.refs_1_, bf16[24,4096]{1,0:T(8,128)(2,1)S(1)} %collective-permute-done.6.refs_2_, bf16[24,4096]{1,0:T(8,128)(2,1)S(1)} %collective-permute-done.7.refs_3_, ...), custom_call_target="tpu_custom_call" | custom-call | flops 37748736 | bytes 25165824 | tf_op jit(solution)/shard_map/combine/pallas_call | solution.py:407
  85.6 1.3 %update.1 = (f32[2,192,512]{2,1,0:T(8,128)}, f32[2,192,512]{2,1,0:T(8,128)}) custom-call(f32[2,192,512]{2,1,0:T(8,128)S(1)} %get-tuple-element.65.summed, f32[2,192,512]{2,1,0:T(8,128)S(1)} %copy-done.2, f32[2,192,512]{2,1,0:T(8,128)S(1)} %copy-done.3), custom_call_target="tpu_custom_call" | custom-call | flops 1572864 | bytes 25165824 | tf_op jit(solution)/shard_map/update/pallas_call | solution.py:336
  86.9 0.0 collective-permute-done.24.refs_2_
  86.9 1.1 %place_first.1.refs_4_ = bf16[192,4096]{1,0:T(8,128)(2,1)} custom-call(bf16[192,512]{1,0:T(8,128)(2,1)S(1)} %get-tuple-element.57.refs_0_, bf16[192,512]{1,0:T(8,128)(2,1)S(1)} %collective-permute-done.23.refs_1_, bf16[192,512]{1,0:T(8,128)(2,1)S(1)} %collective-permute-done.24.refs_2_, bf16[192,512]{1,0:T(8,128)(2,1)S(1)} %collective-permute-done.25.refs_3_, ...), custom_call_target="tpu_custom_call" | custom-call | bytes 50331648 | tf_op jit(solution)/shard_map/place_first/pallas_call | solution.py:439
  88.0 1.0 %collective-permute-done.22.refs_3_ = bf16[96,512]{1,0:T(8,128)(2,1)S(1)} collective-permute-done((bf16[96,512]{1,0:T(8,128)(2,1)S(1)}, bf16[96,512]{1,0:T(8,128)(2,1)S(1)}, u32[]{:S(2)}, u32[]{:S(2)}) %collective-permute-start.22) | collective-permute-done | bytes 98336 | tf_op jit(solution)/shard_map/ppermute | solution.py:453
  89.0 0.8 place_last.1
  (24 shorter events, 0.1 us)
Async XLA Ops:
  1.3 31.9 %copy-start.1 = (bf16[1,4096,192]{1,2,0:T(8,128)(2,1)S(1)}, bf16[1,4096,192]{1,2,0:T(8,128)(2,1)}, u32[]{:S(2)}) copy-start(bf16[1,4096,192]{1,2,0:T(8,128)(2,1)} %param.15) | copy-start | bytes 4718596
  3.9 15.9 %copy-start.5 = (bf16[24,4096]{1,0:T(8,128)(2,1)S(1)}, bf16[24,4096]{1,0:T(8,128)(2,1)}, u32[]{:S(2)}) copy-start(bf16[24,4096]{1,0:T(8,128)(2,1)} %get-tuple-element.38.refs_0_) | copy-start | bytes 589828
  3.9 29.3 %copy-start = (bf16[1,4096,192]{1,2,0:T(8,128)(2,1)S(1)}, bf16[1,4096,192]{1,2,0:T(8,128)(2,1)}, u32[]{:S(2)}) copy-start(bf16[1,4096,192]{1,2,0:T(8,128)(2,1)} %param.14) | copy-start | bytes 4718596
  4.0 0.9 copy-start.6
  6.6 5.7 %collective-permute-start.13 = (bf16[2,24,512]{2,1,0:T(8,128)(2,1)S(1)}, bf16[2,24,512]{2,1,0:T(8,128)(2,1)S(1)}, u32[]{:S(2)}, u32[]{:S(2)}) collective-permute-start(bf16[2,24,512]{2,1,0:T(8,128)(2,1)S(1)} %get-tuple-element.47), channel_id=1, source_target_pairs={{0,8},{4,12},{8,0},{12,4},{16,24},{20,28},{24,16},{28,20},{1,9},{5... | collective-permute-start | bytes 147464 | tf_op jit(solution)/shard_map/ppermute | solution.py:453
  9.7 5.9 %collective-permute-start.14 = (bf16[2,24,512]{2,1,0:T(8,128)(2,1)S(1)}, bf16[2,24,512]{2,1,0:T(8,128)(2,1)S(1)}, u32[]{:S(2)}, u32[]{:S(2)}) collective-permute-start(bf16[2,24,512]{2,1,0:T(8,128)(2,1)S(1)} %get-tuple-element.48), channel_id=1, source_target_pairs={{0,16},{4,20},{8,24},{12,28},{16,0},{20,4},{24,8},{28,12},{1,17},{... | collective-permute-start | bytes 147464 | tf_op jit(solution)/shard_map/ppermute | solution.py:453
  12.3 5.9 %collective-permute-start.15 = (bf16[2,24,512]{2,1,0:T(8,128)(2,1)S(1)}, bf16[2,24,512]{2,1,0:T(8,128)(2,1)S(1)}, u32[]{:S(2)}, u32[]{:S(2)}) collective-permute-start(bf16[2,24,512]{2,1,0:T(8,128)(2,1)S(1)} %get-tuple-element.49), channel_id=1, source_target_pairs={{0,24},{4,28},{8,16},{12,20},{16,8},{20,12},{24,0},{28,4},{1,25},{... | collective-permute-start | bytes 147464 | tf_op jit(solution)/shard_map/ppermute | solution.py:453
  18.2 4.7 %collective-permute-start.16 = (bf16[4,24,512]{2,1,0:T(8,128)(2,1)S(1)}, bf16[4,24,512]{2,1,0:T(8,128)(2,1)S(1)}, u32[]{:S(2)}, u32[]{:S(2)}) collective-permute-start(bf16[4,24,512]{2,1,0:T(8,128)(2,1)S(1)} %get-tuple-element.51), channel_id=1, source_target_pairs={{0,4},{4,0},{8,12},{12,8},{16,20},{20,16},{24,28},{28,24},{1,5},{5... | collective-permute-start | bytes 294920 | tf_op jit(solution)/shard_map/ppermute | solution.py:453
  19.8 7.8 %collective-permute-start.4 = (bf16[24,4096]{1,0:T(8,128)(2,1)S(1)}, bf16[24,4096]{1,0:T(8,128)(2,1)S(1)}, u32[]{:S(2)}, u32[]{:S(2)}) collective-permute-start(bf16[24,4096]{1,0:T(8,128)(2,1)S(1)} %copy-done.5), channel_id=1, source_target_pairs={{0,2},{1,3},{2,0},{3,1},{4,6},{5,7},{6,4},{7,5},{8,10},{9,11},{10,... | collective-permute-start | bytes 589832 | tf_op jit(solution)/shard_map/ppermute | solution.py:453
  22.9 8.2 %collective-permute-start.17 = (bf16[8,24,512]{2,1,0:T(8,128)(2,1)S(1)}, bf16[8,24,512]{2,1,0:T(8,128)(2,1)S(1)}, u32[]{:S(2)}, u32[]{:S(2)}) collective-permute-start(bf16[8,24,512]{2,1,0:T(8,128)(2,1)S(1)} %join.2.one), channel_id=1, source_target_pairs={{0,2},{1,3},{2,0},{3,1},{4,6},{5,7},{6,4},{7,5},{8,10},{9,11},{10,... | collective-permute-start | bytes 589832 | tf_op jit(solution)/shard_map/ppermute | solution.py:453
  24.5 8.7 %collective-permute-start.1 = (bf16[24,4096]{1,0:T(8,128)(2,1)S(1)}, bf16[24,4096]{1,0:T(8,128)(2,1)S(1)}, u32[]{:S(2)}, u32[]{:S(2)}) collective-permute-start(bf16[24,4096]{1,0:T(8,128)(2,1)S(1)} %get-tuple-element.37.refs_0_), channel_id=1, source_target_pairs={{0,2},{1,3},{2,0},{3,1},{4,6},{5,7},{6,4},{7,5},{8,10},{9,11},{10,... | collective-permute-start | bytes 589832 | tf_op jit(solution)/shard_map/ppermute | solution.py:453
  25.0 8.2 %collective-permute-start.3 = (bf16[24,4096]{1,0:T(8,128)(2,1)S(1)}, bf16[24,4096]{1,0:T(8,128)(2,1)S(1)}, u32[]{:S(2)}, u32[]{:S(2)}) collective-permute-start(bf16[24,4096]{1,0:T(8,128)(2,1)S(1)} %copy-done.5), channel_id=1, source_target_pairs={{0,1},{1,0},{2,3},{3,2},{4,5},{5,4},{6,7},{7,6},{8,9},{9,8},{10,11... | collective-permute-start | bytes 589832 | tf_op jit(solution)/shard_map/ppermute | solution.py:453
  27.6 5.6 %collective-permute-start.5 = (bf16[24,4096]{1,0:T(8,128)(2,1)S(1)}, bf16[24,4096]{1,0:T(8,128)(2,1)S(1)}, u32[]{:S(2)}, u32[]{:S(2)}) collective-permute-start(bf16[24,4096]{1,0:T(8,128)(2,1)S(1)} %collective-permute-done.4.refs_2_), channel_id=1, source_target_pairs={{0,1},{1,0},{2,3},{3,2},{4,5},{5,4},{6,7},{7,6},{8,9},{9,8},{10,11... | collective-permute-start | bytes 589832 | tf_op jit(solution)/shard_map/ppermute | solution.py:453
  31.1 20.2 %collective-permute-start.18 = (bf16[16,24,512]{2,1,0:T(8,128)(2,1)S(1)}, bf16[16,24,512]{2,1,0:T(8,128)(2,1)S(1)}, u32[]{:S(2)}, u32[]{:S(2)}) collective-permute-start(bf16[16,24,512]{2,1,0:T(8,128)(2,1)S(1)} %join.3.refs_2_), channel_id=1, source_target_pairs={{0,1},{1,0},{2,3},{3,2},{4,5},{5,4},{6,7},{7,6},{8,9},{9,8},{10,11... | collective-permute-start | bytes 1179656 | tf_op jit(solution)/shard_map/ppermute | solution.py:453
  31.2 15.4 %collective-permute-start = (bf16[24,4096]{1,0:T(8,128)(2,1)S(1)}, bf16[24,4096]{1,0:T(8,128)(2,1)S(1)}, u32[]{:S(2)}, u32[]{:S(2)}) collective-permute-start(bf16[24,4096]{1,0:T(8,128)(2,1)S(1)} %get-tuple-element.37.refs_0_), channel_id=1, source_target_pairs={{0,1},{1,0},{2,3},{3,2},{4,5},{5,4},{6,7},{7,6},{8,9},{9,8},{10,11... | collective-permute-start | bytes 589832 | tf_op jit(solution)/shard_map/ppermute | solution.py:453
  33.2 13.5 %collective-permute-start.2 = (bf16[24,4096]{1,0:T(8,128)(2,1)S(1)}, bf16[24,4096]{1,0:T(8,128)(2,1)S(1)}, u32[]{:S(2)}, u32[]{:S(2)}) collective-permute-start(bf16[24,4096]{1,0:T(8,128)(2,1)S(1)} %collective-permute-done.1.refs_2_), channel_id=1, source_target_pairs={{0,1},{1,0},{2,3},{3,2},{4,5},{5,4},{6,7},{7,6},{8,9},{9,8},{10,11... | collective-permute-start | bytes 589832 | tf_op jit(solution)/shard_map/ppermute | solution.py:453
  33.2 13.4 %copy-start.4 = (bf16[1,192,4096]{2,1,0:T(8,128)(2,1)S(1)}, bf16[1,192,4096]{2,1,0:T(8,128)(2,1)}, u32[]{:S(2)}) copy-start(bf16[1,192,4096]{2,1,0:T(8,128)(2,1)} %param.16) | copy-start | bytes 4718596
  34.4 6.8 %collective-permute-start.10 = (bf16[104,192]{1,0:T(8,128)(2,1)S(1)}, bf16[104,192]{1,0:T(8,128)(2,1)S(1)}, u32[]{:S(2)}, u32[]{:S(2)}) collective-permute-start(bf16[104,192]{1,0:T(8,128)(2,1)S(1)} %get-tuple-element.45.refs_0_), channel_id=1, source_target_pairs={{0,16},{4,20},{8,24},{12,28},{16,0},{20,4},{24,8},{28,12},{1,17},{... | collective-permute-start | bytes 119816 | tf_op jit(solution)/shard_map/ppermute | solution.py:453
  34.5 6.7 %collective-permute-start.11 = (bf16[104,192]{1,0:T(8,128)(2,1)S(1)}, bf16[104,192]{1,0:T(8,128)(2,1)S(1)}, u32[]{:S(2)}, u32[]{:S(2)}) collective-permute-start(bf16[104,192]{1,0:T(8,128)(2,1)S(1)} %get-tuple-element.45.refs_0_), channel_id=1, source_target_pairs={{0,24},{4,28},{8,16},{12,20},{16,8},{20,12},{24,0},{28,4},{1,25},{... | collective-permute-start | bytes 119816 | tf_op jit(solution)/shard_map/ppermute | solution.py:453
  41.2 4.1 %collective-permute-start.9 = (bf16[104,192]{1,0:T(8,128)(2,1)S(1)}, bf16[104,192]{1,0:T(8,128)(2,1)S(1)}, u32[]{:S(2)}, u32[]{:S(2)}) collective-permute-start(bf16[104,192]{1,0:T(8,128)(2,1)S(1)} %get-tuple-element.45.refs_0_), channel_id=1, source_target_pairs={{0,8},{4,12},{8,0},{12,4},{16,24},{20,28},{24,16},{28,20},{1,9},{5... | collective-permute-start | bytes 119816 | tf_op jit(solution)/shard_map/ppermute | solution.py:453
  45.4 5.9 %collective-permute-start.12 = (bf16[4,104,192]{2,1,0:T(8,128)(2,1)S(1)}, bf16[4,104,192]{2,1,0:T(8,128)(2,1)S(1)}, u32[]{:S(2)}, u32[]{:S(2)}) collective-permute-start(bf16[4,104,192]{2,1,0:T(8,128)(2,1)S(1)} %pile.1.refs_0_), channel_id=1, source_target_pairs={{0,4},{4,0},{8,12},{12,8},{16,20},{20,16},{24,28},{28,24},{1,5},{5... | collective-permute-start | bytes 479240 | tf_op jit(solution)/shard_map/ppermute | solution.py:453
  46.7 4.6 %copy-start.2 = (f32[2,192,512]{2,1,0:T(8,128)S(1)}, f32[2,192,512]{2,1,0:T(8,128)}, u32[]{:S(2)}) copy-start(f32[2,192,512]{2,1,0:T(8,128)} %first.1) | copy-start | bytes 2359300
  46.7 4.6 %copy-start.3 = (f32[2,192,512]{2,1,0:T(8,128)S(1)}, f32[2,192,512]{2,1,0:T(8,128)}, u32[]{:S(2)}) copy-start(f32[2,192,512]{2,1,0:T(8,128)} %second.1) | copy-start | bytes 2359300
  48.6 6.8 %collective-permute-start.6 = (bf16[24,4096]{1,0:T(8,128)(2,1)S(1)}, bf16[24,4096]{1,0:T(8,128)(2,1)S(1)}, u32[]{:S(2)}, u32[]{:S(2)}) collective-permute-start(bf16[24,4096]{1,0:T(8,128)(2,1)S(1)} %get-tuple-element.42), channel_id=1, source_target_pairs={{0,1},{1,0},{2,3},{3,2},{4,5},{5,4},{6,7},{7,6},{8,9},{9,8},{10,11... | collective-permute-start | bytes 589832 | tf_op jit(solution)/shard_map/ppermute | solution.py:453
  48.7 7.8 %collective-permute-start.7 = (bf16[24,4096]{1,0:T(8,128)(2,1)S(1)}, bf16[24,4096]{1,0:T(8,128)(2,1)S(1)}, u32[]{:S(2)}, u32[]{:S(2)}) collective-permute-start(bf16[24,4096]{1,0:T(8,128)(2,1)S(1)} %get-tuple-element.43), channel_id=1, source_target_pairs={{0,2},{1,3},{2,0},{3,1},{4,6},{5,7},{6,4},{7,5},{8,10},{9,11},{10,... | collective-permute-start | bytes 589832 | tf_op jit(solution)/shard_map/ppermute | solution.py:453
  50.2 9.4 %collective-permute-start.8 = (bf16[24,4096]{1,0:T(8,128)(2,1)S(1)}, bf16[24,4096]{1,0:T(8,128)(2,1)S(1)}, u32[]{:S(2)}, u32[]{:S(2)}) collective-permute-start(bf16[24,4096]{1,0:T(8,128)(2,1)S(1)} %get-tuple-element.44), channel_id=1, source_target_pairs={{0,3},{1,2},{2,1},{3,0},{4,7},{5,6},{6,5},{7,4},{8,11},{9,10},{10,... | collective-permute-start | bytes 589832 | tf_op jit(solution)/shard_map/ppermute | solution.py:453
  52.4 21.7 %collective-permute-start.19 = (bf16[2,96,512]{2,1,0:T(8,128)(2,1)S(1)}, bf16[2,96,512]{2,1,0:T(8,128)(2,1)S(1)}, u32[]{:S(2)}, u32[]{:S(2)}) collective-permute-start(bf16[2,96,512]{2,1,0:T(8,128)(2,1)S(1)} %get-tuple-element.52), channel_id=1, source_target_pairs={{0,16},{4,20},{8,24},{12,28},{16,0},{20,4},{24,8},{28,12},{1,17},{... | collective-permute-start | bytes 589832 | tf_op jit(solution)/shard_map/ppermute | solution.py:453
  52.9 17.0 %collective-permute-start.26 = (bf16[96,512]{1,0:T(8,128)(2,1)S(1)}, bf16[96,512]{1,0:T(8,128)(2,1)S(1)}, u32[]{:S(2)}, u32[]{:S(2)}) collective-permute-start(bf16[96,512]{1,0:T(8,128)(2,1)S(1)} %get-tuple-element.61), channel_id=1, source_target_pairs={{0,16},{4,20},{8,24},{12,28},{16,0},{20,4},{24,8},{28,12},{1,17},{... | collective-permute-start | bytes 294920 | tf_op jit(solution)/shard_map/ppermute | solution.py:453
  55.4 16.8 %collective-permute-start.27 = (bf16[96,512]{1,0:T(8,128)(2,1)S(1)}, bf16[96,512]{1,0:T(8,128)(2,1)S(1)}, u32[]{:S(2)}, u32[]{:S(2)}) collective-permute-start(bf16[96,512]{1,0:T(8,128)(2,1)S(1)} %get-tuple-element.62), channel_id=1, source_target_pairs={{0,20},{4,16},{8,28},{12,24},{16,4},{20,0},{24,12},{28,8},{1,21},{... | collective-permute-start | bytes 294920 | tf_op jit(solution)/shard_map/ppermute | solution.py:453
  56.5 26.9 %collective-permute-start.23 = (bf16[192,512]{1,0:T(8,128)(2,1)S(1)}, bf16[192,512]{1,0:T(8,128)(2,1)S(1)}, u32[]{:S(2)}, u32[]{:S(2)}) collective-permute-start(bf16[192,512]{1,0:T(8,128)(2,1)S(1)} %get-tuple-element.58), channel_id=1, source_target_pairs={{0,4},{4,0},{8,12},{12,8},{16,20},{20,16},{24,28},{28,24},{1,5},{5... | collective-permute-start | bytes 589832 | tf_op jit(solution)/shard_map/ppermute | solution.py:453
  59.6 27.2 %collective-permute-start.24 = (bf16[192,512]{1,0:T(8,128)(2,1)S(1)}, bf16[192,512]{1,0:T(8,128)(2,1)S(1)}, u32[]{:S(2)}, u32[]{:S(2)}) collective-permute-start(bf16[192,512]{1,0:T(8,128)(2,1)S(1)} %get-tuple-element.59), channel_id=1, source_target_pairs={{0,8},{4,12},{8,0},{12,4},{16,24},{20,28},{24,16},{28,20},{1,9},{5... | collective-permute-start | bytes 589832 | tf_op jit(solution)/shard_map/ppermute | solution.py:453
  69.9 17.0 %collective-permute-start.25 = (bf16[192,512]{1,0:T(8,128)(2,1)S(1)}, bf16[192,512]{1,0:T(8,128)(2,1)S(1)}, u32[]{:S(2)}, u32[]{:S(2)}) collective-permute-start(bf16[192,512]{1,0:T(8,128)(2,1)S(1)} %get-tuple-element.60), channel_id=1, source_target_pairs={{0,12},{4,8},{8,4},{12,0},{16,28},{20,24},{24,20},{28,16},{1,13},{... | collective-permute-start | bytes 589832 | tf_op jit(solution)/shard_map/ppermute | solution.py:453
  72.2 6.8 %collective-permute-start.28 = (bf16[96,512]{1,0:T(8,128)(2,1)S(1)}, bf16[96,512]{1,0:T(8,128)(2,1)S(1)}, u32[]{:S(2)}, u32[]{:S(2)}) collective-permute-start(bf16[96,512]{1,0:T(8,128)(2,1)S(1)} %get-tuple-element.63), channel_id=1, source_target_pairs={{0,24},{4,28},{8,16},{12,20},{16,8},{20,12},{24,0},{28,4},{1,25},{... | collective-permute-start | bytes 294920 | tf_op jit(solution)/shard_map/ppermute | solution.py:453
  74.1 7.5 %collective-permute-start.29 = (bf16[96,512]{1,0:T(8,128)(2,1)S(1)}, bf16[96,512]{1,0:T(8,128)(2,1)S(1)}, u32[]{:S(2)}, u32[]{:S(2)}) collective-permute-start(bf16[96,512]{1,0:T(8,128)(2,1)S(1)} %get-tuple-element.64), channel_id=1, source_target_pairs={{0,28},{4,24},{8,20},{12,16},{16,12},{20,8},{24,4},{28,0},{1,29},{... | collective-permute-start | bytes 294920 | tf_op jit(solution)/shard_map/ppermute | solution.py:453
  79.0 9.0 %collective-permute-start.20 = (bf16[96,512]{1,0:T(8,128)(2,1)S(1)}, bf16[96,512]{1,0:T(8,128)(2,1)S(1)}, u32[]{:S(2)}, u32[]{:S(2)}) collective-permute-start(bf16[96,512]{1,0:T(8,128)(2,1)S(1)} %get-tuple-element.54), channel_id=1, source_target_pairs={{0,4},{4,0},{8,12},{12,8},{16,20},{20,16},{24,28},{28,24},{1,5},{5... | collective-permute-start | bytes 294920 | tf_op jit(solution)/shard_map/ppermute | solution.py:453
  81.6 6.4 %collective-permute-start.21 = (bf16[96,512]{1,0:T(8,128)(2,1)S(1)}, bf16[96,512]{1,0:T(8,128)(2,1)S(1)}, u32[]{:S(2)}, u32[]{:S(2)}) collective-permute-start(bf16[96,512]{1,0:T(8,128)(2,1)S(1)} %get-tuple-element.55), channel_id=1, source_target_pairs={{0,8},{4,12},{8,0},{12,4},{16,24},{20,28},{24,16},{28,20},{1,9},{5... | collective-permute-start | bytes 294920 | tf_op jit(solution)/shard_map/ppermute | solution.py:453
  83.5 5.5 %collective-permute-start.22 = (bf16[96,512]{1,0:T(8,128)(2,1)S(1)}, bf16[96,512]{1,0:T(8,128)(2,1)S(1)}, u32[]{:S(2)}, u32[]{:S(2)}) collective-permute-start(bf16[96,512]{1,0:T(8,128)(2,1)S(1)} %get-tuple-element.56), channel_id=1, source_target_pairs={{0,12},{4,8},{8,4},{12,0},{16,28},{20,24},{24,20},{28,16},{1,13},{... | collective-permute-start | bytes 294920 | tf_op jit(solution)/shard_map/ppermute | solution.py:453
